TPU v7x, 512 devices: a whole 4x8x8 slice. The times are simulated.
512 devices in a mesh: expert: 32 (over x, y), dp: 16 (over z, core).
Axes of the slice: x: 4, y: 8, z: 8, core: 2. Of those that a mesh axis runs over, the one named last changes fastest.
Arguments:
- tokens: bfloat16 [8192, 1664], P(('expert', 'dp')), may hold values from -6 to 6
- cotangent: bfloat16 [8192, 1664], P(('expert', 'dp')), may hold values from -1.1953125 to 1.1953125
- expert_ids: int32 [8192, 2], P(('expert', 'dp')), may hold values from 0 to 31, all different within a row; in each aligned block of 16 rows (0 to 15, 16 to 31, ...) at most 2 rows name the same one
- gates: bfloat16 [8192, 2], P(('expert', 'dp')), may hold values from 0.099609375 to 1
- w_in: bfloat16 [32, 1664, 4096], P('expert', None, 'dp'), may hold values from -0.15625 to 0.15625
- w_out: bfloat16 [32, 4096, 1664], P('expert', 'dp'), may hold values from -0.09375 to 0.09375
Outputs:
- token_grads: bfloat16 [8192, 1664], P(('expert', 'dp'))
- gate_grads: bfloat16 [8192, 2], P(('expert', 'dp'))
- grad_in_weights: bfloat16 [32, 1664, 4096], P('expert', None, 'dp')
- grad_out_weights: bfloat16 [32, 4096, 1664], P('expert', 'dp')
Inputs may be any that keep to these rules, and one draw needn't show every extreme that they name: `expert_ids`: the two experts of a token differ, and no expert is named by more than 2 of the 16 tokens of one device.
All inputs are finite; a program needn't handle non-finite values.
Results may differ from a plain program's by a relative error of at most 0.019.
Values may be sent and summed in bfloat16 or wider, within the bound.
No kernel may reach another device: no remote copies, remote signals or barrier semaphores. Data moves between devices by JAX's collectives and lax.ppermute only.
A program may use at most 64 MiB of HBM per device.

v0:
```python
import math

import jax
import jax.numpy as jnp
from jax import lax
from jax.sharding import PartitionSpec as P


def side_by_side(arrays, axis, split_dim, concat_dim, along):
    columns = [a.reshape(*a.shape[:along], -1) for a in arrays]
    both = jnp.concatenate(columns, axis=along)
    whole, at, done = (
        lax.all_to_all(both, axis, split_axis=split_dim, concat_axis=concat_dim, tiled=True),
        0,
        [],
    )
    for a, column in zip(arrays, columns):
        section = whole[..., at : at + column.shape[along]]
        done.append(section.reshape(*section.shape[:along], *a.shape[along:]))
        at += column.shape[along]
    return tuple(done)


def in_one_piece(arrays, axis, dim, along):
    widths = [math.prod(a.shape[along:]) for a in arrays]
    both = jnp.concatenate(
        [a.reshape(*a.shape[:along], w) for a, w in zip(arrays, widths)], axis=along
    )
    whole = lax.all_gather(both, axis, axis=dim, tiled=True)
    pieces = jnp.split(whole, [sum(widths[:k]) for k in range(1, len(widths))], axis=along)
    return tuple(
        (b.reshape(*whole.shape[:along], *a.shape[along:]) for a, b in zip(arrays, pieces))
    )


def in_blocks(x, dim, devices):
    before, after = (x.shape[:dim], x.shape[dim + 1 :])
    return jnp.moveaxis(x.reshape(*before, devices, -1, *after), dim, 0)


def sent_and_summed(x, axis, dim):
    pieces = in_blocks(x, dim, lax.axis_size(axis))
    arrived = lax.all_to_all(pieces, axis, split_axis=0, concat_axis=0, tiled=True)
    return arrived.sum(axis=0)


def normal_parts(pre):
    cdf = 0.5 * (1.0 + lax.erf(pre * 0.7071067811865476))
    pdf = 0.3989422804014327 * jnp.exp(-0.5 * pre * pre)
    return (cdf, pdf)


def per_device(tokens, cotangent, expert_ids, gates, w_in, w_out):
    tok = tokens.shape[0]
    feat = tokens.shape[1]
    experts = lax.axis_size("expert")
    cap = max(2, 4 * tok // experts)
    assign = 2 * tok
    ids = expert_ids.reshape(assign)
    onehot = (ids[:, None] == jnp.arange(experts, dtype=jnp.int32)[None, :]).astype(jnp.float32)
    lower = (jnp.arange(assign)[:, None] > jnp.arange(assign)[None, :]).astype(jnp.float32)
    before = jnp.dot(lower, onehot, preferred_element_type=jnp.float32)
    slot = jnp.sum(before * onehot, axis=1).astype(jnp.int32)
    target = ids * cap + slot
    pick = (jnp.arange(experts * cap, dtype=jnp.int32)[:, None] == target[None, :]).astype(
        jnp.bfloat16
    )
    src_in = jnp.repeat(tokens, 2, axis=0)
    src_cot = jnp.repeat(cotangent, 2, axis=0)
    send_in = (
        jnp.dot(pick, src_in, preferred_element_type=jnp.float32)
        .astype(jnp.bfloat16)
        .reshape(experts, cap, feat)
    )
    send_cot = (
        jnp.dot(pick, src_cot, preferred_element_type=jnp.float32)
        .astype(jnp.bfloat16)
        .reshape(experts, cap, feat)
    )
    send_gate = (
        jnp.dot(pick, gates.reshape(assign, 1), preferred_element_type=jnp.float32)
        .astype(jnp.bfloat16)
        .reshape(experts, cap)
    )
    w_first = w_in[0]
    w_second = w_out[0]
    arrived = side_by_side((send_in, send_cot, send_gate), "expert", 0, 0, 2)
    shared = in_one_piece((arrived[0], arrived[1], arrived[2]), "dp", 0, 2)
    x_blocks, cot_blocks, gate_blocks = shared
    count = x_blocks.shape[0] * x_blocks.shape[1]
    x_rows = x_blocks.reshape(count, feat)
    cot_rows = cot_blocks.reshape(count, feat)
    gate_f = gate_blocks.reshape(count, 1).astype(jnp.float32)
    pre = jnp.dot(x_rows, w_first, preferred_element_type=jnp.float32)
    cdf, pdf = normal_parts(pre)
    hidden = (pre * cdf).astype(jnp.bfloat16)
    back = lax.dot_general(
        cot_rows, w_second, (((1,), (1,)), ((), ())), preferred_element_type=jnp.float32
    )
    scaled = (gate_f * cot_rows.astype(jnp.float32)).astype(jnp.bfloat16)
    grad_second = lax.dot_general(
        hidden, scaled, (((0,), (0,)), ((), ())), preferred_element_type=jnp.float32
    )
    pre_grad = (gate_f * back * (cdf + pre * pdf)).astype(jnp.bfloat16)
    grad_first = lax.dot_general(
        x_rows, pre_grad, (((0,), (0,)), ((), ())), preferred_element_type=jnp.float32
    )
    row_part = lax.dot_general(
        pre_grad, w_first, (((1,), (1,)), ((), ())), preferred_element_type=jnp.float32
    ).astype(jnp.bfloat16)
    gate_part = jnp.sum(hidden.astype(jnp.float32) * back, axis=1)
    row_sums = lax.psum_scatter(row_part, "dp", scatter_dimension=0, tiled=True)
    gate_sums = sent_and_summed(gate_part, "dp", 0)
    row_back = row_sums.reshape(experts, cap, feat)
    gate_back = gate_sums.astype(jnp.bfloat16).reshape(experts, cap)
    back_rows, back_gate = (
        lax.all_to_all(row_back, "expert", split_axis=0, concat_axis=0, tiled=True),
        lax.all_to_all(gate_back, "expert", split_axis=0, concat_axis=0, tiled=True),
    )
    flat_back = back_rows.reshape(experts * cap, feat)
    per_assign = lax.dot_general(
        pick, flat_back, (((0,), (0,)), ((), ())), preferred_element_type=jnp.float32
    )
    token_grads = jnp.sum(per_assign.reshape(tok, 2, feat), axis=1).astype(jnp.bfloat16)
    gate_assign = lax.dot_general(
        pick,
        back_gate.reshape(experts * cap, 1),
        (((0,), (0,)), ((), ())),
        preferred_element_type=jnp.float32,
    )
    gate_grads = gate_assign.reshape(tok, 2).astype(jnp.bfloat16)
    grad_in_weights = grad_first.astype(jnp.bfloat16)[None]
    grad_out_weights = grad_second.astype(jnp.bfloat16)[None]
    return (token_grads, gate_grads, grad_in_weights, grad_out_weights)


def solution(mesh):
    in_specs = (
        P(("expert", "dp"), None),
        P(("expert", "dp"), None),
        P(("expert", "dp"), None),
        P(("expert", "dp"), None),
        P("expert", None, "dp"),
        P("expert", "dp", None),
    )
    out_specs = (
        P(("expert", "dp"), None),
        P(("expert", "dp"), None),
        P("expert", None, "dp"),
        P("expert", "dp", None),
    )
    return jax.shard_map(
        per_device, mesh=mesh, in_specs=in_specs, out_specs=out_specs, check_vma=False
    )
```

profile of v0, /device:TPU:8, one launch (start us, length us, event | category | flops | bytes accessed | tf_op | source)
XLA Modules:
  0.0 217.4 jit_solution(15647063407286597800)
XLA Ops:
  7.2 0.8 copy.33
  8.1 0.8 copy.32
  9.0 0.1 fusion.5
  9.3 0.2 reshape_reshape.5
  9.4 0.9 broadcast_in_dim.8
  10.4 0.2 convolution_convert_fusion.3
  10.7 0.9 broadcast_in_dim.18
  11.6 0.2 convolution_convert_fusion.2
  11.9 0.4 pad_maximum_fusion
  12.3 26.0 %all_to_all.25 = bf16[32,2,3329]{2,1,0:T(2,128)(2,1)} all-to-all(bf16[32,2,3329]{2,1,0:T(2,128)(2,1)S(1)} %pad_maximum_fusion), channel_id=1, replica_groups=mesh['expert'=32,'dp'=16] {'expert'}, dimensions={0} | all-to-all | bytes 852224 | tf_op jit(solution)/shard_map/all_to_all | solution.py:13
  38.4 52.4 %all-gather.2.cloned.1.call-done = bf16[512,2,3329]{2,1,0:T(2,128)(2,1)} async-done(((bf16[32,2,3329]{2,1,0:T(2,128)(2,1)}), bf16[512,2,3329]{2,1,0:T(2,128)(2,1)}) %all-gather.2.cloned.1.call-update) | async-done | bytes 6817808 | tf_op jit(solution)/shard_map/all_gather | solution.py:29
  90.8 1.6 convert_reduce_fusion
  92.3 0.2 reshape.140
  92.5 7.4 %fusion.25 = (bf16[512,2,1664]{2,1,0:T(2,128)(2,1)}, bf16[512,2,1664]{2,1,0:T(2,128)(2,1)}) fusion(bf16[512,2,3329]{2,1,0:T(2,128)(2,1)} %all-gather.2.cloned.1.call-done), kind=kLoop, calls=%fused_computation.44 | loop fusion | bytes 13631488 | tf_op jit(solution)/shard_map/split | solution.py:30
  99.9 8.1 %reshape.135 = bf16[1024,1664]{1,0:T(8,128)(2,1)} reshape(bf16[512,2,1664]{2,1,0:T(2,128)(2,1)} %get-tuple-element.6) | data formatting | bytes 6815744 | tf_op jit(solution)/shard_map/reshape | solution.py:92
  108.0 8.1 %reshape.136 = bf16[1024,1664]{1,0:T(8,128)(2,1)} reshape(bf16[512,2,1664]{2,1,0:T(2,128)(2,1)} %get-tuple-element.7) | data formatting | bytes 6815744 | tf_op jit(solution)/shard_map/reshape | solution.py:91
  116.1 3.3 %fusion.14 = f32[1024,256]{0,1:T(8,128)S(1)} fusion(bf16[1024,1664]{1,0:T(8,128)(2,1)} %reshape.136, bf16[1,1664,256]{2,1,0:T(8,128)(2,1)S(1)} %copy-done), kind=kOutput, calls=%fused_computation.26 | convolution fusion | flops 872415232 | bytes 5308416 | tf_op jit(solution)/shard_map/dot_general | solution.py:94
  119.4 1.4 multiply_reduce_fusion
  120.9 2.9 %convolution_convert_fusion = bf16[1024,1664]{1,0:T(8,128)(2,1)} fusion(bf16[1024,256]{0,1:T(8,128)(2,1)S(1)} %get-tuple-element.8, bf16[1,1664,256]{2,1,0:T(8,128)(2,1)S(1)} %copy-done), kind=kOutput, calls=%fused_computation.1 | convolution fusion | flops 874119168 | bytes 4784128 | tf_op jit(solution)/shard_map/dot_general | solution.py:108
  123.8 0.7 all_to_all.18
  124.5 4.2 %all-to-all-start.2 = ((f32[16,1,64]{2,1,0:T(1,128)}), f32[16,1,64]{2,1,0:T(1,128)S(1)}, u32[]{:S(2)}, u32[]{:S(2)}) async-start(f32[16,1,64]{2,1,0:T(1,128)} %all_to_all.18), calls=%async_computation.3 | async-start | bytes 16384 | tf_op jit(solution)/shard_map/all_to_all | solution.py:43
  128.8 7.4 %all-to-all-done.2 = f32[16,1,64]{2,1,0:T(1,128)S(1)} async-done(((f32[16,1,64]{2,1,0:T(1,128)}), f32[16,1,64]{2,1,0:T(1,128)S(1)}, u32[]{:S(2)}, u32[]{:S(2)}) %all-to-all-start.2) | async-done | bytes 4128 | tf_op jit(solution)/shard_map/all_to_all | solution.py:43
  136.3 0.7 convert_element_type.94
  137.0 9.8 %all-to-all-start.3 = ((bf16[32,1,2]{2,1,0:T(2,128)(2,1)}), bf16[32,1,2]{2,1,0:T(2,128)(2,1)S(1)}, u32[]{:S(2)}, u32[]{:S(2)}) async-start(bf16[32,1,2]{2,1,0:T(2,128)(2,1)} %convert_element_type.94), calls=%async_computation.4 | async-start | bytes 32768 | tf_op jit(solution)/shard_map/all_to_all | solution.py:118
  146.9 4.2 %fusion.4 = bf16[1,256,1664]{2,1,0:T(8,128)(2,1)} fusion(bf16[1024,256]{0,1:T(8,128)(2,1)S(1)} %get-tuple-element.5, bf16[1024,1664]{1,0:T(8,128)(2,1)} %reshape.135, f32[1024]{0:T(1024)S(1)} %reshape.140), kind=kOutput, calls=%fused_computation.7 | convolution fusion | flops 877953024 | bytes 4788224 | tf_op jit(solution)/shard_map/dot_general | solution.py:101
  151.0 36.7 %reduce-scatter.2.cloned.1.call-done = bf16[64,1664]{1,0:T(8,128)(2,1)} async-done(((bf16[1024,1664]{1,0:T(8,128)(2,1)}), bf16[64,1664]{1,0:T(8,128)(2,1)}) %reduce-scatter.2.cloned.1.call-update) | async-done | bytes 213008 | tf_op jit(solution)/shard_map/reduce_scatter | solution.py:112
  187.7 1.7 reshape.137
  189.5 9.7 %all-to-all-start.1 = ((bf16[32,2,1664]{2,1,0:T(2,128)(2,1)}), bf16[32,2,1664]{2,1,0:T(2,128)(2,1)S(1)}, u32[]{:S(2)}, u32[]{:S(2)}) async-start(bf16[32,2,1664]{2,1,0:T(2,128)(2,1)} %reshape.137), calls=%async_computation.2 | async-start | bytes 425984 | tf_op jit(solution)/shard_map/all_to_all | solution.py:117
  199.1 4.0 %fusion.3 = bf16[1,1664,256]{2,1,0:T(8,128)(2,1)} fusion(bf16[1024,1664]{1,0:T(8,128)(2,1)} %reshape.136, bf16[1024,256]{0,1:T(8,128)(2,1)S(1)} %get-tuple-element.8), kind=kOutput, calls=%fused_computation.6 | convolution fusion | flops 872841216 | bytes 4784128 | tf_op jit(solution)/shard_map/dot_general | solution.py:105
  203.4 0.5 convert_element_type.88
  204.0 5.8 %all-to-all-done.1 = bf16[32,2,1664]{2,1,0:T(2,128)(2,1)S(1)} async-done(((bf16[32,2,1664]{2,1,0:T(2,128)(2,1)}), bf16[32,2,1664]{2,1,0:T(2,128)(2,1)S(1)}, u32[]{:S(2)}, u32[]{:S(2)}) %all-to-all-start.1) | async-done | bytes 213024 | tf_op jit(solution)/shard_map/all_to_all | solution.py:117
  209.8 0.8 convolution_reduce_fusion
  (26 shorter events, 1.2 us)
Async XLA Ops:
  7.2 108.9 %copy-start = (bf16[1,1664,256]{2,1,0:T(8,128)(2,1)S(1)}, bf16[1,1664,256]{2,1,0:T(8,128)(2,1)}, u32[]{:S(2)}) copy-start(bf16[1,1664,256]{2,1,0:T(8,128)(2,1)} %param.10) | copy-start | bytes 2555908
  7.2 83.6 %all-gather.2.cloned.1.call-start = ((), (), s32[]{:S(2)}) async-start(), calls=%async_computation.5 | async-start | bytes 7520256 | tf_op jit(solution)/shard_map/all_gather | solution.py:29
  38.3 149.4 %reduce-scatter.2.cloned.1.call-start = ((), (), s32[]{:S(2)}) async-start(), calls=%async_computation.6 | async-start | bytes 3620864 | tf_op jit(solution)/shard_map/reduce_scatter | solution.py:112
  116.1 3.3 %copy-start.1 = (bf16[1024,1664]{1,0:T(8,128)(2,1)S(1)}, bf16[1024,1664]{1,0:T(8,128)(2,1)}, u32[]{:S(2)}) copy-start(bf16[1024,1664]{1,0:T(8,128)(2,1)} %reshape.135) | copy-start | bytes 10223620
  116.1 3.3 %copy-start.2 = (bf16[1,256,1664]{2,1,0:T(8,128)(2,1)S(1)}, bf16[1,256,1664]{2,1,0:T(8,128)(2,1)}, u32[]{:S(2)}) copy-start(bf16[1,256,1664]{2,1,0:T(8,128)(2,1)} %param.11) | copy-start | bytes 2555908
  124.5 11.7 %all-to-all-start.2 = ((f32[16,1,64]{2,1,0:T(1,128)}), f32[16,1,64]{2,1,0:T(1,128)S(1)}, u32[]{:S(2)}, u32[]{:S(2)}) async-start(f32[16,1,64]{2,1,0:T(1,128)} %all_to_all.18), calls=%async_computation.3 | async-start | bytes 16384 | tf_op jit(solution)/shard_map/all_to_all | solution.py:43
  137.0 52.4 %all-to-all-start.3 = ((bf16[32,1,2]{2,1,0:T(2,128)(2,1)}), bf16[32,1,2]{2,1,0:T(2,128)(2,1)S(1)}, u32[]{:S(2)}, u32[]{:S(2)}) async-start(bf16[32,1,2]{2,1,0:T(2,128)(2,1)} %convert_element_type.94), calls=%async_computation.4 | async-start | bytes 32768 | tf_op jit(solution)/shard_map/all_to_all | solution.py:118
  189.5 20.3 %all-to-all-start.1 = ((bf16[32,2,1664]{2,1,0:T(2,128)(2,1)}), bf16[32,2,1664]{2,1,0:T(2,128)(2,1)S(1)}, u32[]{:S(2)}, u32[]{:S(2)}) async-start(bf16[32,2,1664]{2,1,0:T(2,128)(2,1)} %reshape.137), calls=%async_computation.2 | async-start | bytes 425984 | tf_op jit(solution)/shard_map/all_to_all | solution.py:117
Sparse Core Ops, SparseCore 0:
  38.5 52.2 all-gather.1
  124.0 63.7 reduce-scatter.1
where the time goes:
time: 218 us; the launch traced here: 217 us
  waiting for transfers between devices  102 us (47%)
  local copies, waits for them, and re-layouts  31 us (14%)
  blocking collectives  26 us (12%)
  starting transfers between devices  23.8 us (11%)
  matrix products  17.4 us (8%)
  between operations  14.2 us (7%)
  other arithmetic  2.69 us (1%)
    all_gather x1, waiting for transfers between devices, in_one_piece(): whole = lax.all_gather(both, axis, axis=dim, tiled=True)  52.4 us
    reduce_scatter x1, waiting for transfers between devices, per_device(): row_sums = lax.psum_scatter(row_part, 'dp', scatter_dimension=0, tiled=True)  36.7 us
    all_to_all x1, blocking collectives, side_by_side(): lax.all_to_all(both, axis, split_axis=split_dim, concat_axis=concat_dim,...  26 us
    all_to_all x1, starting transfers between devices, per_device(): lax.all_to_all(gate_back, 'expert', split_axis=0, concat_axis=0, tiled=True)  9.85 us
    all_to_all x1, starting transfers between devices, per_device(): lax.all_to_all(row_back, 'expert', split_axis=0, concat_axis=0, tiled=True)  9.67 us
    reshape x1, local copies, waits for them, and re-layouts, per_device(): x_rows = x_blocks.reshape(count, feat)  8.11 us
    reshape x1, local copies, waits for them, and re-layouts, per_device(): cot_rows = cot_blocks.reshape(count, feat)  8.1 us
    all_to_all x1, waiting for transfers between devices, sent_and_summed(): lax.all_to_all(pieces, axis, split_axis=0, concat_axis=0, tiled=True)  7.43 us
  transfers between devices with their start and end apart: 5, of which 4 were waited for; matrix products, arithmetic and copies ran while one was open for 5% of the time, Pallas kernels for 0%

commit v1 on v0

v1 whole, which is shorter than its diff:
```python
import functools

import jax
import jax.numpy as jnp
from jax import lax
from jax.experimental import pallas as pl
from jax.experimental.pallas import tpu as pltpu
from jax.sharding import PartitionSpec as P


LANES = 128
F32, BF16 = jnp.float32, jnp.bfloat16


def mm(a, b, dims):
    return lax.dot_general(a, b, (dims, ((), ())), preferred_element_type=F32)


def kernel_call(body, out_shapes, *args, flops=0):
    spec = pl.BlockSpec(memory_space=pltpu.VMEM)
    outs = tuple(jax.ShapeDtypeStruct(s, d) for s, d in out_shapes)
    moved = sum(a.size * a.dtype.itemsize for a in args)
    return pl.pallas_call(
        body,
        out_shape=outs,
        in_specs=[spec] * len(args),
        out_specs=tuple([spec] * len(outs)),
        cost_estimate=pl.CostEstimate(flops=flops, bytes_accessed=moved, transcendentals=0),
    )(*args)


def matches(ids, cap, rows):
    tok = ids.shape[1]
    row = lax.broadcasted_iota(jnp.int32, (rows, tok), 0)
    expert, slot = row // cap, row % cap
    hit0 = (ids[0:1, :] == expert).astype(F32)
    hit1 = (ids[1:2, :] == expert).astype(F32)
    hit = hit0 + hit1
    earlier = (
        lax.broadcasted_iota(jnp.int32, (tok, tok), 0)
        < lax.broadcasted_iota(jnp.int32, (tok, tok), 1)
    ).astype(F32)
    before = mm(hit, earlier, ((1,), (0,)))
    held = hit * (before == slot.astype(F32)).astype(F32)
    return held, hit0, hit1


def dispatch_body(cap, rows, tok_ref, cot_ref, ids_ref, gates_ref, send_ref):
    feat = tok_ref.shape[1]
    held, hit0, hit1 = matches(ids_ref[...], cap, rows)
    gates = gates_ref[...].astype(F32)
    gate = jnp.sum(held * (hit0 * gates[0:1, :] + hit1 * gates[1:2, :]), axis=1, keepdims=True)
    pick = held.astype(BF16)
    send_ref[:, :feat] = mm(pick, tok_ref[...], ((1,), (0,))).astype(BF16)
    send_ref[:, feat : 2 * feat] = mm(pick, cot_ref[...], ((1,), (0,))).astype(BF16)
    send_ref[:, 2 * feat :] = jnp.broadcast_to(gate, (rows, LANES)).astype(BF16)


def tail(gate_part):
    hi = gate_part.astype(BF16).astype(F32)
    lo = gate_part - hi
    lane = lax.broadcasted_iota(jnp.int32, (gate_part.shape[0], LANES), 1)
    return jnp.where(lane == 0, hi, jnp.where(lane == 1, lo, 0.0)).astype(BF16)


def work_body(a_ref, b_ref, w1_ref, w1p_ref, w2_ref, w2p_ref, hid_ref, pg_ref, part_ref):
    feat = w1_ref.shape[0]
    half = w1_ref.shape[1]
    n = a_ref.shape[0]
    x = jnp.concatenate([a_ref[:, :feat], b_ref[:, :feat]], axis=0)
    cot = jnp.concatenate([a_ref[:, feat : 2 * feat], b_ref[:, feat : 2 * feat]], axis=0)
    gate = jnp.concatenate([a_ref[:, 2 * feat :], b_ref[:, 2 * feat :]], axis=0).astype(F32)
    gate = gate[:, 0:1]
    gate_part = jnp.zeros((2 * n, 1), F32)
    part = jnp.zeros((2 * n, feat), F32)
    for at, v1, v2 in ((0, w1_ref, w2_ref), (half, w1p_ref, w2p_ref)):
        pre = mm(x, v1[...], ((1,), (0,)))
        back = mm(cot, v2[...], ((1,), (1,)))
        cdf = 0.5 * (1.0 + lax.erf(pre * 0.7071067811865476))
        pdf = 0.3989422804014327 * jnp.exp(-0.5 * pre * pre)
        hidden = (pre * cdf).astype(BF16)
        pre_grad = (gate * back * (cdf + pre * pdf)).astype(BF16)
        hid_ref[:, at : at + half] = hidden
        pg_ref[:, at : at + half] = pre_grad
        gate_part += jnp.sum(hidden.astype(F32) * back, axis=1, keepdims=True)
        part += mm(pre_grad, v1[...], ((1,), (1,)))
    part_ref[:, :feat] = part.astype(BF16)
    part_ref[:, feat:] = tail(gate_part)


def plus_body(feat, *refs):
    *ins, out_ref = refs
    out_ref[:, :feat] = sum(r[:, :feat].astype(F32) for r in ins).astype(BF16)
    g = sum(r[:, feat:].astype(F32) for r in ins)
    out_ref[:, feat:] = tail(g[:, 0:1] + g[:, 1:2])


def plus_head_body(feat, n, s_ref, part_ref, out_ref):
    out_ref[:, :feat] = (s_ref[:n, :feat].astype(F32) + part_ref[:n, :feat].astype(F32)).astype(BF16)
    g = s_ref[:n, feat:].astype(F32) + part_ref[:n, feat:].astype(F32)
    out_ref[:, feat:] = tail(g[:, 0:1] + g[:, 1:2])


def total_body(feat, n, sa_ref, sb_ref, part_ref, out_ref):
    out_ref[:, :feat] = (
        sa_ref[:, :feat].astype(F32) + sb_ref[:, :feat].astype(F32) + part_ref[n:, :feat].astype(F32)
    ).astype(BF16)
    g = sa_ref[:, feat:].astype(F32) + sb_ref[:, feat:].astype(F32) + part_ref[n:, feat:].astype(F32)
    out_ref[:, feat:] = tail(g[:, 0:1] + g[:, 1:2])


def combine_body(cap, rows, back_ref, ids_ref, tg_ref, gg_ref):
    feat = tg_ref.shape[1]
    held, hit0, hit1 = matches(ids_ref[...], cap, rows)
    tg_ref[...] = mm(held.astype(BF16), back_ref[:, :feat], ((0,), (0,))).astype(BF16)
    g = back_ref[:, feat:].astype(F32)
    g = g[:, 0:1] + g[:, 1:2]
    g0 = jnp.sum(held * hit0 * g, axis=0, keepdims=True)
    g1 = jnp.sum(held * hit1 * g, axis=0, keepdims=True)
    gg_ref[...] = jnp.concatenate([g0, g1], axis=0).astype(BF16)


def per_device(tokens, cotangent, expert_ids, gates, w_in, w_out):
    tok, feat = tokens.shape
    experts = lax.axis_size("expert")
    ndp = lax.axis_size("dp")
    nz = ndp // 2
    cap = max(2, 4 * tok // experts)
    rows = experts * cap
    hops = nz // 2
    wide = 2 * feat + LANES
    slim = feat + LANES

    swap = [(i, i ^ 1) for i in range(ndp)]

    def shifted(sign):
        pairs = []
        for z in range(nz):
            pairs.append((2 * z, 2 * ((z + sign) % nz)))
            pairs.append((2 * z + 1, 2 * ((z - sign) % nz) + 1))
        return pairs

    away, home = shifted(1), shifted(-1)

    def move(a, pairs):
        return lax.ppermute(a, "dp", pairs)

    w1 = w_in[0]
    w2 = w_out[0]
    half = w1.shape[1]
    w1p = move(w1, swap)
    w2p = move(w2, swap)

    ids_t = expert_ids.T
    (send,) = kernel_call(
        functools.partial(dispatch_body, cap, rows), [((rows, wide), BF16)],
        tokens, cotangent, ids_t, gates.T,
    )
    send, w1p, w2p = lax.optimization_barrier((send, w1p, w2p))
    own = lax.all_to_all(
        send.reshape(experts, cap, wide), "expert", split_axis=0, concat_axis=0, tiled=True
    ).reshape(rows, wide)

    chain_a, chain_b = [], []
    a, b = own, move(own, swap)
    for k in range(1, hops + 1):
        a = move(a, away)
        chain_a.append(a)
        if k < hops:
            b = move(b, away)
            chain_b.append(b)
    firsts = chain_a
    seconds = [own] + chain_b

    hid, pg, part = [], [], []
    ff = 2 * half
    for k in range(hops):
        h, p, r = kernel_call(
            work_body,
            [((2 * rows, ff), BF16), ((2 * rows, ff), BF16), ((2 * rows, slim), BF16)],
            firsts[k], seconds[k], w1, w1p, w2, w2p,
            flops=2 * 3 * 2 * rows * feat * ff,
        )
        hid.append(h)
        pg.append(p)
        part.append(r)

    s = move(part[hops - 1], home)
    for k in range(hops - 2, 0, -1):
        (s,) = kernel_call(functools.partial(plus_body, feat), [((2 * rows, slim), BF16)], s, part[k])
        s = move(s, home)
    sb = move(s[rows:], swap)
    (sa,) = kernel_call(functools.partial(plus_head_body, feat, rows), [((rows, slim), BF16)], s, part[0])
    sa = move(sa, home)
    (total,) = kernel_call(functools.partial(total_body, feat, rows), [((rows, slim), BF16)], sa, sb, part[0])
    back_rows = lax.all_to_all(
        total.reshape(experts, cap, slim), "expert", split_axis=0, concat_axis=0, tiled=True
    ).reshape(rows, slim)

    blocks = []
    for k in range(hops):
        blocks += [firsts[k], seconds[k]]
    x_all = jnp.concatenate([c[:, :feat] for c in blocks], axis=0)
    scaled_all = jnp.concatenate(
        [(c[:, 2 * feat : 2 * feat + 1].astype(F32) * c[:, feat : 2 * feat].astype(F32)).astype(BF16) for c in blocks],
        axis=0,
    )
    hidden_all = jnp.concatenate(hid, axis=0)
    pg_all = jnp.concatenate(pg, axis=0)
    grad_second = mm(hidden_all, scaled_all, ((0,), (0,)))
    grad_first = mm(x_all, pg_all, ((0,), (0,)))
    gs = move(grad_second[half:].astype(BF16), swap)
    gf = move(grad_first[:, half:].astype(BF16), swap)
    grad_out_weights = (grad_second[:half] + gs.astype(F32)).astype(BF16)[None]
    grad_in_weights = (grad_first[:, :half] + gf.astype(F32)).astype(BF16)[None]

    token_grads, gate_t = kernel_call(
        functools.partial(combine_body, cap, rows),
        [((tok, feat), BF16), ((2, tok), BF16)], back_rows, ids_t,
    )
    return (token_grads, gate_t.T, grad_in_weights, grad_out_weights)


def solution(mesh):
    in_specs = (
        P(("expert", "dp"), None),
        P(("expert", "dp"), None),
        P(("expert", "dp"), None),
        P(("expert", "dp"), None),
        P("expert", None, "dp"),
        P("expert", "dp", None),
    )
    out_specs = (
        P(("expert", "dp"), None),
        P(("expert", "dp"), None),
        P("expert", None, "dp"),
        P("expert", "dp", None),
    )

    return jax.shard_map(per_device, mesh=mesh, in_specs=in_specs, out_specs=out_specs, check_vma=False)
```

time: 218 us -> 185 us (0.85)
  waiting for transfers between devices: 102 us -> 20.9 us
  starting transfers between devices: 23.8 us -> 62.3 us
  Pallas kernels: 0 us -> 32 us
  other arithmetic: 2.69 us -> 23.8 us
  local copies, waits for them, and re-layouts: 31 us -> 12.8 us
  matrix products: 17.4 us -> 3.89 us
  between operations: 14.2 us -> 1.02 us
    ppermute x0 -> x17, starting transfers between devices: none -> 57.4 us  [move(): return lax.ppermute(a, 'dp', pairs)]
    all_gather x1 -> x0, waiting for transfers between devices: 52.4 us -> none  [in_one_piece(): whole = lax.all_gather(both, axis, axis=dim, tiled=True)]
    reduce_scatter x1 -> x0, waiting for transfers between devices: 36.7 us -> none  [per_device(): row_sums = lax.psum_scatter(row_part, 'dp', scatter_dimension=0, tiled=True)]
    pallas_call x0 -> x10, Pallas kernels: none -> 32 us  [kernel_call(): pl.pallas_call(body, out_shape=outs, in_specs=[spec] * len(args), out_spe...]
    all_to_all x3 -> x1, starting transfers between devices: 23.7 us -> 4.89 us  [per_device(): lax.all_to_all(total.reshape(experts, cap, slim), 'expert', split_axis=0,...]
    dot_general x11 -> x2, matrix products: 17.4 us -> 3.89 us  [mm(): return lax.dot_general(a, b, (dims, ((), ())), preferred_element_type=F32)]
    reshape x10 -> x4, local copies, waits for them, and re-layouts: 18.4 us -> 5.08 us  [the longest x1 1.71 us: per_device(): back_rows = lax.all_to_all(total.reshape(experts, cap, slim), 'expert', s...]
    unnamed x0 -> x7, other arithmetic: none -> 11.8 us
  transfers between devices with their start and end apart: 5 -> 18, of which waited for: 4 -> 8; matrix products, arithmetic and copies ran while one was open for 5% -> 18% of each run, Pallas kernels for 0% -> 13%
where the time goes in v1:
time: 185 us; the launch traced here: 183 us
  starting transfers between devices  62.3 us (34%)
  Pallas kernels  32 us (17%)
  blocking collectives  26.3 us (14%)
  other arithmetic  23.8 us (13%)
  waiting for transfers between devices  20.9 us (11%)
  local copies, waits for them, and re-layouts  12.8 us (7%)
  matrix products  3.89 us (2%)
    ppermute x17, starting transfers between devices, move(): return lax.ppermute(a, 'dp', pairs)  57.4 us
    pallas_call x10, Pallas kernels, kernel_call(): pl.pallas_call(body, out_shape=outs, in_specs=[spec] * len(args), out_spe...  32 us
    all_to_all x1, blocking collectives, per_device(): lax.all_to_all(send.reshape(experts, cap, wide), 'expert', split_axis=0,...  26.3 us
    unnamed x7, other arithmetic  11.8 us
    ppermute x17, waiting for transfers between devices, move(): return lax.ppermute(a, 'dp', pairs)  10.8 us
    all_to_all x1, waiting for transfers between devices, per_device(): lax.all_to_all(total.reshape(experts, cap, slim), 'expert', split_axis=0,...  10.1 us
    mul x8, other arithmetic, per_device(): c[:, 2 * feat:2 * feat + 1].astype(F32) * c[:, feat:2 * feat].astype(F32)  5.16 us
    all_to_all x1, starting transfers between devices, per_device(): lax.all_to_all(total.reshape(experts, cap, slim), 'expert', split_axis=0,...  4.89 us
  transfers between devices with their start and end apart: 18, of which 8 were waited for; matrix products, arithmetic and copies ran while one was open for 18% of the time, Pallas kernels for 13%

profile of v1, /device:TPU:8, one launch (start us, length us, event | category | flops | bytes accessed | tf_op | source)
XLA Modules:
  0.0 183.0 jit_solution(321724332644375298)
XLA Ops:
  0.6 1.9 %collective-permute-start = (bf16[1664,256]{1,0:T(8,128)(2,1)}, bf16[1664,256]{1,0:T(8,128)(2,1)S(1)}, u32[]{:S(2)}, u32[]{:S(2)}) collective-permute-start(bf16[1664,256]{1,0:T(8,128)(2,1)} %bitcast.11), channel_id=1, source_target_pairs={{0,1},{1,0},{2,3},{3,2},{4,5},{5,4},{6,7},{7,6},{8,9},{9,8},{10,11... | collective-permute-start | bytes 2555912 | tf_op jit(solution)/shard_map/ppermute | solution.py:146
  2.6 2.4 %collective-permute-start.1 = (bf16[256,1664]{1,0:T(8,128)(2,1)}, bf16[256,1664]{1,0:T(8,128)(2,1)S(1)}, u32[]{:S(2)}, u32[]{:S(2)}) collective-permute-start(bf16[256,1664]{1,0:T(8,128)(2,1)} %bitcast.16), channel_id=1, source_target_pairs={{0,1},{1,0},{2,3},{3,2},{4,5},{5,4},{6,7},{7,6},{8,9},{9,8},{10,11... | collective-permute-start | bytes 2555912 | tf_op jit(solution)/shard_map/ppermute | solution.py:146
  5.0 2.0 %shard_map.93 = bf16[64,3456]{1,0:T(8,128)(2,1)} custom-call(bf16[16,1664]{1,0:T(8,128)(2,1)} %tok_ref.1, bf16[16,1664]{1,0:T(8,128)(2,1)} %cot_ref.1, s32[2,16]{1,0:T(2,128)} %bitcast.21, bf16[2,16]{1,0:T(2,128)(2,1)} %bitcast.23), custom_call_target="tpu_custom_call" | custom-call | bytes 106688 | tf_op jit(solution)/shard_map/pallas_call | solution.py:23
  8.7 26.3 %all_to_all.10 = bf16[32,2,3456]{2,1,0:T(2,128)(2,1)S(1)} all-to-all(bf16[32,2,3456]{2,1,0:T(2,128)(2,1)S(1)} %reshape.20), channel_id=1, replica_groups=mesh['expert'=32,'dp'=16] {'expert'}, dimensions={0} | all-to-all | bytes 884736 | tf_op jit(solution)/shard_map/all_to_all | solution.py:160
  35.2 4.3 %collective-permute-start.2 = (bf16[64,3456]{1,0:T(8,128)(2,1)S(1)}, bf16[64,3456]{1,0:T(8,128)(2,1)S(1)}, u32[]{:S(2)}, u32[]{:S(2)}) collective-permute-start(bf16[64,3456]{1,0:T(8,128)(2,1)S(1)} %reshape.21.b_ref), channel_id=1, source_target_pairs={{0,2},{1,15},{2,4},{3,1},{4,6},{5,3},{6,8},{7,5},{8,10},{9,7},{10,... | collective-permute-start | bytes 1327112 | tf_op jit(solution)/shard_map/ppermute | solution.py:146
  39.5 6.7 %collective-permute-start.6 = (bf16[64,3456]{1,0:T(8,128)(2,1)S(1)}, bf16[64,3456]{1,0:T(8,128)(2,1)}, u32[]{:S(2)}, u32[]{:S(2)}) collective-permute-start(bf16[64,3456]{1,0:T(8,128)(2,1)S(1)} %reshape.21.b_ref), channel_id=1, source_target_pairs={{0,1},{1,0},{2,3},{3,2},{4,5},{5,4},{6,7},{7,6},{8,9},{9,8},{10,11... | collective-permute-start | bytes 1327112 | tf_op jit(solution)/shard_map/ppermute | solution.py:146
  46.3 6.1 %collective-permute-done.2.a_ref = bf16[64,3456]{1,0:T(8,128)(2,1)S(1)} collective-permute-done((bf16[64,3456]{1,0:T(8,128)(2,1)S(1)}, bf16[64,3456]{1,0:T(8,128)(2,1)S(1)}, u32[]{:S(2)}, u32[]{:S(2)}) %collective-permute-start.2) | collective-permute-done | bytes 442400 | tf_op jit(solution)/shard_map/ppermute | solution.py:146
  54.5 1.9 %collective-permute-start.7 = (bf16[64,3456]{1,0:T(8,128)(2,1)}, bf16[64,3456]{1,0:T(8,128)(2,1)S(1)}, u32[]{:S(2)}, u32[]{:S(2)}) collective-permute-start(bf16[64,3456]{1,0:T(8,128)(2,1)} %collective-permute-done.6), channel_id=1, source_target_pairs={{0,2},{1,15},{2,4},{3,1},{4,6},{5,3},{6,8},{7,5},{8,10},{9,7},{10,... | collective-permute-start | bytes 1327112 | tf_op jit(solution)/shard_map/ppermute | solution.py:146
  57.2 4.9 %shard_map.99 = (bf16[128,512]{1,0:T(8,128)(2,1)}, bf16[128,512]{1,0:T(8,128)(2,1)}, bf16[128,1792]{1,0:T(8,128)(2,1)}) custom-call(bf16[64,3456]{1,0:T(8,128)(2,1)} %copy-done.10, bf16[64,3456]{1,0:T(8,128)(2,1)} %copy-done.2, bf16[1664,256]{1,0:T(8,128)(2,1)} %bitcast.12, bf16[1664,256]{1,0:T(8,128)(2,1)} %copy-done, bf16[256,1664]{1,0:T(8,128)(2,1)} %bitcast.17, ...), custom_call_target="tpu_custom_call" | custom-call | flops 654311424 | bytes 4292608 | tf_op jit(solution)/shard_map/pallas_call | solution.py:23
  63.9 3.1 %collective-permute-start.4 = (bf16[64,3456]{1,0:T(8,128)(2,1)S(1)}, bf16[64,3456]{1,0:T(8,128)(2,1)S(1)}, u32[]{:S(2)}, u32[]{:S(2)}) collective-permute-start(bf16[64,3456]{1,0:T(8,128)(2,1)S(1)} %collective-permute-done.3.a_ref), channel_id=1, source_target_pairs={{0,2},{1,15},{2,4},{3,1},{4,6},{5,3},{6,8},{7,5},{8,10},{9,7},{10,... | collective-permute-start | bytes 1327112 | tf_op jit(solution)/shard_map/ppermute | solution.py:146
  68.6 4.1 %collective-permute-start.8 = (bf16[64,3456]{1,0:T(8,128)(2,1)S(1)}, bf16[64,3456]{1,0:T(8,128)(2,1)S(1)}, u32[]{:S(2)}, u32[]{:S(2)}) collective-permute-start(bf16[64,3456]{1,0:T(8,128)(2,1)S(1)} %collective-permute-done.7.b_ref), channel_id=1, source_target_pairs={{0,2},{1,15},{2,4},{3,1},{4,6},{5,3},{6,8},{7,5},{8,10},{9,7},{10,... | collective-permute-start | bytes 1327112 | tf_op jit(solution)/shard_map/ppermute | solution.py:146
  72.7 4.9 %shard_map.97 = (bf16[128,512]{1,0:T(8,128)(2,1)}, bf16[128,512]{1,0:T(8,128)(2,1)}, bf16[128,1792]{1,0:T(8,128)(2,1)}) custom-call(bf16[64,3456]{1,0:T(8,128)(2,1)} %copy-done.5, bf16[64,3456]{1,0:T(8,128)(2,1)} %copy-done.6, bf16[1664,256]{1,0:T(8,128)(2,1)} %bitcast.13, bf16[1664,256]{1,0:T(8,128)(2,1)} %copy-done, bf16[256,1664]{1,0:T(8,128)(2,1)} %bitcast.18, ...), custom_call_target="tpu_custom_call" | custom-call | flops 654311424 | bytes 4292608 | tf_op jit(solution)/shard_map/pallas_call | solution.py:23
  82.9 2.2 %collective-permute-start.5 = (bf16[64,3456]{1,0:T(8,128)(2,1)S(1)}, bf16[64,3456]{1,0:T(8,128)(2,1)S(1)}, u32[]{:S(2)}, u32[]{:S(2)}) collective-permute-start(bf16[64,3456]{1,0:T(8,128)(2,1)S(1)} %collective-permute-done.4.a_ref), channel_id=1, source_target_pairs={{0,2},{1,15},{2,4},{3,1},{4,6},{5,3},{6,8},{7,5},{8,10},{9,7},{10,... | collective-permute-start | bytes 1327112 | tf_op jit(solution)/shard_map/ppermute | solution.py:146
  85.1 3.5 %collective-permute-start.9 = (bf16[64,3456]{1,0:T(8,128)(2,1)S(1)}, bf16[64,3456]{1,0:T(8,128)(2,1)S(1)}, u32[]{:S(2)}, u32[]{:S(2)}) collective-permute-start(bf16[64,3456]{1,0:T(8,128)(2,1)S(1)} %collective-permute-done.8.b_ref), channel_id=1, source_target_pairs={{0,2},{1,15},{2,4},{3,1},{4,6},{5,3},{6,8},{7,5},{8,10},{9,7},{10,... | collective-permute-start | bytes 1327112 | tf_op jit(solution)/shard_map/ppermute | solution.py:146
  88.6 4.9 %shard_map.95 = (bf16[128,512]{1,0:T(8,128)(2,1)}, bf16[128,512]{1,0:T(8,128)(2,1)}, bf16[128,1792]{1,0:T(8,128)(2,1)}) custom-call(bf16[64,3456]{1,0:T(8,128)(2,1)} %copy-done.4, bf16[64,3456]{1,0:T(8,128)(2,1)} %copy-done.7, bf16[1664,256]{1,0:T(8,128)(2,1)} %bitcast.14, bf16[1664,256]{1,0:T(8,128)(2,1)} %copy-done, bf16[256,1664]{1,0:T(8,128)(2,1)} %bitcast.19, ...), custom_call_target="tpu_custom_call" | custom-call | flops 654311424 | bytes 4292608 | tf_op jit(solution)/shard_map/pallas_call | solution.py:23
  100.4 4.9 %shard_map.94 = (bf16[128,512]{1,0:T(8,128)(2,1)}, bf16[128,512]{1,0:T(8,128)(2,1)}, bf16[128,1792]{1,0:T(8,128)(2,1)}) custom-call(bf16[64,3456]{1,0:T(8,128)(2,1)} %copy-done.8, bf16[64,3456]{1,0:T(8,128)(2,1)} %copy-done.9, bf16[1664,256]{1,0:T(8,128)(2,1)} %bitcast.15, bf16[1664,256]{1,0:T(8,128)(2,1)} %copy-done, bf16[256,1664]{1,0:T(8,128)(2,1)} %bitcast.20, ...), custom_call_target="tpu_custom_call" | custom-call | flops 654311424 | bytes 4292608 | tf_op jit(solution)/shard_map/pallas_call | solution.py:23
  105.3 3.8 %collective-permute-start.10 = (bf16[128,1792]{1,0:T(8,128)(2,1)}, bf16[128,1792]{1,0:T(8,128)(2,1)S(1)}, u32[]{:S(2)}, u32[]{:S(2)}) collective-permute-start(bf16[128,1792]{1,0:T(8,128)(2,1)} %get-tuple-element.24), channel_id=1, source_target_pairs={{0,14},{1,3},{2,0},{3,5},{4,2},{5,7},{6,4},{7,9},{8,6},{9,11},{10,... | collective-permute-start | bytes 1376264 | tf_op jit(solution)/shard_map/ppermute | solution.py:146
  116.8 2.2 %shard_map.96 = bf16[128,1792]{1,0:T(8,128)(2,1)} custom-call(bf16[128,1792]{1,0:T(8,128)(2,1)} %copy-done.11, bf16[128,1792]{1,0:T(8,128)(2,1)} %get-tuple-element.25.refs_1_), custom_call_target="tpu_custom_call" | custom-call | bytes 917504 | tf_op jit(solution)/shard_map/pallas_call | solution.py:23
  119.0 4.9 %collective-permute-start.11 = (bf16[128,1792]{1,0:T(8,128)(2,1)}, bf16[128,1792]{1,0:T(8,128)(2,1)S(1)}, u32[]{:S(2)}, u32[]{:S(2)}) collective-permute-start(bf16[128,1792]{1,0:T(8,128)(2,1)} %shard_map.96), channel_id=1, source_target_pairs={{0,14},{1,3},{2,0},{3,5},{4,2},{5,7},{6,4},{7,9},{8,6},{9,11},{10,... | collective-permute-start | bytes 1376264 | tf_op jit(solution)/shard_map/ppermute | solution.py:146
  127.8 1.9 %collective-permute-start.15 = (bf16[1664,256]{1,0:T(8,128)(2,1)}, bf16[1664,256]{1,0:T(8,128)(2,1)}, u32[]{:S(2)}, u32[]{:S(2)}) collective-permute-start(bf16[1664,256]{1,0:T(8,128)(2,1)} %slice.184), channel_id=1, source_target_pairs={{0,1},{1,0},{2,3},{3,2},{4,5},{5,4},{6,7},{7,6},{8,9},{9,8},{10,11... | collective-permute-start | bytes 2555912 | tf_op jit(solution)/shard_map/ppermute | solution.py:146
  131.0 2.2 %shard_map.98 = bf16[128,1792]{1,0:T(8,128)(2,1)} custom-call(bf16[128,1792]{1,0:T(8,128)(2,1)} %copy-done.12, bf16[128,1792]{1,0:T(8,128)(2,1)} %get-tuple-element.26.refs_1_), custom_call_target="tpu_custom_call" | custom-call | bytes 917504 | tf_op jit(solution)/shard_map/pallas_call | solution.py:23
  133.2 5.5 %collective-permute-start.12 = (bf16[128,1792]{1,0:T(8,128)(2,1)}, bf16[128,1792]{1,0:T(8,128)(2,1)}, u32[]{:S(2)}, u32[]{:S(2)}) collective-permute-start(bf16[128,1792]{1,0:T(8,128)(2,1)} %shard_map.98), channel_id=1, source_target_pairs={{0,14},{1,3},{2,0},{3,5},{4,2},{5,7},{6,4},{7,9},{8,6},{9,11},{10,... | collective-permute-start | bytes 1376264 | tf_op jit(solution)/shard_map/ppermute | solution.py:146
  138.7 2.8 %fusion.12 = f32[512,1664]{1,0:T(8,128)S(1)} fusion(bf16[512,1664]{1,0:T(8,128)(2,1)} %get-tuple-element.38, bf16[128,512]{1,0:T(8,128)(2,1)} %get-tuple-element.37, bf16[128,512]{1,0:T(8,128)(2,1)} %get-tuple-element.36, bf16[128,512]{1,0:T(8,128)(2,1)} %get-tuple-element.35, bf16[128,512]{1,0:T(8,128)(2,1)S(1)} %copy-done.13), kind=kOutput, calls=%fused_computation.16 | convolution fusion | flops 874512384 | bytes 5636096 | tf_op jit(solution)/shard_map/dot_general | solution.py:16
  142.5 1.9 %collective-permute-start.16 = (bf16[256,1664]{1,0:T(8,128)(2,1)}, bf16[256,1664]{1,0:T(8,128)(2,1)}, u32[]{:S(2)}, u32[]{:S(2)}) collective-permute-start(bf16[256,1664]{1,0:T(8,128)(2,1)} %slice.183), channel_id=1, source_target_pairs={{0,1},{1,0},{2,3},{3,2},{4,5},{5,4},{6,7},{7,6},{8,9},{9,8},{10,11... | collective-permute-start | bytes 2555912 | tf_op jit(solution)/shard_map/ppermute | solution.py:146
  145.0 2.0 %shard_map.100 = bf16[64,1792]{1,0:T(8,128)(2,1)} custom-call(bf16[128,1792]{1,0:T(8,128)(2,1)} %collective-permute-done.12.s_ref, bf16[128,1792]{1,0:T(8,128)(2,1)} %get-tuple-element.27.part_ref), custom_call_target="tpu_custom_call" | custom-call | bytes 917504 | tf_op jit(solution)/shard_map/pallas_call | solution.py:23
  147.0 5.6 %collective-permute-start.13 = (bf16[64,1792]{1,0:T(8,128)(2,1)}, bf16[64,1792]{1,0:T(8,128)(2,1)}, u32[]{:S(2)}, u32[]{:S(2)}) collective-permute-start(bf16[64,1792]{1,0:T(8,128)(2,1)} %shard_map.100), channel_id=1, source_target_pairs={{0,14},{1,3},{2,0},{3,5},{4,2},{5,7},{6,4},{7,9},{8,6},{9,11},{10,... | collective-permute-start | bytes 688136 | tf_op jit(solution)/shard_map/ppermute | solution.py:146
  153.5 1.9 %collective-permute-start.14 = (bf16[64,1792]{1,0:T(8,128)(2,1)S(1)}, bf16[64,1792]{1,0:T(8,128)(2,1)}, u32[]{:S(2)}, u32[]{:S(2)}) collective-permute-start(bf16[64,1792]{1,0:T(8,128)(2,1)S(1)} %slice.118), channel_id=1, source_target_pairs={{0,1},{1,0},{2,3},{3,2},{4,5},{5,4},{6,7},{7,6},{8,9},{9,8},{10,11... | collective-permute-start | bytes 688136 | tf_op jit(solution)/shard_map/ppermute | solution.py:146
  155.5 2.8 %fusion.2 = bf16[1,1664,256]{2,1,0:T(8,128)(2,1)} fusion(bf16[1664,256]{1,0:T(8,128)(2,1)} %collective-permute-done.15, f32[1664,512]{1,0:T(8,128)} %copy-done.3), kind=kLoop, calls=%fused_computation.6 | loop fusion | flops 1277952 | bytes 3407872 | tf_op jit(solution)/shard_map/broadcast_in_dim | solution.py:215
  158.3 2.1 %shard_map.101 = bf16[64,1792]{1,0:T(8,128)(2,1)} custom-call(bf16[64,1792]{1,0:T(8,128)(2,1)} %collective-permute-done.13.sa_ref, bf16[64,1792]{1,0:T(8,128)(2,1)} %collective-permute-done.14.sb_ref, bf16[128,1792]{1,0:T(8,128)(2,1)} %get-tuple-element.27.part_ref), custom_call_target="tpu_custom_call" | custom-call | bytes 917504 | tf_op jit(solution)/shard_map/pallas_call | solution.py:23
  162.1 4.9 %all-to-all-start.1 = ((bf16[32,2,1792]{2,1,0:T(2,128)(2,1)}), bf16[32,2,1792]{2,1,0:T(2,128)(2,1)}, u32[]{:S(2)}, u32[]{:S(2)}) async-start(bf16[32,2,1792]{2,1,0:T(2,128)(2,1)} %reshape.22), calls=%async_computation.1 | async-start | bytes 458752 | tf_op jit(solution)/shard_map/all_to_all | solution.py:196
  167.1 2.2 %fusion.3 = bf16[1,256,1664]{2,1,0:T(8,128)(2,1)} fusion(bf16[256,1664]{1,0:T(8,128)(2,1)} %collective-permute-done.16, f32[512,1664]{1,0:T(8,128)S(1)} %fusion.12), kind=kLoop, calls=%fused_computation.7 | loop fusion | flops 1277952 | bytes 3407872 | tf_op jit(solution)/shard_map/broadcast_in_dim | solution.py:214
  169.3 10.1 %all-to-all-done.1 = bf16[32,2,1792]{2,1,0:T(2,128)(2,1)} async-done(((bf16[32,2,1792]{2,1,0:T(2,128)(2,1)}), bf16[32,2,1792]{2,1,0:T(2,128)(2,1)}, u32[]{:S(2)}, u32[]{:S(2)}) %all-to-all-start.1) | async-done | bytes 229408 | tf_op jit(solution)/shard_map/all_to_all | solution.py:196
  (80 shorter events, 41.0 us)
Async XLA Ops:
  0.6 6.3 %collective-permute-start = (bf16[1664,256]{1,0:T(8,128)(2,1)}, bf16[1664,256]{1,0:T(8,128)(2,1)S(1)}, u32[]{:S(2)}, u32[]{:S(2)}) collective-permute-start(bf16[1664,256]{1,0:T(8,128)(2,1)} %bitcast.11), channel_id=1, source_target_pairs={{0,1},{1,0},{2,3},{3,2},{4,5},{5,4},{6,7},{7,6},{8,9},{9,8},{10,11... | collective-permute-start | bytes 2555912 | tf_op jit(solution)/shard_map/ppermute | solution.py:146
  2.6 4.6 %collective-permute-start.1 = (bf16[256,1664]{1,0:T(8,128)(2,1)}, bf16[256,1664]{1,0:T(8,128)(2,1)S(1)}, u32[]{:S(2)}, u32[]{:S(2)}) collective-permute-start(bf16[256,1664]{1,0:T(8,128)(2,1)} %bitcast.16), channel_id=1, source_target_pairs={{0,1},{1,0},{2,3},{3,2},{4,5},{5,4},{6,7},{7,6},{8,9},{9,8},{10,11... | collective-permute-start | bytes 2555912 | tf_op jit(solution)/shard_map/ppermute | solution.py:146
  7.0 50.2 %copy-start = (bf16[1664,256]{1,0:T(8,128)(2,1)}, bf16[1664,256]{1,0:T(8,128)(2,1)S(1)}, u32[]{:S(2)}) copy-start(bf16[1664,256]{1,0:T(8,128)(2,1)S(1)} %collective-permute-done.w1p_ref) | copy-start | bytes 2555908
  7.2 50.0 %copy-start.1 = (bf16[256,1664]{1,0:T(8,128)(2,1)}, bf16[256,1664]{1,0:T(8,128)(2,1)S(1)}, u32[]{:S(2)}) copy-start(bf16[256,1664]{1,0:T(8,128)(2,1)S(1)} %collective-permute-done.1.w2p_ref) | copy-start | bytes 2555908
  35.2 22.0 %copy-start.2 = (bf16[64,3456]{1,0:T(8,128)(2,1)}, bf16[64,3456]{1,0:T(8,128)(2,1)S(1)}, u32[]{:S(2)}) copy-start(bf16[64,3456]{1,0:T(8,128)(2,1)S(1)} %reshape.21.b_ref) | copy-start | bytes 1327108
  35.2 17.2 %collective-permute-start.2 = (bf16[64,3456]{1,0:T(8,128)(2,1)S(1)}, bf16[64,3456]{1,0:T(8,128)(2,1)S(1)}, u32[]{:S(2)}, u32[]{:S(2)}) collective-permute-start(bf16[64,3456]{1,0:T(8,128)(2,1)S(1)} %reshape.21.b_ref), channel_id=1, source_target_pairs={{0,2},{1,15},{2,4},{3,1},{4,6},{5,3},{6,8},{7,5},{8,10},{9,7},{10,... | collective-permute-start | bytes 1327112 | tf_op jit(solution)/shard_map/ppermute | solution.py:146
  39.5 15.0 %collective-permute-start.6 = (bf16[64,3456]{1,0:T(8,128)(2,1)S(1)}, bf16[64,3456]{1,0:T(8,128)(2,1)}, u32[]{:S(2)}, u32[]{:S(2)}) collective-permute-start(bf16[64,3456]{1,0:T(8,128)(2,1)S(1)} %reshape.21.b_ref), channel_id=1, source_target_pairs={{0,1},{1,0},{2,3},{3,2},{4,5},{5,4},{6,7},{7,6},{8,9},{9,8},{10,11... | collective-permute-start | bytes 1327112 | tf_op jit(solution)/shard_map/ppermute | solution.py:146
  52.4 4.8 %copy-start.10 = (bf16[64,3456]{1,0:T(8,128)(2,1)}, bf16[64,3456]{1,0:T(8,128)(2,1)S(1)}, u32[]{:S(2)}) copy-start(bf16[64,3456]{1,0:T(8,128)(2,1)S(1)} %collective-permute-done.2.a_ref) | copy-start | bytes 1327108
  52.4 11.5 %collective-permute-start.3 = (bf16[64,3456]{1,0:T(8,128)(2,1)S(1)}, bf16[64,3456]{1,0:T(8,128)(2,1)S(1)}, u32[]{:S(2)}, u32[]{:S(2)}) collective-permute-start(bf16[64,3456]{1,0:T(8,128)(2,1)S(1)} %collective-permute-done.2.a_ref), channel_id=1, source_target_pairs={{0,2},{1,15},{2,4},{3,1},{4,6},{5,3},{6,8},{7,5},{8,10},{9,7},{10,... | collective-permute-start | bytes 1327112 | tf_op jit(solution)/shard_map/ppermute | solution.py:146
  54.5 14.1 %collective-permute-start.7 = (bf16[64,3456]{1,0:T(8,128)(2,1)}, bf16[64,3456]{1,0:T(8,128)(2,1)S(1)}, u32[]{:S(2)}, u32[]{:S(2)}) collective-permute-start(bf16[64,3456]{1,0:T(8,128)(2,1)} %collective-permute-done.6), channel_id=1, source_target_pairs={{0,2},{1,15},{2,4},{3,1},{4,6},{5,3},{6,8},{7,5},{8,10},{9,7},{10,... | collective-permute-start | bytes 1327112 | tf_op jit(solution)/shard_map/ppermute | solution.py:146
  63.9 8.7 %copy-start.5 = (bf16[64,3456]{1,0:T(8,128)(2,1)}, bf16[64,3456]{1,0:T(8,128)(2,1)S(1)}, u32[]{:S(2)}) copy-start(bf16[64,3456]{1,0:T(8,128)(2,1)S(1)} %collective-permute-done.3.a_ref) | copy-start | bytes 1327108
  63.9 18.9 %collective-permute-start.4 = (bf16[64,3456]{1,0:T(8,128)(2,1)S(1)}, bf16[64,3456]{1,0:T(8,128)(2,1)S(1)}, u32[]{:S(2)}, u32[]{:S(2)}) collective-permute-start(bf16[64,3456]{1,0:T(8,128)(2,1)S(1)} %collective-permute-done.3.a_ref), channel_id=1, source_target_pairs={{0,2},{1,15},{2,4},{3,1},{4,6},{5,3},{6,8},{7,5},{8,10},{9,7},{10,... | collective-permute-start | bytes 1327112 | tf_op jit(solution)/shard_map/ppermute | solution.py:146
  68.6 4.1 %copy-start.6 = (bf16[64,3456]{1,0:T(8,128)(2,1)}, bf16[64,3456]{1,0:T(8,128)(2,1)S(1)}, u32[]{:S(2)}) copy-start(bf16[64,3456]{1,0:T(8,128)(2,1)S(1)} %collective-permute-done.7.b_ref) | copy-start | bytes 1327108
  68.6 16.5 %collective-permute-start.8 = (bf16[64,3456]{1,0:T(8,128)(2,1)S(1)}, bf16[64,3456]{1,0:T(8,128)(2,1)S(1)}, u32[]{:S(2)}, u32[]{:S(2)}) collective-permute-start(bf16[64,3456]{1,0:T(8,128)(2,1)S(1)} %collective-permute-done.7.b_ref), channel_id=1, source_target_pairs={{0,2},{1,15},{2,4},{3,1},{4,6},{5,3},{6,8},{7,5},{8,10},{9,7},{10,... | collective-permute-start | bytes 1327112 | tf_op jit(solution)/shard_map/ppermute | solution.py:146
  82.9 5.7 %copy-start.4 = (bf16[64,3456]{1,0:T(8,128)(2,1)}, bf16[64,3456]{1,0:T(8,128)(2,1)S(1)}, u32[]{:S(2)}) copy-start(bf16[64,3456]{1,0:T(8,128)(2,1)S(1)} %collective-permute-done.4.a_ref) | copy-start | bytes 1327108
  82.9 16.0 %collective-permute-start.5 = (bf16[64,3456]{1,0:T(8,128)(2,1)S(1)}, bf16[64,3456]{1,0:T(8,128)(2,1)S(1)}, u32[]{:S(2)}, u32[]{:S(2)}) collective-permute-start(bf16[64,3456]{1,0:T(8,128)(2,1)S(1)} %collective-permute-done.4.a_ref), channel_id=1, source_target_pairs={{0,2},{1,15},{2,4},{3,1},{4,6},{5,3},{6,8},{7,5},{8,10},{9,7},{10,... | collective-permute-start | bytes 1327112 | tf_op jit(solution)/shard_map/ppermute | solution.py:146
  85.0 3.6 %copy-start.7 = (bf16[64,3456]{1,0:T(8,128)(2,1)}, bf16[64,3456]{1,0:T(8,128)(2,1)S(1)}, u32[]{:S(2)}) copy-start(bf16[64,3456]{1,0:T(8,128)(2,1)S(1)} %collective-permute-done.8.b_ref) | copy-start | bytes 1327108
  85.1 10.1 %copy-start.14 = (bf16[512,1664]{1,0:T(8,128)(2,1)S(1)}, bf16[512,1664]{1,0:T(8,128)(2,1)}, u32[]{:S(2)}) copy-start(bf16[512,1664]{1,0:T(8,128)(2,1)} %get-tuple-element.47) | copy-start | bytes 5111812
  85.1 13.9 %collective-permute-start.9 = (bf16[64,3456]{1,0:T(8,128)(2,1)S(1)}, bf16[64,3456]{1,0:T(8,128)(2,1)S(1)}, u32[]{:S(2)}, u32[]{:S(2)}) collective-permute-start(bf16[64,3456]{1,0:T(8,128)(2,1)S(1)} %collective-permute-done.8.b_ref), channel_id=1, source_target_pairs={{0,2},{1,15},{2,4},{3,1},{4,6},{5,3},{6,8},{7,5},{8,10},{9,7},{10,... | collective-permute-start | bytes 1327112 | tf_op jit(solution)/shard_map/ppermute | solution.py:146
  105.3 18.6 %copy-start.15 = (bf16[128,512]{1,0:T(8,128)(2,1)S(1)}, bf16[128,512]{1,0:T(8,128)(2,1)}, u32[]{:S(2)}) copy-start(bf16[128,512]{1,0:T(8,128)(2,1)} %get-tuple-element.30) | copy-start | bytes 393220
  105.3 18.6 %copy-start.16 = (bf16[128,512]{1,0:T(8,128)(2,1)S(1)}, bf16[128,512]{1,0:T(8,128)(2,1)}, u32[]{:S(2)}) copy-start(bf16[128,512]{1,0:T(8,128)(2,1)} %get-tuple-element.31) | copy-start | bytes 393220
  105.3 18.6 %copy-start.17 = (bf16[128,512]{1,0:T(8,128)(2,1)S(1)}, bf16[128,512]{1,0:T(8,128)(2,1)}, u32[]{:S(2)}) copy-start(bf16[128,512]{1,0:T(8,128)(2,1)} %get-tuple-element.32) | copy-start | bytes 393220
  105.3 18.6 %copy-start.18 = (bf16[128,512]{1,0:T(8,128)(2,1)S(1)}, bf16[128,512]{1,0:T(8,128)(2,1)}, u32[]{:S(2)}) copy-start(bf16[128,512]{1,0:T(8,128)(2,1)} %get-tuple-element.33) | copy-start | bytes 393220
  105.3 10.7 %collective-permute-start.10 = (bf16[128,1792]{1,0:T(8,128)(2,1)}, bf16[128,1792]{1,0:T(8,128)(2,1)S(1)}, u32[]{:S(2)}, u32[]{:S(2)}) collective-permute-start(bf16[128,1792]{1,0:T(8,128)(2,1)} %get-tuple-element.24), channel_id=1, source_target_pairs={{0,14},{1,3},{2,0},{3,5},{4,2},{5,7},{6,4},{7,9},{8,6},{9,11},{10,... | collective-permute-start | bytes 1376264 | tf_op jit(solution)/shard_map/ppermute | solution.py:146
  119.0 11.2 %collective-permute-start.11 = (bf16[128,1792]{1,0:T(8,128)(2,1)}, bf16[128,1792]{1,0:T(8,128)(2,1)S(1)}, u32[]{:S(2)}, u32[]{:S(2)}) collective-permute-start(bf16[128,1792]{1,0:T(8,128)(2,1)} %shard_map.96), channel_id=1, source_target_pairs={{0,14},{1,3},{2,0},{3,5},{4,2},{5,7},{6,4},{7,9},{8,6},{9,11},{10,... | collective-permute-start | bytes 1376264 | tf_op jit(solution)/shard_map/ppermute | solution.py:146
  126.8 11.9 %copy-start.13 = (bf16[128,512]{1,0:T(8,128)(2,1)S(1)}, bf16[128,512]{1,0:T(8,128)(2,1)}, u32[]{:S(2)}) copy-start(bf16[128,512]{1,0:T(8,128)(2,1)} %get-tuple-element.34) | copy-start | bytes 393220
  127.8 27.7 %collective-permute-start.15 = (bf16[1664,256]{1,0:T(8,128)(2,1)}, bf16[1664,256]{1,0:T(8,128)(2,1)}, u32[]{:S(2)}, u32[]{:S(2)}) collective-permute-start(bf16[1664,256]{1,0:T(8,128)(2,1)} %slice.184), channel_id=1, source_target_pairs={{0,1},{1,0},{2,3},{3,2},{4,5},{5,4},{6,7},{7,6},{8,9},{9,8},{10,11... | collective-permute-start | bytes 2555912 | tf_op jit(solution)/shard_map/ppermute | solution.py:146
  133.2 11.8 %collective-permute-start.12 = (bf16[128,1792]{1,0:T(8,128)(2,1)}, bf16[128,1792]{1,0:T(8,128)(2,1)}, u32[]{:S(2)}, u32[]{:S(2)}) collective-permute-start(bf16[128,1792]{1,0:T(8,128)(2,1)} %shard_map.98), channel_id=1, source_target_pairs={{0,14},{1,3},{2,0},{3,5},{4,2},{5,7},{6,4},{7,9},{8,6},{9,11},{10,... | collective-permute-start | bytes 1376264 | tf_op jit(solution)/shard_map/ppermute | solution.py:146
  142.5 24.5 %collective-permute-start.16 = (bf16[256,1664]{1,0:T(8,128)(2,1)}, bf16[256,1664]{1,0:T(8,128)(2,1)}, u32[]{:S(2)}, u32[]{:S(2)}) collective-permute-start(bf16[256,1664]{1,0:T(8,128)(2,1)} %slice.183), channel_id=1, source_target_pairs={{0,1},{1,0},{2,3},{3,2},{4,5},{5,4},{6,7},{7,6},{8,9},{9,8},{10,11... | collective-permute-start | bytes 2555912 | tf_op jit(solution)/shard_map/ppermute | solution.py:146
  147.0 11.3 %collective-permute-start.13 = (bf16[64,1792]{1,0:T(8,128)(2,1)}, bf16[64,1792]{1,0:T(8,128)(2,1)}, u32[]{:S(2)}, u32[]{:S(2)}) collective-permute-start(bf16[64,1792]{1,0:T(8,128)(2,1)} %shard_map.100), channel_id=1, source_target_pairs={{0,14},{1,3},{2,0},{3,5},{4,2},{5,7},{6,4},{7,9},{8,6},{9,11},{10,... | collective-permute-start | bytes 688136 | tf_op jit(solution)/shard_map/ppermute | solution.py:146
  153.5 4.8 %collective-permute-start.14 = (bf16[64,1792]{1,0:T(8,128)(2,1)S(1)}, bf16[64,1792]{1,0:T(8,128)(2,1)}, u32[]{:S(2)}, u32[]{:S(2)}) collective-permute-start(bf16[64,1792]{1,0:T(8,128)(2,1)S(1)} %slice.118), channel_id=1, source_target_pairs={{0,1},{1,0},{2,3},{3,2},{4,5},{5,4},{6,7},{7,6},{8,9},{9,8},{10,11... | collective-permute-start | bytes 688136 | tf_op jit(solution)/shard_map/ppermute | solution.py:146
  162.1 17.2 %all-to-all-start.1 = ((bf16[32,2,1792]{2,1,0:T(2,128)(2,1)}), bf16[32,2,1792]{2,1,0:T(2,128)(2,1)}, u32[]{:S(2)}, u32[]{:S(2)}) async-start(bf16[32,2,1792]{2,1,0:T(2,128)(2,1)} %reshape.22), calls=%async_computation.1 | async-start | bytes 458752 | tf_op jit(solution)/shard_map/all_to_all | solution.py:196
  (5 other events, 4.8 us)

commit v2 on v1

v2 whole, which is shorter than its diff:
```python
import functools

import jax
import jax.numpy as jnp
from jax import lax
from jax.experimental import pallas as pl
from jax.experimental.pallas import tpu as pltpu
from jax.sharding import PartitionSpec as P


LANES = 128
F32, BF16 = jnp.float32, jnp.bfloat16


def mm(a, b, dims):
    return lax.dot_general(a, b, (dims, ((), ())), preferred_element_type=F32)


def kernel_call(body, out_shapes, *args, flops=0, limit=4):
    spec = pl.BlockSpec(memory_space=pltpu.VMEM)
    outs = tuple(jax.ShapeDtypeStruct(s, d) for s, d in out_shapes)
    moved = sum(a.size * a.dtype.itemsize for a in args)
    return pl.pallas_call(
        body,
        out_shape=outs,
        in_specs=[spec] * len(args),
        out_specs=tuple([spec] * len(outs)),
        compiler_params=pltpu.CompilerParams(vmem_limit_bytes=limit << 20),
        cost_estimate=pl.CostEstimate(flops=flops, bytes_accessed=moved, transcendentals=0),
    )(*args)


def matches(ids, cap, rows):
    tok = ids.shape[1]
    row = lax.broadcasted_iota(jnp.int32, (rows, tok), 0)
    expert, slot = row // cap, row % cap
    hit0 = (ids[0:1, :] == expert).astype(F32)
    hit1 = (ids[1:2, :] == expert).astype(F32)
    hit = hit0 + hit1
    earlier = (
        lax.broadcasted_iota(jnp.int32, (tok, tok), 0)
        < lax.broadcasted_iota(jnp.int32, (tok, tok), 1)
    ).astype(F32)
    before = mm(hit, earlier, ((1,), (0,)))
    held = hit * (before == slot.astype(F32)).astype(F32)
    return held, hit0, hit1


def dispatch_body(cap, rows, tok_hbm, cot_hbm, ids_hbm, gates_hbm, send_ref, tok_ref, cot_ref, ids_ref, gates_ref, sems):
    feat = tok_ref.shape[1]
    pairs = ((ids_hbm, ids_ref), (gates_hbm, gates_ref), (tok_hbm, tok_ref), (cot_hbm, cot_ref))
    copies = [pltpu.make_async_copy(a, b, sems.at[k]) for k, (a, b) in enumerate(pairs)]
    for c in copies:
        c.start()
    for c in copies:
        c.wait()
    held, hit0, hit1 = matches(ids_ref[...], cap, rows)
    gates = gates_ref[...].astype(F32)
    gate = jnp.sum(held * (hit0 * gates[0:1, :] + hit1 * gates[1:2, :]), axis=1, keepdims=True)
    pick = held.astype(BF16)
    send_ref[:, :feat] = mm(pick, tok_ref[...], ((1,), (0,))).astype(BF16)
    send_ref[:, feat:] = (gate * mm(pick, cot_ref[...], ((1,), (0,)))).astype(BF16)


def tail(gate_part):
    hi = gate_part.astype(BF16).astype(F32)
    lo = gate_part - hi
    lane = lax.broadcasted_iota(jnp.int32, (gate_part.shape[0], LANES), 1)
    return jnp.where(lane == 0, hi, jnp.where(lane == 1, lo, 0.0)).astype(BF16)


def work_body(a_ref, b_ref, w1_ref, w1p_ref, w2_ref, w2p_ref, hid_ref, pg_ref, pa_ref, pb_ref):
    feat = w1_ref.shape[0]
    half = w1_ref.shape[1]
    n = a_ref.shape[0]
    x = jnp.concatenate([a_ref[:, :feat], b_ref[:, :feat]], axis=0)
    scaled = jnp.concatenate([a_ref[:, feat:], b_ref[:, feat:]], axis=0)
    gate_part = jnp.zeros((2 * n, 1), F32)
    part = jnp.zeros((2 * n, feat), F32)
    for at, v1, v2 in ((0, w1_ref, w2_ref), (half, w1p_ref, w2p_ref)):
        pre = mm(x, v1[...], ((1,), (0,)))
        back = mm(scaled, v2[...], ((1,), (1,)))
        cdf = 0.5 * (1.0 + lax.erf(pre * 0.7071067811865476))
        pdf = 0.3989422804014327 * jnp.exp(-0.5 * pre * pre)
        hidden = (pre * cdf).astype(BF16)
        pre_grad = (back * (cdf + pre * pdf)).astype(BF16)
        hid_ref[:, at : at + half] = hidden
        pg_ref[:, at : at + half] = pre_grad
        gate_part += jnp.sum(hidden.astype(F32) * back, axis=1, keepdims=True)
        part += mm(pre_grad, v1[...], ((1,), (1,)))
    gates = tail(gate_part)
    pa_ref[:, :feat] = part[:n].astype(BF16)
    pb_ref[:, :feat] = part[n:].astype(BF16)
    pa_ref[:, feat:] = gates[:n]
    pb_ref[:, feat:] = gates[n:]


def plus_body(feat, *refs):
    *ins, out_ref = refs
    out_ref[:, :feat] = sum(r[:, :feat].astype(F32) for r in ins).astype(BF16)
    g = sum(r[:, feat:].astype(F32) for r in ins)
    out_ref[:, feat:] = tail(g[:, 0:1] + g[:, 1:2])


def combine_body(cap, rows, back_ref, ids_ref, gates_ref, tg_ref, gg_ref):
    feat = tg_ref.shape[1]
    held, hit0, hit1 = matches(ids_ref[...], cap, rows)
    tg_ref[...] = mm(held.astype(BF16), back_ref[:, :feat], ((0,), (0,))).astype(BF16)
    g = back_ref[:, feat:].astype(F32)
    g = g[:, 0:1] + g[:, 1:2]
    g0 = jnp.sum(held * hit0 * g, axis=0, keepdims=True)
    g1 = jnp.sum(held * hit1 * g, axis=0, keepdims=True)
    sums = jnp.concatenate([g0, g1], axis=0)
    gg_ref[...] = (sums / gates_ref[...].astype(F32)).astype(BF16)


def per_device(tokens, cotangent, expert_ids, gates, w_in, w_out):
    tok, feat = tokens.shape
    experts = lax.axis_size("expert")
    ndp = lax.axis_size("dp")
    nz = ndp // 2
    cap = max(2, 4 * tok // experts)
    rows = experts * cap
    hops = nz // 2
    wide = 2 * feat
    slim = feat + LANES

    swap = [(i, i ^ 1) for i in range(ndp)]

    def shifted(step, cross=0):
        pairs = []
        for z in range(nz):
            for core in range(2):
                up = step if core == 0 else -step
                pairs.append((2 * z + core, 2 * ((z + up) % nz) + (core ^ cross)))
        return pairs

    away, home = shifted(1), shifted(-1)
    over = shifted(-1, 1)

    def move(a, pairs):
        return lax.ppermute(a, "dp", pairs)

    w1 = w_in[0]
    w2 = w_out[0]
    half = w1.shape[1]
    w1p = move(w1, swap)
    w2p = move(w2, swap)

    ids_t, gates_t = expert_ids.T, gates.T
    taken = [pltpu.with_memory_space_constraint(a, pltpu.HBM) for a in (tokens, cotangent, ids_t, gates_t)]
    send = pl.pallas_call(
        functools.partial(dispatch_body, cap, rows),
        out_shape=jax.ShapeDtypeStruct((rows, wide), BF16),
        in_specs=[pl.BlockSpec(memory_space=pltpu.HBM)] * 4,
        out_specs=pl.BlockSpec(memory_space=pltpu.VMEM),
        scratch_shapes=[pltpu.VMEM(a.shape, a.dtype) for a in taken] + [pltpu.SemaphoreType.DMA((4,))],
        name="dispatch",
        compiler_params=pltpu.CompilerParams(vmem_limit_bytes=4 << 20),
    )(*taken)
    own = lax.all_to_all(
        send.reshape(experts, cap, wide), "expert", split_axis=0, concat_axis=0, tiled=True
    ).reshape(rows, wide)

    chain_a, chain_b = [], []
    a = b = own
    for k in range(1, hops + 1):
        a = move(a, away)
        chain_a.append(a)
        if k < hops:
            b = move(b, over if k == 1 else away)
            chain_b.append(b)
    firsts = chain_a
    seconds = chain_b + [own]

    hid, pg, part_a, part_b = [], [], [], []
    ff = 2 * half
    for k in range(hops):
        h, p, ra, rb = kernel_call(
            work_body,
            [((2 * rows, ff), BF16), ((2 * rows, ff), BF16), ((rows, slim), BF16), ((rows, slim), BF16)],
            firsts[k], seconds[k], w1, w1p, w2, w2p,
            limit=16, flops=2 * 3 * 2 * rows * feat * ff,
        )
        hid.append(h)
        pg.append(p)
        part_a.append(ra)
        part_b.append(rb)

    def plus(*args):
        return kernel_call(functools.partial(plus_body, feat), [((rows, slim), BF16)], *args)[0]

    sb = move(part_b[hops - 2], home)
    for k in range(hops - 3, -1, -1):
        sb = move(plus(sb, part_b[k]), over if k == 0 else home)
    sa = move(part_a[hops - 1], home)
    for k in range(hops - 2, -1, -1):
        sa = move(plus(sa, part_a[k]), home)
    total = plus(sa, sb, part_b[hops - 1])
    back_rows = lax.all_to_all(
        total.reshape(experts, cap, slim), "expert", split_axis=0, concat_axis=0, tiled=True
    ).reshape(rows, slim)

    blocks = []
    for k in range(hops):
        blocks += [firsts[k], seconds[k]]
    x_all = jnp.concatenate([c[:, :feat] for c in blocks], axis=0)
    scaled_all = jnp.concatenate([c[:, feat:] for c in blocks], axis=0)
    hidden_all = jnp.concatenate(hid, axis=0)
    pg_all = jnp.concatenate(pg, axis=0)
    peer_second = mm(hidden_all[:, half:], scaled_all, ((0,), (0,))).astype(BF16)
    peer_first = mm(x_all, pg_all[:, half:], ((0,), (0,))).astype(BF16)
    gs = move(peer_second, swap)
    gf = move(peer_first, swap)
    own_second = mm(hidden_all[:, :half], scaled_all, ((0,), (0,)))
    own_first = mm(x_all, pg_all[:, :half], ((0,), (0,)))
    grad_out_weights = (own_second + gs.astype(F32)).astype(BF16)[None]
    grad_in_weights = (own_first + gf.astype(F32)).astype(BF16)[None]

    token_grads, gate_t = kernel_call(
        functools.partial(combine_body, cap, rows),
        [((tok, feat), BF16), ((2, tok), BF16)], back_rows, ids_t, gates_t,
    )
    return (token_grads, gate_t.T, grad_in_weights, grad_out_weights)


def solution(mesh):
    in_specs = (
        P(("expert", "dp"), None),
        P(("expert", "dp"), None),
        P(("expert", "dp"), None),
        P(("expert", "dp"), None),
        P("expert", None, "dp"),
        P("expert", "dp", None),
    )
    out_specs = (
        P(("expert", "dp"), None),
        P(("expert", "dp"), None),
        P("expert", None, "dp"),
        P("expert", "dp", None),
    )

    return jax.shard_map(per_device, mesh=mesh, in_specs=in_specs, out_specs=out_specs, check_vma=False)
```

time: 185 us -> 159 us (0.86)
  waiting for transfers between devices: 20.9 us -> 67.4 us
  blocking collectives: 26.3 us -> 0 us
  other arithmetic: 23.8 us -> 0 us
  Pallas kernels: 32 us -> 11.4 us
  local copies, waits for them, and re-layouts: 12.8 us -> 4.17 us
  matrix products: 3.89 us -> 7.92 us
  starting transfers between devices: 62.3 us -> 66.1 us
    ppermute x17 -> x18, waiting for transfers between devices: 10.8 us -> 48.4 us  [move(): return lax.ppermute(a, 'dp', pairs)]
    all_to_all x1 -> x0, blocking collectives: 26.3 us -> none  [per_device(): lax.all_to_all(send.reshape(experts, cap, wide), 'expert', split_axis=0,...]
    pallas_call x10 -> x11, Pallas kernels: 32 us -> 9.99 us  [kernel_call(): pl.pallas_call(body, out_shape=outs, in_specs=[spec] * len(args), out_spe...]
    unnamed x7 -> x0, other arithmetic: 11.8 us -> none
    all_to_all x0 -> x1, waiting for transfers between devices: none -> 11.3 us  [per_device(): lax.all_to_all(send.reshape(experts, cap, wide), 'expert', split_axis=0,...]
    all_to_all x0 -> x1, starting transfers between devices: none -> 10.2 us  [per_device(): lax.all_to_all(send.reshape(experts, cap, wide), 'expert', split_axis=0,...]
    ppermute x17 -> x18, starting transfers between devices: 57.4 us -> 51.2 us  [move(): return lax.ppermute(a, 'dp', pairs)]
    mul x8 -> x0, other arithmetic: 5.16 us -> none  [per_device(): c[:, 2 * feat:2 * feat + 1].astype(F32) * c[:, feat:2 * feat].astype(F32)]
  transfers between devices with their start and end apart: 18 -> 20, of which waited for: 8 -> 14; matrix products, arithmetic and copies ran while one was open for 18% -> 7% of each run, Pallas kernels for 13% -> 2%
where the time goes in v2:
time: 159 us; the launch traced here: 158 us
  waiting for transfers between devices  67.4 us (42%)
  starting transfers between devices  66.1 us (42%)
  Pallas kernels  11.4 us (7%)
  matrix products  7.92 us (5%)
  local copies, waits for them, and re-layouts  4.17 us (3%)
    ppermute x18, starting transfers between devices, move(): return lax.ppermute(a, 'dp', pairs)  51.2 us
    ppermute x18, waiting for transfers between devices, move(): return lax.ppermute(a, 'dp', pairs)  48.4 us
    all_to_all x1, waiting for transfers between devices, per_device(): lax.all_to_all(send.reshape(experts, cap, wide), 'expert', split_axis=0,...  11.3 us
    all_to_all x1, starting transfers between devices, per_device(): lax.all_to_all(send.reshape(experts, cap, wide), 'expert', split_axis=0,...  10.2 us
    pallas_call x11, Pallas kernels, kernel_call(): pl.pallas_call(body, out_shape=outs, in_specs=[spec] * len(args), out_spe...  9.99 us
    dot_general x4, matrix products, mm(): return lax.dot_general(a, b, (dims, ((), ())), preferred_element_type=F32)  7.92 us
    all_to_all x1, waiting for transfers between devices, per_device(): lax.all_to_all(total.reshape(experts, cap, slim), 'expert', split_axis=0,...  7.67 us
    all_to_all x1, starting transfers between devices, per_device(): lax.all_to_all(total.reshape(experts, cap, slim), 'expert', split_axis=0,...  4.71 us
  transfers between devices with their start and end apart: 20, of which 14 were waited for; matrix products, arithmetic and copies ran while one was open for 7% of the time, Pallas kernels for 2%

profile of v2, /device:TPU:8, one launch (start us, length us, event | category | flops | bytes accessed | tf_op | source)
XLA Modules:
  0.0 158.1 jit_solution(1912053917630580328)
XLA Ops:
  3.0 10.2 %all-to-all-start = ((bf16[32,2,3328]{2,1,0:T(2,128)(2,1)}), bf16[32,2,3328]{2,1,0:T(2,128)(2,1)}, u32[]{:S(2)}, u32[]{:S(2)}) async-start(bf16[32,2,3328]{2,1,0:T(2,128)(2,1)} %reshape.20), calls=%async_computation | async-start | bytes 851968 | tf_op jit(solution)/shard_map/all_to_all | solution.py:161
  13.2 1.9 %collective-permute-start.4 = (bf16[1664,256]{1,0:T(8,128)(2,1)S(1)}, bf16[1664,256]{1,0:T(8,128)(2,1)S(1)}, u32[]{:S(2)}, u32[]{:S(2)}) collective-permute-start(bf16[1664,256]{1,0:T(8,128)(2,1)S(1)} %bitcast.13), channel_id=1, source_target_pairs={{0,1},{1,0},{2,3},{3,2},{4,5},{5,4},{6,7},{7,6},{8,9},{9,8},{10,11... | collective-permute-start | bytes 2555912 | tf_op jit(solution)/shard_map/ppermute | solution.py:142
  15.1 2.4 %collective-permute-start.5 = (bf16[256,1664]{1,0:T(8,128)(2,1)S(1)}, bf16[256,1664]{1,0:T(8,128)(2,1)S(1)}, u32[]{:S(2)}, u32[]{:S(2)}) collective-permute-start(bf16[256,1664]{1,0:T(8,128)(2,1)S(1)} %bitcast.18), channel_id=1, source_target_pairs={{0,1},{1,0},{2,3},{3,2},{4,5},{5,4},{6,7},{7,6},{8,9},{9,8},{10,11... | collective-permute-start | bytes 2555912 | tf_op jit(solution)/shard_map/ppermute | solution.py:142
  17.5 11.3 %all-to-all-done = bf16[32,2,3328]{2,1,0:T(2,128)(2,1)} async-done(((bf16[32,2,3328]{2,1,0:T(2,128)(2,1)}), bf16[32,2,3328]{2,1,0:T(2,128)(2,1)}, u32[]{:S(2)}, u32[]{:S(2)}) %all-to-all-start) | async-done | bytes 426016 | tf_op jit(solution)/shard_map/all_to_all | solution.py:161
  28.9 1.9 %reshape.21.b_ref = bf16[64,3328]{1,0:T(8,128)(2,1)} reshape(bf16[32,2,3328]{2,1,0:T(2,128)(2,1)} %all-to-all-done) | data formatting | bytes 851968 | tf_op jit(solution)/shard_map/reshape | solution.py:163
  30.8 8.4 %collective-permute-start.7 = (bf16[64,3328]{1,0:T(8,128)(2,1)}, bf16[64,3328]{1,0:T(8,128)(2,1)S(1)}, u32[]{:S(2)}, u32[]{:S(2)}) collective-permute-start(bf16[64,3328]{1,0:T(8,128)(2,1)} %reshape.21.b_ref), channel_id=1, source_target_pairs={{0,15},{1,2},{2,1},{3,4},{4,3},{5,6},{6,5},{7,8},{8,7},{9,10},{10,... | collective-permute-start | bytes 1277960 | tf_op jit(solution)/shard_map/ppermute | solution.py:142
  39.2 1.9 %collective-permute-start = (bf16[64,3328]{1,0:T(8,128)(2,1)}, bf16[64,3328]{1,0:T(8,128)(2,1)S(1)}, u32[]{:S(2)}, u32[]{:S(2)}) collective-permute-start(bf16[64,3328]{1,0:T(8,128)(2,1)} %reshape.21.b_ref), channel_id=1, source_target_pairs={{0,2},{1,15},{2,4},{3,1},{4,6},{5,3},{6,8},{7,5},{8,10},{9,7},{10,... | collective-permute-start | bytes 1277960 | tf_op jit(solution)/shard_map/ppermute | solution.py:142
  41.2 7.2 %collective-permute-done.7.b_ref = bf16[64,3328]{1,0:T(8,128)(2,1)S(1)} collective-permute-done((bf16[64,3328]{1,0:T(8,128)(2,1)}, bf16[64,3328]{1,0:T(8,128)(2,1)S(1)}, u32[]{:S(2)}, u32[]{:S(2)}) %collective-permute-start.7) | collective-permute-done | bytes 426016 | tf_op jit(solution)/shard_map/ppermute | solution.py:142
  48.4 2.3 %collective-permute-done.a_ref = bf16[64,3328]{1,0:T(8,128)(2,1)S(1)} collective-permute-done((bf16[64,3328]{1,0:T(8,128)(2,1)}, bf16[64,3328]{1,0:T(8,128)(2,1)S(1)}, u32[]{:S(2)}, u32[]{:S(2)}) %collective-permute-start) | collective-permute-done | bytes 426016 | tf_op jit(solution)/shard_map/ppermute | solution.py:142
  52.6 1.9 %collective-permute-start.8 = (bf16[64,3328]{1,0:T(8,128)(2,1)S(1)}, bf16[64,3328]{1,0:T(8,128)(2,1)S(1)}, u32[]{:S(2)}, u32[]{:S(2)}) collective-permute-start(bf16[64,3328]{1,0:T(8,128)(2,1)S(1)} %collective-permute-done.7.b_ref), channel_id=1, source_target_pairs={{0,2},{1,15},{2,4},{3,1},{4,6},{5,3},{6,8},{7,5},{8,10},{9,7},{10,... | collective-permute-start | bytes 1277960 | tf_op jit(solution)/shard_map/ppermute | solution.py:142
  54.5 1.9 %collective-permute-start.1 = (bf16[64,3328]{1,0:T(8,128)(2,1)S(1)}, bf16[64,3328]{1,0:T(8,128)(2,1)S(1)}, u32[]{:S(2)}, u32[]{:S(2)}) collective-permute-start(bf16[64,3328]{1,0:T(8,128)(2,1)S(1)} %collective-permute-done.a_ref), channel_id=1, source_target_pairs={{0,2},{1,15},{2,4},{3,1},{4,6},{5,3},{6,8},{7,5},{8,10},{9,7},{10,... | collective-permute-start | bytes 1277960 | tf_op jit(solution)/shard_map/ppermute | solution.py:142
  56.5 7.5 %collective-permute-done.8.b_ref = bf16[64,3328]{1,0:T(8,128)(2,1)S(1)} collective-permute-done((bf16[64,3328]{1,0:T(8,128)(2,1)S(1)}, bf16[64,3328]{1,0:T(8,128)(2,1)S(1)}, u32[]{:S(2)}, u32[]{:S(2)}) %collective-permute-start.8) | collective-permute-done | bytes 426016 | tf_op jit(solution)/shard_map/ppermute | solution.py:142
  64.0 4.6 %collective-permute-done.1.a_ref = bf16[64,3328]{1,0:T(8,128)(2,1)S(1)} collective-permute-done((bf16[64,3328]{1,0:T(8,128)(2,1)S(1)}, bf16[64,3328]{1,0:T(8,128)(2,1)S(1)}, u32[]{:S(2)}, u32[]{:S(2)}) %collective-permute-start.1) | collective-permute-done | bytes 426016 | tf_op jit(solution)/shard_map/ppermute | solution.py:142
  70.5 1.9 %collective-permute-start.9 = (bf16[64,3328]{1,0:T(8,128)(2,1)S(1)}, bf16[64,3328]{1,0:T(8,128)(2,1)S(1)}, u32[]{:S(2)}, u32[]{:S(2)}) collective-permute-start(bf16[64,3328]{1,0:T(8,128)(2,1)S(1)} %collective-permute-done.8.b_ref), channel_id=1, source_target_pairs={{0,2},{1,15},{2,4},{3,1},{4,6},{5,3},{6,8},{7,5},{8,10},{9,7},{10,... | collective-permute-start | bytes 1277960 | tf_op jit(solution)/shard_map/ppermute | solution.py:142
  72.5 1.9 %collective-permute-start.2 = (bf16[64,3328]{1,0:T(8,128)(2,1)S(1)}, bf16[64,3328]{1,0:T(8,128)(2,1)S(1)}, u32[]{:S(2)}, u32[]{:S(2)}) collective-permute-start(bf16[64,3328]{1,0:T(8,128)(2,1)S(1)} %collective-permute-done.1.a_ref), channel_id=1, source_target_pairs={{0,2},{1,15},{2,4},{3,1},{4,6},{5,3},{6,8},{7,5},{8,10},{9,7},{10,... | collective-permute-start | bytes 1277960 | tf_op jit(solution)/shard_map/ppermute | solution.py:142
  74.5 7.3 %collective-permute-done.9.b_ref = bf16[64,3328]{1,0:T(8,128)(2,1)S(1)} collective-permute-done((bf16[64,3328]{1,0:T(8,128)(2,1)S(1)}, bf16[64,3328]{1,0:T(8,128)(2,1)S(1)}, u32[]{:S(2)}, u32[]{:S(2)}) %collective-permute-start.9) | collective-permute-done | bytes 426016 | tf_op jit(solution)/shard_map/ppermute | solution.py:142
  81.8 4.6 %collective-permute-done.2.a_ref = bf16[64,3328]{1,0:T(8,128)(2,1)S(1)} collective-permute-done((bf16[64,3328]{1,0:T(8,128)(2,1)S(1)}, bf16[64,3328]{1,0:T(8,128)(2,1)S(1)}, u32[]{:S(2)}, u32[]{:S(2)}) %collective-permute-start.2) | collective-permute-done | bytes 426016 | tf_op jit(solution)/shard_map/ppermute | solution.py:142
  88.2 2.8 %collective-permute-start.13 = (bf16[64,1792]{1,0:T(8,128)(2,1)S(1)}, bf16[64,1792]{1,0:T(8,128)(2,1)S(1)}, u32[]{:S(2)}, u32[]{:S(2)}) collective-permute-start(bf16[64,1792]{1,0:T(8,128)(2,1)S(1)} %get-tuple-element.26), channel_id=1, source_target_pairs={{0,14},{1,3},{2,0},{3,5},{4,2},{5,7},{6,4},{7,9},{8,6},{9,11},{10,... | collective-permute-start | bytes 688136 | tf_op jit(solution)/shard_map/ppermute | solution.py:142
  91.1 3.1 %collective-permute-start.3 = (bf16[64,3328]{1,0:T(8,128)(2,1)S(1)}, bf16[64,3328]{1,0:T(8,128)(2,1)S(1)}, u32[]{:S(2)}, u32[]{:S(2)}) collective-permute-start(bf16[64,3328]{1,0:T(8,128)(2,1)S(1)} %collective-permute-done.2.a_ref), channel_id=1, source_target_pairs={{0,2},{1,15},{2,4},{3,1},{4,6},{5,3},{6,8},{7,5},{8,10},{9,7},{10,... | collective-permute-start | bytes 1277960 | tf_op jit(solution)/shard_map/ppermute | solution.py:142
  94.4 8.0 %collective-permute-done.3.a_ref = bf16[64,3328]{1,0:T(8,128)(2,1)S(1)} collective-permute-done((bf16[64,3328]{1,0:T(8,128)(2,1)S(1)}, bf16[64,3328]{1,0:T(8,128)(2,1)S(1)}, u32[]{:S(2)}, u32[]{:S(2)}) %collective-permute-start.3) | collective-permute-done | bytes 426016 | tf_op jit(solution)/shard_map/ppermute | solution.py:142
  104.3 1.9 %collective-permute-start.6 = (bf16[64,1792]{1,0:T(8,128)(2,1)S(1)}, bf16[64,1792]{1,0:T(8,128)(2,1)S(1)}, u32[]{:S(2)}, u32[]{:S(2)}) collective-permute-start(bf16[64,1792]{1,0:T(8,128)(2,1)S(1)} %get-tuple-element.22), channel_id=1, source_target_pairs={{0,14},{1,3},{2,0},{3,5},{4,2},{5,7},{6,4},{7,9},{8,6},{9,11},{10,... | collective-permute-start | bytes 688136 | tf_op jit(solution)/shard_map/ppermute | solution.py:142
  106.3 2.1 %convolution_convert_fusion = bf16[256,1664]{1,0:T(8,128)(2,1)} fusion(bf16[512,1664]{1,0:T(8,128)(2,1)S(1)} %get-tuple-element.40, bf16[512,512]{1,0:T(8,128)(2,1)S(1)} %constant_dynamic-update-slice_fusion.4), kind=kOutput, calls=%fused_computation.2 | convolution fusion | flops 436633600 | bytes 2818048 | tf_op jit(solution)/shard_map/dot_general | solution.py:16
  112.4 3.1 %collective-permute-start.10 = (bf16[64,1792]{1,0:T(8,128)(2,1)S(1)}, bf16[64,1792]{1,0:T(8,128)(2,1)S(1)}, u32[]{:S(2)}, u32[]{:S(2)}) collective-permute-start(bf16[64,1792]{1,0:T(8,128)(2,1)S(1)} %shard_map.95), channel_id=1, source_target_pairs={{0,14},{1,3},{2,0},{3,5},{4,2},{5,7},{6,4},{7,9},{8,6},{9,11},{10,... | collective-permute-start | bytes 688136 | tf_op jit(solution)/shard_map/ppermute | solution.py:142
  117.1 1.9 %collective-permute-start.16 = (bf16[1664,256]{1,0:T(8,128)(2,1)}, bf16[1664,256]{1,0:T(8,128)(2,1)}, u32[]{:S(2)}, u32[]{:S(2)}) collective-permute-start(bf16[1664,256]{1,0:T(8,128)(2,1)} %convolution_convert_fusion.1), channel_id=1, source_target_pairs={{0,1},{1,0},{2,3},{3,2},{4,5},{5,4},{6,7},{7,6},{8,9},{9,8},{10,11... | collective-permute-start | bytes 2555912 | tf_op jit(solution)/shard_map/ppermute | solution.py:142
  119.3 2.9 %collective-permute-start.14 = (bf16[64,1792]{1,0:T(8,128)(2,1)S(1)}, bf16[64,1792]{1,0:T(8,128)(2,1)S(1)}, u32[]{:S(2)}, u32[]{:S(2)}) collective-permute-start(bf16[64,1792]{1,0:T(8,128)(2,1)S(1)} %shard_map.100), channel_id=1, source_target_pairs={{0,14},{1,3},{2,0},{3,5},{4,2},{5,7},{6,4},{7,9},{8,6},{9,11},{10,... | collective-permute-start | bytes 688136 | tf_op jit(solution)/shard_map/ppermute | solution.py:142
  122.5 3.9 %collective-permute-start.11 = (bf16[64,1792]{1,0:T(8,128)(2,1)S(1)}, bf16[64,1792]{1,0:T(8,128)(2,1)S(1)}, u32[]{:S(2)}, u32[]{:S(2)}) collective-permute-start(bf16[64,1792]{1,0:T(8,128)(2,1)S(1)} %shard_map.97), channel_id=1, source_target_pairs={{0,14},{1,3},{2,0},{3,5},{4,2},{5,7},{6,4},{7,9},{8,6},{9,11},{10,... | collective-permute-start | bytes 688136 | tf_op jit(solution)/shard_map/ppermute | solution.py:142
  127.4 2.3 %collective-permute-start.15 = (bf16[64,1792]{1,0:T(8,128)(2,1)S(1)}, bf16[64,1792]{1,0:T(8,128)(2,1)S(1)}, u32[]{:S(2)}, u32[]{:S(2)}) collective-permute-start(bf16[64,1792]{1,0:T(8,128)(2,1)S(1)} %shard_map.101), channel_id=1, source_target_pairs={{0,15},{1,2},{2,1},{3,4},{4,3},{5,6},{6,5},{7,8},{8,7},{9,10},{10,... | collective-permute-start | bytes 688136 | tf_op jit(solution)/shard_map/ppermute | solution.py:142
  130.8 4.9 %collective-permute-start.12 = (bf16[64,1792]{1,0:T(8,128)(2,1)S(1)}, bf16[64,1792]{1,0:T(8,128)(2,1)S(1)}, u32[]{:S(2)}, u32[]{:S(2)}) collective-permute-start(bf16[64,1792]{1,0:T(8,128)(2,1)S(1)} %shard_map.99), channel_id=1, source_target_pairs={{0,14},{1,3},{2,0},{3,5},{4,2},{5,7},{6,4},{7,9},{8,6},{9,11},{10,... | collective-permute-start | bytes 688136 | tf_op jit(solution)/shard_map/ppermute | solution.py:142
  136.0 3.3 %collective-permute-done.12.refs_0_ = bf16[64,1792]{1,0:T(8,128)(2,1)S(1)} collective-permute-done((bf16[64,1792]{1,0:T(8,128)(2,1)S(1)}, bf16[64,1792]{1,0:T(8,128)(2,1)S(1)}, u32[]{:S(2)}, u32[]{:S(2)}) %collective-permute-start.12) | collective-permute-done | bytes 229408 | tf_op jit(solution)/shard_map/ppermute | solution.py:142
  140.3 4.7 %all-to-all-start.1 = ((bf16[32,2,1792]{2,1,0:T(2,128)(2,1)}), bf16[32,2,1792]{2,1,0:T(2,128)(2,1)S(1)}, u32[]{:S(2)}, u32[]{:S(2)}) async-start(bf16[32,2,1792]{2,1,0:T(2,128)(2,1)} %reshape.22), calls=%async_computation.1 | async-start | bytes 458752 | tf_op jit(solution)/shard_map/all_to_all | solution.py:200
  146.7 2.7 %fusion.3 = bf16[1,1664,256]{2,1,0:T(8,128)(2,1)} fusion(bf16[512,1664]{1,0:T(8,128)(2,1)S(1)} %copy-done.12, bf16[1664,256]{1,0:T(8,128)(2,1)} %collective-permute-done.16, bf16[512,512]{1,0:T(8,128)(2,1)S(1)} %copy-done.10), kind=kOutput, calls=%fused_computation.7 | convolution fusion | flops 437485568 | bytes 3670016 | tf_op jit(solution)/shard_map/dot_general | solution.py:16
  149.4 7.7 %all-to-all-done.1 = bf16[32,2,1792]{2,1,0:T(2,128)(2,1)S(1)} async-done(((bf16[32,2,1792]{2,1,0:T(2,128)(2,1)}), bf16[32,2,1792]{2,1,0:T(2,128)(2,1)S(1)}, u32[]{:S(2)}, u32[]{:S(2)}) %all-to-all-start.1) | async-done | bytes 229408 | tf_op jit(solution)/shard_map/all_to_all | solution.py:200
  (69 shorter events, 22.4 us)
Async XLA Ops:
  0.6 12.6 %copy-start = (bf16[1,1664,256]{2,1,0:T(8,128)(2,1)S(1)}, bf16[1,1664,256]{2,1,0:T(8,128)(2,1)}, u32[]{:S(2)}) copy-start(bf16[1,1664,256]{2,1,0:T(8,128)(2,1)} %param.10) | copy-start | bytes 2555908
  0.6 14.5 %copy-start.1 = (bf16[1,256,1664]{2,1,0:T(8,128)(2,1)S(1)}, bf16[1,256,1664]{2,1,0:T(8,128)(2,1)}, u32[]{:S(2)}) copy-start(bf16[1,256,1664]{2,1,0:T(8,128)(2,1)} %param.11) | copy-start | bytes 2555908
  3.0 25.9 %all-to-all-start = ((bf16[32,2,3328]{2,1,0:T(2,128)(2,1)}), bf16[32,2,3328]{2,1,0:T(2,128)(2,1)}, u32[]{:S(2)}, u32[]{:S(2)}) async-start(bf16[32,2,3328]{2,1,0:T(2,128)(2,1)} %reshape.20), calls=%async_computation | async-start | bytes 851968 | tf_op jit(solution)/shard_map/all_to_all | solution.py:161
  13.2 27.9 %collective-permute-start.4 = (bf16[1664,256]{1,0:T(8,128)(2,1)S(1)}, bf16[1664,256]{1,0:T(8,128)(2,1)S(1)}, u32[]{:S(2)}, u32[]{:S(2)}) collective-permute-start(bf16[1664,256]{1,0:T(8,128)(2,1)S(1)} %bitcast.13), channel_id=1, source_target_pairs={{0,1},{1,0},{2,3},{3,2},{4,5},{5,4},{6,7},{7,6},{8,9},{9,8},{10,11... | collective-permute-start | bytes 2555912 | tf_op jit(solution)/shard_map/ppermute | solution.py:142
  15.1 26.0 %collective-permute-start.5 = (bf16[256,1664]{1,0:T(8,128)(2,1)S(1)}, bf16[256,1664]{1,0:T(8,128)(2,1)S(1)}, u32[]{:S(2)}, u32[]{:S(2)}) collective-permute-start(bf16[256,1664]{1,0:T(8,128)(2,1)S(1)} %bitcast.18), channel_id=1, source_target_pairs={{0,1},{1,0},{2,3},{3,2},{4,5},{5,4},{6,7},{7,6},{8,9},{9,8},{10,11... | collective-permute-start | bytes 2555912 | tf_op jit(solution)/shard_map/ppermute | solution.py:142
  30.8 17.5 %collective-permute-start.7 = (bf16[64,3328]{1,0:T(8,128)(2,1)}, bf16[64,3328]{1,0:T(8,128)(2,1)S(1)}, u32[]{:S(2)}, u32[]{:S(2)}) collective-permute-start(bf16[64,3328]{1,0:T(8,128)(2,1)} %reshape.21.b_ref), channel_id=1, source_target_pairs={{0,15},{1,2},{2,1},{3,4},{4,3},{5,6},{6,5},{7,8},{8,7},{9,10},{10,... | collective-permute-start | bytes 1277960 | tf_op jit(solution)/shard_map/ppermute | solution.py:142
  39.2 11.4 %collective-permute-start = (bf16[64,3328]{1,0:T(8,128)(2,1)}, bf16[64,3328]{1,0:T(8,128)(2,1)S(1)}, u32[]{:S(2)}, u32[]{:S(2)}) collective-permute-start(bf16[64,3328]{1,0:T(8,128)(2,1)} %reshape.21.b_ref), channel_id=1, source_target_pairs={{0,2},{1,15},{2,4},{3,1},{4,6},{5,3},{6,8},{7,5},{8,10},{9,7},{10,... | collective-permute-start | bytes 1277960 | tf_op jit(solution)/shard_map/ppermute | solution.py:142
  52.6 11.4 %collective-permute-start.8 = (bf16[64,3328]{1,0:T(8,128)(2,1)S(1)}, bf16[64,3328]{1,0:T(8,128)(2,1)S(1)}, u32[]{:S(2)}, u32[]{:S(2)}) collective-permute-start(bf16[64,3328]{1,0:T(8,128)(2,1)S(1)} %collective-permute-done.7.b_ref), channel_id=1, source_target_pairs={{0,2},{1,15},{2,4},{3,1},{4,6},{5,3},{6,8},{7,5},{8,10},{9,7},{10,... | collective-permute-start | bytes 1277960 | tf_op jit(solution)/shard_map/ppermute | solution.py:142
  54.5 14.1 %collective-permute-start.1 = (bf16[64,3328]{1,0:T(8,128)(2,1)S(1)}, bf16[64,3328]{1,0:T(8,128)(2,1)S(1)}, u32[]{:S(2)}, u32[]{:S(2)}) collective-permute-start(bf16[64,3328]{1,0:T(8,128)(2,1)S(1)} %collective-permute-done.a_ref), channel_id=1, source_target_pairs={{0,2},{1,15},{2,4},{3,1},{4,6},{5,3},{6,8},{7,5},{8,10},{9,7},{10,... | collective-permute-start | bytes 1277960 | tf_op jit(solution)/shard_map/ppermute | solution.py:142
  70.5 11.2 %collective-permute-start.9 = (bf16[64,3328]{1,0:T(8,128)(2,1)S(1)}, bf16[64,3328]{1,0:T(8,128)(2,1)S(1)}, u32[]{:S(2)}, u32[]{:S(2)}) collective-permute-start(bf16[64,3328]{1,0:T(8,128)(2,1)S(1)} %collective-permute-done.8.b_ref), channel_id=1, source_target_pairs={{0,2},{1,15},{2,4},{3,1},{4,6},{5,3},{6,8},{7,5},{8,10},{9,7},{10,... | collective-permute-start | bytes 1277960 | tf_op jit(solution)/shard_map/ppermute | solution.py:142
  72.5 13.9 %collective-permute-start.2 = (bf16[64,3328]{1,0:T(8,128)(2,1)S(1)}, bf16[64,3328]{1,0:T(8,128)(2,1)S(1)}, u32[]{:S(2)}, u32[]{:S(2)}) collective-permute-start(bf16[64,3328]{1,0:T(8,128)(2,1)S(1)} %collective-permute-done.1.a_ref), channel_id=1, source_target_pairs={{0,2},{1,15},{2,4},{3,1},{4,6},{5,3},{6,8},{7,5},{8,10},{9,7},{10,... | collective-permute-start | bytes 1277960 | tf_op jit(solution)/shard_map/ppermute | solution.py:142
  88.2 14.1 %copy-start.2 = (bf16[64,3328]{1,0:T(8,128)(2,1)S(1)}, bf16[64,3328]{1,0:T(8,128)(2,1)}, u32[]{:S(2)}) copy-start(bf16[64,3328]{1,0:T(8,128)(2,1)} %reshape.21.b_ref) | copy-start | bytes 1277956
  88.2 30.8 %collective-permute-start.13 = (bf16[64,1792]{1,0:T(8,128)(2,1)S(1)}, bf16[64,1792]{1,0:T(8,128)(2,1)S(1)}, u32[]{:S(2)}, u32[]{:S(2)}) collective-permute-start(bf16[64,1792]{1,0:T(8,128)(2,1)S(1)} %get-tuple-element.26), channel_id=1, source_target_pairs={{0,14},{1,3},{2,0},{3,5},{4,2},{5,7},{6,4},{7,9},{8,6},{9,11},{10,... | collective-permute-start | bytes 688136 | tf_op jit(solution)/shard_map/ppermute | solution.py:142
  91.1 11.2 %collective-permute-start.3 = (bf16[64,3328]{1,0:T(8,128)(2,1)S(1)}, bf16[64,3328]{1,0:T(8,128)(2,1)S(1)}, u32[]{:S(2)}, u32[]{:S(2)}) collective-permute-start(bf16[64,3328]{1,0:T(8,128)(2,1)S(1)} %collective-permute-done.2.a_ref), channel_id=1, source_target_pairs={{0,2},{1,15},{2,4},{3,1},{4,6},{5,3},{6,8},{7,5},{8,10},{9,7},{10,... | collective-permute-start | bytes 1277960 | tf_op jit(solution)/shard_map/ppermute | solution.py:142
  104.3 7.9 %collective-permute-start.6 = (bf16[64,1792]{1,0:T(8,128)(2,1)S(1)}, bf16[64,1792]{1,0:T(8,128)(2,1)S(1)}, u32[]{:S(2)}, u32[]{:S(2)}) collective-permute-start(bf16[64,1792]{1,0:T(8,128)(2,1)S(1)} %get-tuple-element.22), channel_id=1, source_target_pairs={{0,14},{1,3},{2,0},{3,5},{4,2},{5,7},{6,4},{7,9},{8,6},{9,11},{10,... | collective-permute-start | bytes 688136 | tf_op jit(solution)/shard_map/ppermute | solution.py:142
  106.2 2.2 %copy-start.7 = (bf16[512,512]{1,0:T(8,128)(2,1)}, bf16[512,512]{1,0:T(8,128)(2,1)S(1)}, u32[]{:S(2)}) copy-start(bf16[512,512]{1,0:T(8,128)(2,1)S(1)} %constant_dynamic-update-slice_fusion.4) | copy-start | bytes 1572868
  106.3 6.1 %copy-start.5 = (bf16[512,1664]{1,0:T(8,128)(2,1)}, bf16[512,1664]{1,0:T(8,128)(2,1)S(1)}, u32[]{:S(2)}) copy-start(bf16[512,1664]{1,0:T(8,128)(2,1)S(1)} %get-tuple-element.40) | copy-start | bytes 5111812
  106.3 9.2 %copy-start.11 = (bf16[512,1664]{1,0:T(8,128)(2,1)}, bf16[512,1664]{1,0:T(8,128)(2,1)S(1)}, u32[]{:S(2)}) copy-start(bf16[512,1664]{1,0:T(8,128)(2,1)S(1)} %get-tuple-element.41) | copy-start | bytes 5111812
  108.4 36.6 %collective-permute-start.17 = (bf16[256,1664]{1,0:T(8,128)(2,1)}, bf16[256,1664]{1,0:T(8,128)(2,1)S(1)}, u32[]{:S(2)}, u32[]{:S(2)}) collective-permute-start(bf16[256,1664]{1,0:T(8,128)(2,1)} %convolution_convert_fusion), channel_id=1, source_target_pairs={{0,1},{1,0},{2,3},{3,2},{4,5},{5,4},{6,7},{7,6},{8,9},{9,8},{10,11... | collective-permute-start | bytes 2555912 | tf_op jit(solution)/shard_map/ppermute | solution.py:142
  110.3 6.8 %copy-start.9 = (bf16[512,512]{1,0:T(8,128)(2,1)}, bf16[512,512]{1,0:T(8,128)(2,1)S(1)}, u32[]{:S(2)}) copy-start(bf16[512,512]{1,0:T(8,128)(2,1)S(1)} %constant_dynamic-update-slice_fusion) | copy-start | bytes 1572868
  112.4 9.8 %collective-permute-start.10 = (bf16[64,1792]{1,0:T(8,128)(2,1)S(1)}, bf16[64,1792]{1,0:T(8,128)(2,1)S(1)}, u32[]{:S(2)}, u32[]{:S(2)}) collective-permute-start(bf16[64,1792]{1,0:T(8,128)(2,1)S(1)} %shard_map.95), channel_id=1, source_target_pairs={{0,14},{1,3},{2,0},{3,5},{4,2},{5,7},{6,4},{7,9},{8,6},{9,11},{10,... | collective-permute-start | bytes 688136 | tf_op jit(solution)/shard_map/ppermute | solution.py:142
  117.1 29.5 %collective-permute-start.16 = (bf16[1664,256]{1,0:T(8,128)(2,1)}, bf16[1664,256]{1,0:T(8,128)(2,1)}, u32[]{:S(2)}, u32[]{:S(2)}) collective-permute-start(bf16[1664,256]{1,0:T(8,128)(2,1)} %convolution_convert_fusion.1), channel_id=1, source_target_pairs={{0,1},{1,0},{2,3},{3,2},{4,5},{5,4},{6,7},{7,6},{8,9},{9,8},{10,11... | collective-permute-start | bytes 2555912 | tf_op jit(solution)/shard_map/ppermute | solution.py:142
  119.3 7.9 %collective-permute-start.14 = (bf16[64,1792]{1,0:T(8,128)(2,1)S(1)}, bf16[64,1792]{1,0:T(8,128)(2,1)S(1)}, u32[]{:S(2)}, u32[]{:S(2)}) collective-permute-start(bf16[64,1792]{1,0:T(8,128)(2,1)S(1)} %shard_map.100), channel_id=1, source_target_pairs={{0,14},{1,3},{2,0},{3,5},{4,2},{5,7},{6,4},{7,9},{8,6},{9,11},{10,... | collective-permute-start | bytes 688136 | tf_op jit(solution)/shard_map/ppermute | solution.py:142
  122.5 22.6 %copy-start.6 = (bf16[512,1664]{1,0:T(8,128)(2,1)S(1)}, bf16[512,1664]{1,0:T(8,128)(2,1)}, u32[]{:S(2)}) copy-start(bf16[512,1664]{1,0:T(8,128)(2,1)} %copy-done.5) | copy-start | bytes 5111812
  122.5 22.6 %copy-start.8 = (bf16[512,512]{1,0:T(8,128)(2,1)S(1)}, bf16[512,512]{1,0:T(8,128)(2,1)}, u32[]{:S(2)}) copy-start(bf16[512,512]{1,0:T(8,128)(2,1)} %copy-done.7) | copy-start | bytes 1572868
  122.5 8.0 %collective-permute-start.11 = (bf16[64,1792]{1,0:T(8,128)(2,1)S(1)}, bf16[64,1792]{1,0:T(8,128)(2,1)S(1)}, u32[]{:S(2)}, u32[]{:S(2)}) collective-permute-start(bf16[64,1792]{1,0:T(8,128)(2,1)S(1)} %shard_map.97), channel_id=1, source_target_pairs={{0,14},{1,3},{2,0},{3,5},{4,2},{5,7},{6,4},{7,9},{8,6},{9,11},{10,... | collective-permute-start | bytes 688136 | tf_op jit(solution)/shard_map/ppermute | solution.py:142
  127.4 8.6 %collective-permute-start.15 = (bf16[64,1792]{1,0:T(8,128)(2,1)S(1)}, bf16[64,1792]{1,0:T(8,128)(2,1)S(1)}, u32[]{:S(2)}, u32[]{:S(2)}) collective-permute-start(bf16[64,1792]{1,0:T(8,128)(2,1)S(1)} %shard_map.101), channel_id=1, source_target_pairs={{0,15},{1,2},{2,1},{3,4},{4,3},{5,6},{6,5},{7,8},{8,7},{9,10},{10,... | collective-permute-start | bytes 688136 | tf_op jit(solution)/shard_map/ppermute | solution.py:142
  130.8 8.5 %collective-permute-start.12 = (bf16[64,1792]{1,0:T(8,128)(2,1)S(1)}, bf16[64,1792]{1,0:T(8,128)(2,1)S(1)}, u32[]{:S(2)}, u32[]{:S(2)}) collective-permute-start(bf16[64,1792]{1,0:T(8,128)(2,1)S(1)} %shard_map.99), channel_id=1, source_target_pairs={{0,14},{1,3},{2,0},{3,5},{4,2},{5,7},{6,4},{7,9},{8,6},{9,11},{10,... | collective-permute-start | bytes 688136 | tf_op jit(solution)/shard_map/ppermute | solution.py:142
  140.3 16.8 %all-to-all-start.1 = ((bf16[32,2,1792]{2,1,0:T(2,128)(2,1)}), bf16[32,2,1792]{2,1,0:T(2,128)(2,1)S(1)}, u32[]{:S(2)}, u32[]{:S(2)}) async-start(bf16[32,2,1792]{2,1,0:T(2,128)(2,1)} %reshape.22), calls=%async_computation.1 | async-start | bytes 458752 | tf_op jit(solution)/shard_map/all_to_all | solution.py:200
  145.0 1.6 %copy-start.10 = (bf16[512,512]{1,0:T(8,128)(2,1)S(1)}, bf16[512,512]{1,0:T(8,128)(2,1)}, u32[]{:S(2)}) copy-start(bf16[512,512]{1,0:T(8,128)(2,1)} %copy-done.9) | copy-start | bytes 1572868
  146.7 10.5 %copy-start.3 = (s32[16,2]{0,1:T(2,128)S(1)}, s32[16,2]{0,1:T(2,128)}, u32[]{:S(2)}) copy-start(s32[16,2]{0,1:T(2,128)} %param.8) | copy-start | bytes 388
  146.7 10.5 %copy-start.4 = (bf16[16,2]{0,1:T(2,128)(2,1)S(1)}, bf16[16,2]{0,1:T(2,128)(2,1)}, u32[]{:S(2)}) copy-start(bf16[16,2]{0,1:T(2,128)(2,1)} %param.9) | copy-start | bytes 196
  (1 other events, 1.6 us)

commit v3 on v2

--- a/solution.py
+++ b/solution.py
@@ -69,14 +69,15 @@
     return jnp.where(lane == 0, hi, jnp.where(lane == 1, lo, 0.0)).astype(BF16)
 
 
-def work_body(a_ref, b_ref, w1_ref, w1p_ref, w2_ref, w2p_ref, hid_ref, pg_ref, pa_ref, pb_ref):
-    feat = w1_ref.shape[0]
-    half = w1_ref.shape[1]
-    n = a_ref.shape[0]
-    x = jnp.concatenate([a_ref[:, :feat], b_ref[:, :feat]], axis=0)
-    scaled = jnp.concatenate([a_ref[:, feat:], b_ref[:, feat:]], axis=0)
-    gate_part = jnp.zeros((2 * n, 1), F32)
-    part = jnp.zeros((2 * n, feat), F32)
+def work_body(count, *refs):
+    blocks, (w1_ref, w1p_ref, w2_ref, w2p_ref) = refs[:count], refs[count : count + 4]
+    hid_ref, pg_ref, *part_refs = refs[count + 4 :]
+    feat, half = w1_ref.shape
+    n = blocks[0].shape[0]
+    x = jnp.concatenate([r[:, :feat] for r in blocks], axis=0)
+    scaled = jnp.concatenate([r[:, feat:] for r in blocks], axis=0)
+    gate_part = jnp.zeros((count * n, 1), F32)
+    part = jnp.zeros((count * n, feat), F32)
     for at, v1, v2 in ((0, w1_ref, w2_ref), (half, w1p_ref, w2p_ref)):
         pre = mm(x, v1[...], ((1,), (0,)))
         back = mm(scaled, v2[...], ((1,), (1,)))
@@ -89,10 +90,9 @@
         gate_part += jnp.sum(hidden.astype(F32) * back, axis=1, keepdims=True)
         part += mm(pre_grad, v1[...], ((1,), (1,)))
     gates = tail(gate_part)
-    pa_ref[:, :feat] = part[:n].astype(BF16)
-    pb_ref[:, :feat] = part[n:].astype(BF16)
-    pa_ref[:, feat:] = gates[:n]
-    pb_ref[:, feat:] = gates[n:]
+    for k, part_ref in enumerate(part_refs):
+        part_ref[:, :feat] = part[k * n : (k + 1) * n].astype(BF16)
+        part_ref[:, feat:] = gates[k * n : (k + 1) * n]
 
 
 def plus_body(feat, *refs):
@@ -127,16 +127,16 @@
 
     swap = [(i, i ^ 1) for i in range(ndp)]
 
-    def shifted(step, cross=0):
+    def shifted(step, cross):
         pairs = []
         for z in range(nz):
             for core in range(2):
-                up = step if core == 0 else -step
+                up = step if (z + core) % 2 == 0 else -step
                 pairs.append((2 * z + core, 2 * ((z + up) % nz) + (core ^ cross)))
         return pairs
 
-    away, home = shifted(1), shifted(-1)
-    over = shifted(-1, 1)
+    away, home = shifted(1, 1), shifted(-1, 1)
+    over = shifted(-1, 0)
 
     def move(a, pairs):
         return lax.ppermute(a, "dp", pairs)
@@ -170,40 +170,41 @@
         if k < hops:
             b = move(b, over if k == 1 else away)
             chain_b.append(b)
-    firsts = chain_a
-    seconds = chain_b + [own]
+    groups = [[chain_a[k], chain_b[k]] for k in range(hops - 1)] + [[chain_a[hops - 1], own]]
 
     hid, pg, part_a, part_b = [], [], [], []
     ff = 2 * half
-    for k in range(hops):
-        h, p, ra, rb = kernel_call(
-            work_body,
-            [((2 * rows, ff), BF16), ((2 * rows, ff), BF16), ((rows, slim), BF16), ((rows, slim), BF16)],
-            firsts[k], seconds[k], w1, w1p, w2, w2p,
-            limit=16, flops=2 * 3 * 2 * rows * feat * ff,
+    for group in groups:
+        count = len(group)
+        h, p, *parts = kernel_call(
+            functools.partial(work_body, count),
+            [((count * rows, ff), BF16)] * 2 + [((rows, slim), BF16)] * count,
+            *group, w1, w1p, w2, w2p,
+            limit=16, flops=2 * 3 * count * rows * feat * ff,
         )
         hid.append(h)
         pg.append(p)
-        part_a.append(ra)
-        part_b.append(rb)
+        part_a.append(parts[0])
+        part_b.append(parts[1])
 
     def plus(*args):
         return kernel_call(functools.partial(plus_body, feat), [((rows, slim), BF16)], *args)[0]
 
+    sa = move(part_a[hops - 2], home)
     sb = move(part_b[hops - 2], home)
+    join = 0
+    jump = hops - 1 - join
+    far = move(part_a[hops - 1], shifted(-jump, jump % 2))
     for k in range(hops - 3, -1, -1):
         sb = move(plus(sb, part_b[k]), over if k == 0 else home)
-    sa = move(part_a[hops - 1], home)
-    for k in range(hops - 2, -1, -1):
-        sa = move(plus(sa, part_a[k]), home)
+        extra = (far,) if k == join else ()
+        sa = move(plus(sa, part_a[k], *extra), home)
     total = plus(sa, sb, part_b[hops - 1])
     back_rows = lax.all_to_all(
         total.reshape(experts, cap, slim), "expert", split_axis=0, concat_axis=0, tiled=True
     ).reshape(rows, slim)
 
-    blocks = []
-    for k in range(hops):
-        blocks += [firsts[k], seconds[k]]
+    blocks = [c for group in groups for c in group]
     x_all = jnp.concatenate([c[:, :feat] for c in blocks], axis=0)
     scaled_all = jnp.concatenate([c[:, feat:] for c in blocks], axis=0)
     hidden_all = jnp.concatenate(hid, axis=0)

time: 159 us -> 162 us (1.019)
  the two profiles are of different devices: /device:TPU:8 before, /device:TPU:73 now
where the time goes in v3:
time: 162 us; the launch traced here: 161 us
  starting transfers between devices  70.4 us (43%)
  waiting for transfers between devices  66.6 us (41%)
  Pallas kernels  11.2 us (7%)
  matrix products  7.92 us (5%)
  local copies, waits for them, and re-layouts  4.17 us (3%)
    ppermute x18, starting transfers between devices, move(): return lax.ppermute(a, 'dp', pairs)  56.6 us
    ppermute x18, waiting for transfers between devices, move(): return lax.ppermute(a, 'dp', pairs)  50 us
    pallas_call x10, Pallas kernels, kernel_call(): pl.pallas_call(body, out_shape=outs, in_specs=[spec] * len(args), out_spe...  9.81 us
    all_to_all x1, starting transfers between devices, per_device(): lax.all_to_all(send.reshape(experts, cap, wide), 'expert', split_axis=0,...  9.65 us
    all_to_all x1, waiting for transfers between devices, per_device(): lax.all_to_all(send.reshape(experts, cap, wide), 'expert', split_axis=0,...  9.15 us
    dot_general x4, matrix products, mm(): return lax.dot_general(a, b, (dims, ((), ())), preferred_element_type=F32)  7.92 us
    all_to_all x1, waiting for transfers between devices, per_device(): lax.all_to_all(total.reshape(experts, cap, slim), 'expert', split_axis=0,...  7.45 us
    all_to_all x1, starting transfers between devices, per_device(): lax.all_to_all(total.reshape(experts, cap, slim), 'expert', split_axis=0,...  4.14 us
  transfers between devices with their start and end apart: 20, of which 11 were waited for; matrix products, arithmetic and copies ran while one was open for 7% of the time, Pallas kernels for 2%

profile of v3, /device:TPU:73, one launch (start us, length us, event | category | flops | bytes accessed | tf_op | source)
XLA Modules:
  0.0 161.5 jit_solution(13783099232412517559)
XLA Ops:
  3.0 9.7 %all-to-all-start = ((bf16[32,2,3328]{2,1,0:T(2,128)(2,1)}), bf16[32,2,3328]{2,1,0:T(2,128)(2,1)}, u32[]{:S(2)}, u32[]{:S(2)}) async-start(bf16[32,2,3328]{2,1,0:T(2,128)(2,1)} %reshape.20), calls=%async_computation | async-start | bytes 851968 | tf_op jit(solution)/shard_map/all_to_all | solution.py:161
  12.6 3.1 %collective-permute-start.6 = (bf16[1664,256]{1,0:T(8,128)(2,1)S(1)}, bf16[1664,256]{1,0:T(8,128)(2,1)S(1)}, u32[]{:S(2)}, u32[]{:S(2)}) collective-permute-start(bf16[1664,256]{1,0:T(8,128)(2,1)S(1)} %bitcast.13), channel_id=1, source_target_pairs={{0,1},{1,0},{2,3},{3,2},{4,5},{5,4},{6,7},{7,6},{8,9},{9,8},{10,11... | collective-permute-start | bytes 2555912 | tf_op jit(solution)/shard_map/ppermute | solution.py:142
  15.8 1.9 %collective-permute-start.7 = (bf16[256,1664]{1,0:T(8,128)(2,1)S(1)}, bf16[256,1664]{1,0:T(8,128)(2,1)S(1)}, u32[]{:S(2)}, u32[]{:S(2)}) collective-permute-start(bf16[256,1664]{1,0:T(8,128)(2,1)S(1)} %bitcast.18), channel_id=1, source_target_pairs={{0,1},{1,0},{2,3},{3,2},{4,5},{5,4},{6,7},{7,6},{8,9},{9,8},{10,11... | collective-permute-start | bytes 2555912 | tf_op jit(solution)/shard_map/ppermute | solution.py:142
  17.7 9.2 %all-to-all-done = bf16[32,2,3328]{2,1,0:T(2,128)(2,1)} async-done(((bf16[32,2,3328]{2,1,0:T(2,128)(2,1)}), bf16[32,2,3328]{2,1,0:T(2,128)(2,1)}, u32[]{:S(2)}, u32[]{:S(2)}) %all-to-all-start) | async-done | bytes 426016 | tf_op jit(solution)/shard_map/all_to_all | solution.py:161
  26.9 1.9 %reshape.21.refs_1_ = bf16[64,3328]{1,0:T(8,128)(2,1)} reshape(bf16[32,2,3328]{2,1,0:T(2,128)(2,1)} %all-to-all-done) | data formatting | bytes 851968 | tf_op jit(solution)/shard_map/reshape | solution.py:163
  30.7 6.6 %collective-permute-start = (bf16[64,3328]{1,0:T(8,128)(2,1)}, bf16[64,3328]{1,0:T(8,128)(2,1)S(1)}, u32[]{:S(2)}, u32[]{:S(2)}) collective-permute-start(bf16[64,3328]{1,0:T(8,128)(2,1)} %reshape.21.refs_1_), channel_id=1, source_target_pairs={{0,3},{1,14},{2,1},{3,4},{4,7},{5,2},{6,5},{7,8},{8,11},{9,6},{10,... | collective-permute-start | bytes 1277960 | tf_op jit(solution)/shard_map/ppermute | solution.py:142
  38.2 11.4 %collective-permute-done.refs_0_ = bf16[64,3328]{1,0:T(8,128)(2,1)S(1)} collective-permute-done((bf16[64,3328]{1,0:T(8,128)(2,1)}, bf16[64,3328]{1,0:T(8,128)(2,1)S(1)}, u32[]{:S(2)}, u32[]{:S(2)}) %collective-permute-start) | collective-permute-done | bytes 426016 | tf_op jit(solution)/shard_map/ppermute | solution.py:142
  51.6 1.9 %collective-permute-start.4 = (bf16[64,3328]{1,0:T(8,128)(2,1)S(1)}, bf16[64,3328]{1,0:T(8,128)(2,1)S(1)}, u32[]{:S(2)}, u32[]{:S(2)}) collective-permute-start(bf16[64,3328]{1,0:T(8,128)(2,1)S(1)} %collective-permute-done.3.refs_1_), channel_id=1, source_target_pairs={{0,3},{1,14},{2,1},{3,4},{4,7},{5,2},{6,5},{7,8},{8,11},{9,6},{10,... | collective-permute-start | bytes 1277960 | tf_op jit(solution)/shard_map/ppermute | solution.py:142
  53.5 3.8 %collective-permute-start.1 = (bf16[64,3328]{1,0:T(8,128)(2,1)S(1)}, bf16[64,3328]{1,0:T(8,128)(2,1)S(1)}, u32[]{:S(2)}, u32[]{:S(2)}) collective-permute-start(bf16[64,3328]{1,0:T(8,128)(2,1)S(1)} %collective-permute-done.refs_0_), channel_id=1, source_target_pairs={{0,3},{1,14},{2,1},{3,4},{4,7},{5,2},{6,5},{7,8},{8,11},{9,6},{10,... | collective-permute-start | bytes 1277960 | tf_op jit(solution)/shard_map/ppermute | solution.py:142
  57.4 5.1 %collective-permute-done.4.refs_1_ = bf16[64,3328]{1,0:T(8,128)(2,1)S(1)} collective-permute-done((bf16[64,3328]{1,0:T(8,128)(2,1)S(1)}, bf16[64,3328]{1,0:T(8,128)(2,1)S(1)}, u32[]{:S(2)}, u32[]{:S(2)}) %collective-permute-start.4) | collective-permute-done | bytes 426016 | tf_op jit(solution)/shard_map/ppermute | solution.py:142
  62.5 4.3 %collective-permute-done.1.refs_0_ = bf16[64,3328]{1,0:T(8,128)(2,1)S(1)} collective-permute-done((bf16[64,3328]{1,0:T(8,128)(2,1)S(1)}, bf16[64,3328]{1,0:T(8,128)(2,1)S(1)}, u32[]{:S(2)}, u32[]{:S(2)}) %collective-permute-start.1) | collective-permute-done | bytes 426016 | tf_op jit(solution)/shard_map/ppermute | solution.py:142
  68.7 1.9 %collective-permute-start.5 = (bf16[64,3328]{1,0:T(8,128)(2,1)S(1)}, bf16[64,3328]{1,0:T(8,128)(2,1)S(1)}, u32[]{:S(2)}, u32[]{:S(2)}) collective-permute-start(bf16[64,3328]{1,0:T(8,128)(2,1)S(1)} %collective-permute-done.4.refs_1_), channel_id=1, source_target_pairs={{0,3},{1,14},{2,1},{3,4},{4,7},{5,2},{6,5},{7,8},{8,11},{9,6},{10,... | collective-permute-start | bytes 1277960 | tf_op jit(solution)/shard_map/ppermute | solution.py:142
  70.7 3.8 %collective-permute-start.2 = (bf16[64,3328]{1,0:T(8,128)(2,1)S(1)}, bf16[64,3328]{1,0:T(8,128)(2,1)S(1)}, u32[]{:S(2)}, u32[]{:S(2)}) collective-permute-start(bf16[64,3328]{1,0:T(8,128)(2,1)S(1)} %collective-permute-done.1.refs_0_), channel_id=1, source_target_pairs={{0,3},{1,14},{2,1},{3,4},{4,7},{5,2},{6,5},{7,8},{8,11},{9,6},{10,... | collective-permute-start | bytes 1277960 | tf_op jit(solution)/shard_map/ppermute | solution.py:142
  74.6 5.1 %collective-permute-done.5.refs_1_ = bf16[64,3328]{1,0:T(8,128)(2,1)S(1)} collective-permute-done((bf16[64,3328]{1,0:T(8,128)(2,1)S(1)}, bf16[64,3328]{1,0:T(8,128)(2,1)S(1)}, u32[]{:S(2)}, u32[]{:S(2)}) %collective-permute-start.5) | collective-permute-done | bytes 426016 | tf_op jit(solution)/shard_map/ppermute | solution.py:142
  79.7 4.3 %collective-permute-done.2.refs_0_ = bf16[64,3328]{1,0:T(8,128)(2,1)S(1)} collective-permute-done((bf16[64,3328]{1,0:T(8,128)(2,1)S(1)}, bf16[64,3328]{1,0:T(8,128)(2,1)S(1)}, u32[]{:S(2)}, u32[]{:S(2)}) %collective-permute-start.2) | collective-permute-done | bytes 426016 | tf_op jit(solution)/shard_map/ppermute | solution.py:142
  85.9 5.0 %collective-permute-start.8 = (bf16[64,1792]{1,0:T(8,128)(2,1)S(1)}, bf16[64,1792]{1,0:T(8,128)(2,1)S(1)}, u32[]{:S(2)}, u32[]{:S(2)}) collective-permute-start(bf16[64,1792]{1,0:T(8,128)(2,1)S(1)} %get-tuple-element.22), channel_id=1, source_target_pairs={{0,15},{1,2},{2,5},{3,0},{4,3},{5,6},{6,9},{7,4},{8,7},{9,10},{10,... | collective-permute-start | bytes 688136 | tf_op jit(solution)/shard_map/ppermute | solution.py:142
  90.9 1.9 %collective-permute-start.13 = (bf16[64,1792]{1,0:T(8,128)(2,1)S(1)}, bf16[64,1792]{1,0:T(8,128)(2,1)S(1)}, u32[]{:S(2)}, u32[]{:S(2)}) collective-permute-start(bf16[64,1792]{1,0:T(8,128)(2,1)S(1)} %get-tuple-element.26), channel_id=1, source_target_pairs={{0,15},{1,2},{2,5},{3,0},{4,3},{5,6},{6,9},{7,4},{8,7},{9,10},{10,... | collective-permute-start | bytes 688136 | tf_op jit(solution)/shard_map/ppermute | solution.py:142
  92.8 3.6 %collective-permute-start.10 = (bf16[64,3328]{1,0:T(8,128)(2,1)S(1)}, bf16[64,3328]{1,0:T(8,128)(2,1)S(1)}, u32[]{:S(2)}, u32[]{:S(2)}) collective-permute-start(bf16[64,3328]{1,0:T(8,128)(2,1)S(1)} %collective-permute-done.2.refs_0_), channel_id=1, source_target_pairs={{0,3},{1,14},{2,1},{3,4},{4,7},{5,2},{6,5},{7,8},{8,11},{9,6},{10,... | collective-permute-start | bytes 1277960 | tf_op jit(solution)/shard_map/ppermute | solution.py:142
  96.6 6.0 %collective-permute-done.10.refs_0_ = bf16[64,3328]{1,0:T(8,128)(2,1)S(1)} collective-permute-done((bf16[64,3328]{1,0:T(8,128)(2,1)S(1)}, bf16[64,3328]{1,0:T(8,128)(2,1)S(1)}, u32[]{:S(2)}, u32[]{:S(2)}) %collective-permute-start.10) | collective-permute-done | bytes 426016 | tf_op jit(solution)/shard_map/ppermute | solution.py:142
  104.6 2.1 %convolution_convert_fusion = bf16[256,1664]{1,0:T(8,128)(2,1)} fusion(bf16[512,1664]{1,0:T(8,128)(2,1)S(1)} %get-tuple-element.40, bf16[512,512]{1,0:T(8,128)(2,1)S(1)} %constant_dynamic-update-slice_fusion.4), kind=kOutput, calls=%fused_computation.2 | convolution fusion | flops 436633600 | bytes 2818048 | tf_op jit(solution)/shard_map/dot_general | solution.py:16
  106.7 2.8 %collective-permute-start.17 = (bf16[256,1664]{1,0:T(8,128)(2,1)}, bf16[256,1664]{1,0:T(8,128)(2,1)S(1)}, u32[]{:S(2)}, u32[]{:S(2)}) collective-permute-start(bf16[256,1664]{1,0:T(8,128)(2,1)} %convolution_convert_fusion), channel_id=1, source_target_pairs={{0,1},{1,0},{2,3},{3,2},{4,5},{5,4},{6,7},{7,6},{8,9},{9,8},{10,11... | collective-permute-start | bytes 2555912 | tf_op jit(solution)/shard_map/ppermute | solution.py:142
  111.1 1.9 %collective-permute-start.16 = (bf16[1664,256]{1,0:T(8,128)(2,1)}, bf16[1664,256]{1,0:T(8,128)(2,1)}, u32[]{:S(2)}, u32[]{:S(2)}) collective-permute-start(bf16[1664,256]{1,0:T(8,128)(2,1)} %convolution_convert_fusion.1), channel_id=1, source_target_pairs={{0,1},{1,0},{2,3},{3,2},{4,5},{5,4},{6,7},{7,6},{8,9},{9,8},{10,11... | collective-permute-start | bytes 2555912 | tf_op jit(solution)/shard_map/ppermute | solution.py:142
  113.3 4.0 %collective-permute-start.14 = (bf16[64,1792]{1,0:T(8,128)(2,1)S(1)}, bf16[64,1792]{1,0:T(8,128)(2,1)S(1)}, u32[]{:S(2)}, u32[]{:S(2)}) collective-permute-start(bf16[64,1792]{1,0:T(8,128)(2,1)S(1)} %shard_map.99), channel_id=1, source_target_pairs={{0,15},{1,2},{2,5},{3,0},{4,3},{5,6},{6,9},{7,4},{8,7},{9,10},{10,... | collective-permute-start | bytes 688136 | tf_op jit(solution)/shard_map/ppermute | solution.py:142
  117.5 3.1 %collective-permute-start.9 = (bf16[64,1792]{1,0:T(8,128)(2,1)S(1)}, bf16[64,1792]{1,0:T(8,128)(2,1)S(1)}, u32[]{:S(2)}, u32[]{:S(2)}) collective-permute-start(bf16[64,1792]{1,0:T(8,128)(2,1)S(1)} %shard_map.95), channel_id=1, source_target_pairs={{0,15},{1,2},{2,5},{3,0},{4,3},{5,6},{6,9},{7,4},{8,7},{9,10},{10,... | collective-permute-start | bytes 688136 | tf_op jit(solution)/shard_map/ppermute | solution.py:142
  120.7 3.3 %collective-permute-start.11 = (bf16[64,1792]{1,0:T(8,128)(2,1)S(1)}, bf16[64,1792]{1,0:T(8,128)(2,1)S(1)}, u32[]{:S(2)}, u32[]{:S(2)}) collective-permute-start(bf16[64,1792]{1,0:T(8,128)(2,1)S(1)} %get-tuple-element.25), channel_id=1, source_target_pairs={{0,11},{1,6},{2,9},{3,12},{4,15},{5,10},{6,13},{7,0},{8,3},{9,14},... | collective-permute-start | bytes 688136 | tf_op jit(solution)/shard_map/ppermute | solution.py:142
  124.3 3.9 %collective-permute-start.15 = (bf16[64,1792]{1,0:T(8,128)(2,1)S(1)}, bf16[64,1792]{1,0:T(8,128)(2,1)S(1)}, u32[]{:S(2)}, u32[]{:S(2)}) collective-permute-start(bf16[64,1792]{1,0:T(8,128)(2,1)S(1)} %shard_map.100), channel_id=1, source_target_pairs={{0,14},{1,3},{2,4},{3,1},{4,2},{5,7},{6,8},{7,5},{8,6},{9,11},{10,... | collective-permute-start | bytes 688136 | tf_op jit(solution)/shard_map/ppermute | solution.py:142
  128.2 7.6 %collective-permute-done.11.refs_2_ = bf16[64,1792]{1,0:T(8,128)(2,1)S(1)} collective-permute-done((bf16[64,1792]{1,0:T(8,128)(2,1)S(1)}, bf16[64,1792]{1,0:T(8,128)(2,1)S(1)}, u32[]{:S(2)}, u32[]{:S(2)}) %collective-permute-start.11) | collective-permute-done | bytes 229408 | tf_op jit(solution)/shard_map/ppermute | solution.py:142
  136.0 1.9 %collective-permute-start.12 = (bf16[64,1792]{1,0:T(8,128)(2,1)S(1)}, bf16[64,1792]{1,0:T(8,128)(2,1)S(1)}, u32[]{:S(2)}, u32[]{:S(2)}) collective-permute-start(bf16[64,1792]{1,0:T(8,128)(2,1)S(1)} %shard_map.98), channel_id=1, source_target_pairs={{0,15},{1,2},{2,5},{3,0},{4,3},{5,6},{6,9},{7,4},{8,7},{9,10},{10,... | collective-permute-start | bytes 688136 | tf_op jit(solution)/shard_map/ppermute | solution.py:142
  138.0 5.4 %collective-permute-done.12.refs_0_ = bf16[64,1792]{1,0:T(8,128)(2,1)S(1)} collective-permute-done((bf16[64,1792]{1,0:T(8,128)(2,1)S(1)}, bf16[64,1792]{1,0:T(8,128)(2,1)S(1)}, u32[]{:S(2)}, u32[]{:S(2)}) %collective-permute-start.12) | collective-permute-done | bytes 229408 | tf_op jit(solution)/shard_map/ppermute | solution.py:142
  144.4 4.1 %all-to-all-start.1 = ((bf16[32,2,1792]{2,1,0:T(2,128)(2,1)}), bf16[32,2,1792]{2,1,0:T(2,128)(2,1)S(1)}, u32[]{:S(2)}, u32[]{:S(2)}) async-start(bf16[32,2,1792]{2,1,0:T(2,128)(2,1)} %reshape.22), calls=%async_computation.1 | async-start | bytes 458752 | tf_op jit(solution)/shard_map/all_to_all | solution.py:203
  150.2 2.7 %fusion.3 = bf16[1,1664,256]{2,1,0:T(8,128)(2,1)} fusion(bf16[512,1664]{1,0:T(8,128)(2,1)S(1)} %copy-done.12, bf16[1664,256]{1,0:T(8,128)(2,1)} %collective-permute-done.16, bf16[512,512]{1,0:T(8,128)(2,1)S(1)} %copy-done.10), kind=kOutput, calls=%fused_computation.7 | convolution fusion | flops 437485568 | bytes 3670016 | tf_op jit(solution)/shard_map/dot_general | solution.py:16
  153.0 7.5 %all-to-all-done.1 = bf16[32,2,1792]{2,1,0:T(2,128)(2,1)S(1)} async-done(((bf16[32,2,1792]{2,1,0:T(2,128)(2,1)}), bf16[32,2,1792]{2,1,0:T(2,128)(2,1)S(1)}, u32[]{:S(2)}, u32[]{:S(2)}) %all-to-all-start.1) | async-done | bytes 229408 | tf_op jit(solution)/shard_map/all_to_all | solution.py:203
  (68 shorter events, 19.3 us)
Async XLA Ops:
  0.6 12.0 %copy-start = (bf16[1,1664,256]{2,1,0:T(8,128)(2,1)S(1)}, bf16[1,1664,256]{2,1,0:T(8,128)(2,1)}, u32[]{:S(2)}) copy-start(bf16[1,1664,256]{2,1,0:T(8,128)(2,1)} %param.10) | copy-start | bytes 2555908
  0.6 15.1 %copy-start.1 = (bf16[1,256,1664]{2,1,0:T(8,128)(2,1)S(1)}, bf16[1,256,1664]{2,1,0:T(8,128)(2,1)}, u32[]{:S(2)}) copy-start(bf16[1,256,1664]{2,1,0:T(8,128)(2,1)} %param.11) | copy-start | bytes 2555908
  3.0 23.9 %all-to-all-start = ((bf16[32,2,3328]{2,1,0:T(2,128)(2,1)}), bf16[32,2,3328]{2,1,0:T(2,128)(2,1)}, u32[]{:S(2)}, u32[]{:S(2)}) async-start(bf16[32,2,3328]{2,1,0:T(2,128)(2,1)} %reshape.20), calls=%async_computation | async-start | bytes 851968 | tf_op jit(solution)/shard_map/all_to_all | solution.py:161
  12.6 24.7 %collective-permute-start.6 = (bf16[1664,256]{1,0:T(8,128)(2,1)S(1)}, bf16[1664,256]{1,0:T(8,128)(2,1)S(1)}, u32[]{:S(2)}, u32[]{:S(2)}) collective-permute-start(bf16[1664,256]{1,0:T(8,128)(2,1)S(1)} %bitcast.13), channel_id=1, source_target_pairs={{0,1},{1,0},{2,3},{3,2},{4,5},{5,4},{6,7},{7,6},{8,9},{9,8},{10,11... | collective-permute-start | bytes 2555912 | tf_op jit(solution)/shard_map/ppermute | solution.py:142
  15.8 21.5 %collective-permute-start.7 = (bf16[256,1664]{1,0:T(8,128)(2,1)S(1)}, bf16[256,1664]{1,0:T(8,128)(2,1)S(1)}, u32[]{:S(2)}, u32[]{:S(2)}) collective-permute-start(bf16[256,1664]{1,0:T(8,128)(2,1)S(1)} %bitcast.18), channel_id=1, source_target_pairs={{0,1},{1,0},{2,3},{3,2},{4,5},{5,4},{6,7},{7,6},{8,9},{9,8},{10,11... | collective-permute-start | bytes 2555912 | tf_op jit(solution)/shard_map/ppermute | solution.py:142
  28.8 9.4 %collective-permute-start.3 = (bf16[64,3328]{1,0:T(8,128)(2,1)}, bf16[64,3328]{1,0:T(8,128)(2,1)S(1)}, u32[]{:S(2)}, u32[]{:S(2)}) collective-permute-start(bf16[64,3328]{1,0:T(8,128)(2,1)} %reshape.21.refs_1_), channel_id=1, source_target_pairs={{0,14},{1,3},{2,4},{3,1},{4,2},{5,7},{6,8},{7,5},{8,6},{9,11},{10,... | collective-permute-start | bytes 1277960 | tf_op jit(solution)/shard_map/ppermute | solution.py:142
  30.7 18.9 %collective-permute-start = (bf16[64,3328]{1,0:T(8,128)(2,1)}, bf16[64,3328]{1,0:T(8,128)(2,1)S(1)}, u32[]{:S(2)}, u32[]{:S(2)}) collective-permute-start(bf16[64,3328]{1,0:T(8,128)(2,1)} %reshape.21.refs_1_), channel_id=1, source_target_pairs={{0,3},{1,14},{2,1},{3,4},{4,7},{5,2},{6,5},{7,8},{8,11},{9,6},{10,... | collective-permute-start | bytes 1277960 | tf_op jit(solution)/shard_map/ppermute | solution.py:142
  51.6 11.0 %collective-permute-start.4 = (bf16[64,3328]{1,0:T(8,128)(2,1)S(1)}, bf16[64,3328]{1,0:T(8,128)(2,1)S(1)}, u32[]{:S(2)}, u32[]{:S(2)}) collective-permute-start(bf16[64,3328]{1,0:T(8,128)(2,1)S(1)} %collective-permute-done.3.refs_1_), channel_id=1, source_target_pairs={{0,3},{1,14},{2,1},{3,4},{4,7},{5,2},{6,5},{7,8},{8,11},{9,6},{10,... | collective-permute-start | bytes 1277960 | tf_op jit(solution)/shard_map/ppermute | solution.py:142
  53.5 13.3 %collective-permute-start.1 = (bf16[64,3328]{1,0:T(8,128)(2,1)S(1)}, bf16[64,3328]{1,0:T(8,128)(2,1)S(1)}, u32[]{:S(2)}, u32[]{:S(2)}) collective-permute-start(bf16[64,3328]{1,0:T(8,128)(2,1)S(1)} %collective-permute-done.refs_0_), channel_id=1, source_target_pairs={{0,3},{1,14},{2,1},{3,4},{4,7},{5,2},{6,5},{7,8},{8,11},{9,6},{10,... | collective-permute-start | bytes 1277960 | tf_op jit(solution)/shard_map/ppermute | solution.py:142
  68.7 11.0 %collective-permute-start.5 = (bf16[64,3328]{1,0:T(8,128)(2,1)S(1)}, bf16[64,3328]{1,0:T(8,128)(2,1)S(1)}, u32[]{:S(2)}, u32[]{:S(2)}) collective-permute-start(bf16[64,3328]{1,0:T(8,128)(2,1)S(1)} %collective-permute-done.4.refs_1_), channel_id=1, source_target_pairs={{0,3},{1,14},{2,1},{3,4},{4,7},{5,2},{6,5},{7,8},{8,11},{9,6},{10,... | collective-permute-start | bytes 1277960 | tf_op jit(solution)/shard_map/ppermute | solution.py:142
  70.7 13.3 %collective-permute-start.2 = (bf16[64,3328]{1,0:T(8,128)(2,1)S(1)}, bf16[64,3328]{1,0:T(8,128)(2,1)S(1)}, u32[]{:S(2)}, u32[]{:S(2)}) collective-permute-start(bf16[64,3328]{1,0:T(8,128)(2,1)S(1)} %collective-permute-done.1.refs_0_), channel_id=1, source_target_pairs={{0,3},{1,14},{2,1},{3,4},{4,7},{5,2},{6,5},{7,8},{8,11},{9,6},{10,... | collective-permute-start | bytes 1277960 | tf_op jit(solution)/shard_map/ppermute | solution.py:142
  85.9 16.7 %copy-start.2 = (bf16[64,3328]{1,0:T(8,128)(2,1)S(1)}, bf16[64,3328]{1,0:T(8,128)(2,1)}, u32[]{:S(2)}) copy-start(bf16[64,3328]{1,0:T(8,128)(2,1)} %reshape.21.refs_1_) | copy-start | bytes 1277956
  85.9 31.4 %collective-permute-start.8 = (bf16[64,1792]{1,0:T(8,128)(2,1)S(1)}, bf16[64,1792]{1,0:T(8,128)(2,1)S(1)}, u32[]{:S(2)}, u32[]{:S(2)}) collective-permute-start(bf16[64,1792]{1,0:T(8,128)(2,1)S(1)} %get-tuple-element.22), channel_id=1, source_target_pairs={{0,15},{1,2},{2,5},{3,0},{4,3},{5,6},{6,9},{7,4},{8,7},{9,10},{10,... | collective-permute-start | bytes 688136 | tf_op jit(solution)/shard_map/ppermute | solution.py:142
  90.9 22.2 %collective-permute-start.13 = (bf16[64,1792]{1,0:T(8,128)(2,1)S(1)}, bf16[64,1792]{1,0:T(8,128)(2,1)S(1)}, u32[]{:S(2)}, u32[]{:S(2)}) collective-permute-start(bf16[64,1792]{1,0:T(8,128)(2,1)S(1)} %get-tuple-element.26), channel_id=1, source_target_pairs={{0,15},{1,2},{2,5},{3,0},{4,3},{5,6},{6,9},{7,4},{8,7},{9,10},{10,... | collective-permute-start | bytes 688136 | tf_op jit(solution)/shard_map/ppermute | solution.py:142
  92.8 9.7 %collective-permute-start.10 = (bf16[64,3328]{1,0:T(8,128)(2,1)S(1)}, bf16[64,3328]{1,0:T(8,128)(2,1)S(1)}, u32[]{:S(2)}, u32[]{:S(2)}) collective-permute-start(bf16[64,3328]{1,0:T(8,128)(2,1)S(1)} %collective-permute-done.2.refs_0_), channel_id=1, source_target_pairs={{0,3},{1,14},{2,1},{3,4},{4,7},{5,2},{6,5},{7,8},{8,11},{9,6},{10,... | collective-permute-start | bytes 1277960 | tf_op jit(solution)/shard_map/ppermute | solution.py:142
  104.5 2.2 %copy-start.7 = (bf16[512,512]{1,0:T(8,128)(2,1)}, bf16[512,512]{1,0:T(8,128)(2,1)S(1)}, u32[]{:S(2)}) copy-start(bf16[512,512]{1,0:T(8,128)(2,1)S(1)} %constant_dynamic-update-slice_fusion.4) | copy-start | bytes 1572868
  104.6 6.5 %copy-start.5 = (bf16[512,1664]{1,0:T(8,128)(2,1)}, bf16[512,1664]{1,0:T(8,128)(2,1)S(1)}, u32[]{:S(2)}) copy-start(bf16[512,1664]{1,0:T(8,128)(2,1)S(1)} %get-tuple-element.40) | copy-start | bytes 5111812
  104.6 6.5 %copy-start.11 = (bf16[512,1664]{1,0:T(8,128)(2,1)}, bf16[512,1664]{1,0:T(8,128)(2,1)S(1)}, u32[]{:S(2)}) copy-start(bf16[512,1664]{1,0:T(8,128)(2,1)S(1)} %get-tuple-element.41) | copy-start | bytes 5111812
  106.7 41.9 %collective-permute-start.17 = (bf16[256,1664]{1,0:T(8,128)(2,1)}, bf16[256,1664]{1,0:T(8,128)(2,1)S(1)}, u32[]{:S(2)}, u32[]{:S(2)}) collective-permute-start(bf16[256,1664]{1,0:T(8,128)(2,1)} %convolution_convert_fusion), channel_id=1, source_target_pairs={{0,1},{1,0},{2,3},{3,2},{4,5},{5,4},{6,7},{7,6},{8,9},{9,8},{10,11... | collective-permute-start | bytes 2555912 | tf_op jit(solution)/shard_map/ppermute | solution.py:142
  111.1 39.1 %collective-permute-start.16 = (bf16[1664,256]{1,0:T(8,128)(2,1)}, bf16[1664,256]{1,0:T(8,128)(2,1)}, u32[]{:S(2)}, u32[]{:S(2)}) collective-permute-start(bf16[1664,256]{1,0:T(8,128)(2,1)} %convolution_convert_fusion.1), channel_id=1, source_target_pairs={{0,1},{1,0},{2,3},{3,2},{4,5},{5,4},{6,7},{7,6},{8,9},{9,8},{10,11... | collective-permute-start | bytes 2555912 | tf_op jit(solution)/shard_map/ppermute | solution.py:142
  113.3 10.8 %collective-permute-start.14 = (bf16[64,1792]{1,0:T(8,128)(2,1)S(1)}, bf16[64,1792]{1,0:T(8,128)(2,1)S(1)}, u32[]{:S(2)}, u32[]{:S(2)}) collective-permute-start(bf16[64,1792]{1,0:T(8,128)(2,1)S(1)} %shard_map.99), channel_id=1, source_target_pairs={{0,15},{1,2},{2,5},{3,0},{4,3},{5,6},{6,9},{7,4},{8,7},{9,10},{10,... | collective-permute-start | bytes 688136 | tf_op jit(solution)/shard_map/ppermute | solution.py:142
  117.5 10.6 %collective-permute-start.9 = (bf16[64,1792]{1,0:T(8,128)(2,1)S(1)}, bf16[64,1792]{1,0:T(8,128)(2,1)S(1)}, u32[]{:S(2)}, u32[]{:S(2)}) collective-permute-start(bf16[64,1792]{1,0:T(8,128)(2,1)S(1)} %shard_map.95), channel_id=1, source_target_pairs={{0,15},{1,2},{2,5},{3,0},{4,3},{5,6},{6,9},{7,4},{8,7},{9,10},{10,... | collective-permute-start | bytes 688136 | tf_op jit(solution)/shard_map/ppermute | solution.py:142
  120.7 15.0 %collective-permute-start.11 = (bf16[64,1792]{1,0:T(8,128)(2,1)S(1)}, bf16[64,1792]{1,0:T(8,128)(2,1)S(1)}, u32[]{:S(2)}, u32[]{:S(2)}) collective-permute-start(bf16[64,1792]{1,0:T(8,128)(2,1)S(1)} %get-tuple-element.25), channel_id=1, source_target_pairs={{0,11},{1,6},{2,9},{3,12},{4,15},{5,10},{6,13},{7,0},{8,3},{9,14},... | collective-permute-start | bytes 688136 | tf_op jit(solution)/shard_map/ppermute | solution.py:142
  124.0 24.6 %copy-start.6 = (bf16[512,1664]{1,0:T(8,128)(2,1)S(1)}, bf16[512,1664]{1,0:T(8,128)(2,1)}, u32[]{:S(2)}) copy-start(bf16[512,1664]{1,0:T(8,128)(2,1)} %copy-done.5) | copy-start | bytes 5111812
  124.1 24.6 %copy-start.8 = (bf16[512,512]{1,0:T(8,128)(2,1)S(1)}, bf16[512,512]{1,0:T(8,128)(2,1)}, u32[]{:S(2)}) copy-start(bf16[512,512]{1,0:T(8,128)(2,1)} %copy-done.7) | copy-start | bytes 1572868
  124.3 13.7 %collective-permute-start.15 = (bf16[64,1792]{1,0:T(8,128)(2,1)S(1)}, bf16[64,1792]{1,0:T(8,128)(2,1)S(1)}, u32[]{:S(2)}, u32[]{:S(2)}) collective-permute-start(bf16[64,1792]{1,0:T(8,128)(2,1)S(1)} %shard_map.100), channel_id=1, source_target_pairs={{0,14},{1,3},{2,4},{3,1},{4,2},{5,7},{6,8},{7,5},{8,6},{9,11},{10,... | collective-permute-start | bytes 688136 | tf_op jit(solution)/shard_map/ppermute | solution.py:142
  136.0 7.3 %collective-permute-start.12 = (bf16[64,1792]{1,0:T(8,128)(2,1)S(1)}, bf16[64,1792]{1,0:T(8,128)(2,1)S(1)}, u32[]{:S(2)}, u32[]{:S(2)}) collective-permute-start(bf16[64,1792]{1,0:T(8,128)(2,1)S(1)} %shard_map.98), channel_id=1, source_target_pairs={{0,15},{1,2},{2,5},{3,0},{4,3},{5,6},{6,9},{7,4},{8,7},{9,10},{10,... | collective-permute-start | bytes 688136 | tf_op jit(solution)/shard_map/ppermute | solution.py:142
  144.4 16.0 %all-to-all-start.1 = ((bf16[32,2,1792]{2,1,0:T(2,128)(2,1)}), bf16[32,2,1792]{2,1,0:T(2,128)(2,1)S(1)}, u32[]{:S(2)}, u32[]{:S(2)}) async-start(bf16[32,2,1792]{2,1,0:T(2,128)(2,1)} %reshape.22), calls=%async_computation.1 | async-start | bytes 458752 | tf_op jit(solution)/shard_map/all_to_all | solution.py:203
  148.6 1.6 %copy-start.10 = (bf16[512,512]{1,0:T(8,128)(2,1)S(1)}, bf16[512,512]{1,0:T(8,128)(2,1)}, u32[]{:S(2)}) copy-start(bf16[512,512]{1,0:T(8,128)(2,1)} %copy-done.9) | copy-start | bytes 1572868
  148.6 1.6 %copy-start.12 = (bf16[512,1664]{1,0:T(8,128)(2,1)S(1)}, bf16[512,1664]{1,0:T(8,128)(2,1)}, u32[]{:S(2)}) copy-start(bf16[512,1664]{1,0:T(8,128)(2,1)} %copy-done.11) | copy-start | bytes 5111812
  150.2 10.3 %copy-start.3 = (s32[16,2]{0,1:T(2,128)S(1)}, s32[16,2]{0,1:T(2,128)}, u32[]{:S(2)}) copy-start(s32[16,2]{0,1:T(2,128)} %param.8) | copy-start | bytes 388
  150.2 10.3 %copy-start.4 = (bf16[16,2]{0,1:T(2,128)(2,1)S(1)}, bf16[16,2]{0,1:T(2,128)(2,1)}, u32[]{:S(2)}) copy-start(bf16[16,2]{0,1:T(2,128)(2,1)} %param.9) | copy-start | bytes 196
  (1 other events, 1.6 us)

commit v4 on v3

--- a/solution.py
+++ b/solution.py
@@ -102,6 +102,20 @@
     out_ref[:, feat:] = tail(g[:, 0:1] + g[:, 1:2])
 
 
+def transposed_dot(parts, others):
+    return mm(jnp.concatenate(parts, axis=0), jnp.concatenate(others, axis=0), ((0,), (0,)))
+
+
+def grads_body(count, at, *refs):
+    blocks, hid, pg = refs[: 2 * count], refs[2 * count : 3 * count], refs[3 * count : 4 * count]
+    second_ref, first_ref = refs[4 * count :]
+    feat, half = first_ref.shape
+    second = transposed_dot([r[:, at : at + half] for r in hid], [r[:, feat:] for r in blocks])
+    first = transposed_dot([r[:, :feat] for r in blocks], [r[:, at : at + half] for r in pg])
+    second_ref[...] = second.astype(second_ref.dtype)
+    first_ref[...] = first.astype(first_ref.dtype)
+
+
 def combine_body(cap, rows, back_ref, ids_ref, gates_ref, tg_ref, gg_ref):
     feat = tg_ref.shape[1]
     held, hit0, hit1 = matches(ids_ref[...], cap, rows)
@@ -205,16 +219,24 @@
     ).reshape(rows, slim)
 
     blocks = [c for group in groups for c in group]
+    held = blocks + hid + pg
+    work = 4 * hops * 2 * rows * feat * half
+
+    def grads(at, dtype):
+        return kernel_call(
+            functools.partial(grads_body, hops, at), [((half, feat), dtype), ((feat, half), dtype)],
+            *held, limit=20, flops=work,
+        )
+
+    peer_second, peer_first = grads(half, BF16)
+    gs = move(peer_second, swap)
+    gf = move(peer_first, swap)
     x_all = jnp.concatenate([c[:, :feat] for c in blocks], axis=0)
     scaled_all = jnp.concatenate([c[:, feat:] for c in blocks], axis=0)
-    hidden_all = jnp.concatenate(hid, axis=0)
-    pg_all = jnp.concatenate(pg, axis=0)
-    peer_second = mm(hidden_all[:, half:], scaled_all, ((0,), (0,))).astype(BF16)
-    peer_first = mm(x_all, pg_all[:, half:], ((0,), (0,))).astype(BF16)
-    gs = move(peer_second, swap)
-    gf = move(peer_first, swap)
-    own_second = mm(hidden_all[:, :half], scaled_all, ((0,), (0,)))
-    own_first = mm(x_all, pg_all[:, :half], ((0,), (0,)))
+    hid_own = jnp.concatenate([h[:, :half] for h in hid], axis=0)
+    pg_own = jnp.concatenate([p[:, :half] for p in pg], axis=0)
+    own_second = mm(hid_own, scaled_all, ((0,), (0,)))
+    own_first = mm(x_all, pg_own, ((0,), (0,)))
     grad_out_weights = (own_second + gs.astype(F32)).astype(BF16)[None]
     grad_in_weights = (own_first + gf.astype(F32)).astype(BF16)[None]
 

time: 162 us -> 150 us (0.926)
  the two profiles are of different devices: /device:TPU:73 before, /device:TPU:8 now
where the time goes in v4:
time: 150 us; the launch traced here: 149 us
  starting transfers between devices  69.6 us (46%)
  waiting for transfers between devices  54.6 us (36%)
  Pallas kernels  12.3 us (8%)
  local copies, waits for them, and re-layouts  6.62 us (4%)
  matrix products  4.94 us (3%)
    ppermute x18, starting transfers between devices, move(): return lax.ppermute(a, 'dp', pairs)  54.7 us
    ppermute x18, waiting for transfers between devices, move(): return lax.ppermute(a, 'dp', pairs)  35.6 us
    all_to_all x1, waiting for transfers between devices, per_device(): lax.all_to_all(send.reshape(experts, cap, wide), 'expert', split_axis=0,...  11.3 us
    pallas_call x11, Pallas kernels, kernel_call(): pl.pallas_call(body, out_shape=outs, in_specs=[spec] * len(args), out_spe...  10.9 us
    all_to_all x1, starting transfers between devices, per_device(): lax.all_to_all(send.reshape(experts, cap, wide), 'expert', split_axis=0,...  10.2 us
    all_to_all x1, waiting for transfers between devices, per_device(): lax.all_to_all(total.reshape(experts, cap, slim), 'expert', split_axis=0,...  7.65 us
    dot_general x2, matrix products, mm(): return lax.dot_general(a, b, (dims, ((), ())), preferred_element_type=F32)  4.94 us
    all_to_all x1, starting transfers between devices, per_device(): lax.all_to_all(total.reshape(experts, cap, slim), 'expert', split_axis=0,...  4.71 us
  transfers between devices with their start and end apart: 20, of which 12 were waited for; matrix products, arithmetic and copies ran while one was open for 6% of the time, Pallas kernels for 3%

profile of v4, /device:TPU:8, one launch (start us, length us, event | category | flops | bytes accessed | tf_op | source)
XLA Modules:
  0.0 149.3 jit_solution(5452375888107490923)
XLA Ops:
  3.0 10.2 %all-to-all-start = ((bf16[32,2,3328]{2,1,0:T(2,128)(2,1)}), bf16[32,2,3328]{2,1,0:T(2,128)(2,1)}, u32[]{:S(2)}, u32[]{:S(2)}) async-start(bf16[32,2,3328]{2,1,0:T(2,128)(2,1)} %reshape.20), calls=%async_computation | async-start | bytes 851968 | tf_op jit(solution)/shard_map/all_to_all | solution.py:175
  13.2 1.9 %collective-permute-start.6 = (bf16[1664,256]{1,0:T(8,128)(2,1)S(1)}, bf16[1664,256]{1,0:T(8,128)(2,1)S(1)}, u32[]{:S(2)}, u32[]{:S(2)}) collective-permute-start(bf16[1664,256]{1,0:T(8,128)(2,1)S(1)} %bitcast.11), channel_id=1, source_target_pairs={{0,1},{1,0},{2,3},{3,2},{4,5},{5,4},{6,7},{7,6},{8,9},{9,8},{10,11... | collective-permute-start | bytes 2555912 | tf_op jit(solution)/shard_map/ppermute | solution.py:156
  15.1 2.4 %collective-permute-start.7 = (bf16[256,1664]{1,0:T(8,128)(2,1)S(1)}, bf16[256,1664]{1,0:T(8,128)(2,1)S(1)}, u32[]{:S(2)}, u32[]{:S(2)}) collective-permute-start(bf16[256,1664]{1,0:T(8,128)(2,1)S(1)} %bitcast.16), channel_id=1, source_target_pairs={{0,1},{1,0},{2,3},{3,2},{4,5},{5,4},{6,7},{7,6},{8,9},{9,8},{10,11... | collective-permute-start | bytes 2555912 | tf_op jit(solution)/shard_map/ppermute | solution.py:156
  17.5 11.3 %all-to-all-done = bf16[32,2,3328]{2,1,0:T(2,128)(2,1)} async-done(((bf16[32,2,3328]{2,1,0:T(2,128)(2,1)}), bf16[32,2,3328]{2,1,0:T(2,128)(2,1)}, u32[]{:S(2)}, u32[]{:S(2)}) %all-to-all-start) | async-done | bytes 426016 | tf_op jit(solution)/shard_map/all_to_all | solution.py:175
  28.9 1.9 %reshape.21.refs_1_.refs_7_ = bf16[64,3328]{1,0:T(8,128)(2,1)} reshape(bf16[32,2,3328]{2,1,0:T(2,128)(2,1)} %all-to-all-done) | data formatting | bytes 851968 | tf_op jit(solution)/shard_map/reshape | solution.py:177
  30.8 1.9 %collective-permute-start = (bf16[64,3328]{1,0:T(8,128)(2,1)}, bf16[64,3328]{1,0:T(8,128)(2,1)S(1)}, u32[]{:S(2)}, u32[]{:S(2)}) collective-permute-start(bf16[64,3328]{1,0:T(8,128)(2,1)} %reshape.21.refs_1_.refs_7_), channel_id=1, source_target_pairs={{0,3},{1,14},{2,1},{3,4},{4,7},{5,2},{6,5},{7,8},{8,11},{9,6},{10,... | collective-permute-start | bytes 1277960 | tf_op jit(solution)/shard_map/ppermute | solution.py:156
  32.7 10.9 %collective-permute-start.3 = (bf16[64,3328]{1,0:T(8,128)(2,1)}, bf16[64,3328]{1,0:T(8,128)(2,1)S(1)}, u32[]{:S(2)}, u32[]{:S(2)}) collective-permute-start(bf16[64,3328]{1,0:T(8,128)(2,1)} %reshape.21.refs_1_.refs_7_), channel_id=1, source_target_pairs={{0,14},{1,3},{2,4},{3,1},{4,2},{5,7},{6,8},{7,5},{8,6},{9,11},{10,... | collective-permute-start | bytes 1277960 | tf_op jit(solution)/shard_map/ppermute | solution.py:156
  45.2 6.5 %collective-permute-done.3.refs_1_ = bf16[64,3328]{1,0:T(8,128)(2,1)S(1)} collective-permute-done((bf16[64,3328]{1,0:T(8,128)(2,1)}, bf16[64,3328]{1,0:T(8,128)(2,1)S(1)}, u32[]{:S(2)}, u32[]{:S(2)}) %collective-permute-start.3) | collective-permute-done | bytes 426016 | tf_op jit(solution)/shard_map/ppermute | solution.py:156
  53.6 1.9 %collective-permute-start.1 = (bf16[64,3328]{1,0:T(8,128)(2,1)S(1)}, bf16[64,3328]{1,0:T(8,128)(2,1)S(1)}, u32[]{:S(2)}, u32[]{:S(2)}) collective-permute-start(bf16[64,3328]{1,0:T(8,128)(2,1)S(1)} %collective-permute-done.refs_0_), channel_id=1, source_target_pairs={{0,3},{1,14},{2,1},{3,4},{4,7},{5,2},{6,5},{7,8},{8,11},{9,6},{10,... | collective-permute-start | bytes 1277960 | tf_op jit(solution)/shard_map/ppermute | solution.py:156
  55.5 1.9 %collective-permute-start.4 = (bf16[64,3328]{1,0:T(8,128)(2,1)S(1)}, bf16[64,3328]{1,0:T(8,128)(2,1)S(1)}, u32[]{:S(2)}, u32[]{:S(2)}) collective-permute-start(bf16[64,3328]{1,0:T(8,128)(2,1)S(1)} %collective-permute-done.3.refs_1_), channel_id=1, source_target_pairs={{0,3},{1,14},{2,1},{3,4},{4,7},{5,2},{6,5},{7,8},{8,11},{9,6},{10,... | collective-permute-start | bytes 1277960 | tf_op jit(solution)/shard_map/ppermute | solution.py:156
  57.6 6.7 %collective-permute-done.1.refs_0_.refs_2_ = bf16[64,3328]{1,0:T(8,128)(2,1)S(1)} collective-permute-done((bf16[64,3328]{1,0:T(8,128)(2,1)S(1)}, bf16[64,3328]{1,0:T(8,128)(2,1)S(1)}, u32[]{:S(2)}, u32[]{:S(2)}) %collective-permute-start.1) | collective-permute-done | bytes 426016 | tf_op jit(solution)/shard_map/ppermute | solution.py:156
  64.3 4.6 %collective-permute-done.4.refs_1_.refs_3_ = bf16[64,3328]{1,0:T(8,128)(2,1)S(1)} collective-permute-done((bf16[64,3328]{1,0:T(8,128)(2,1)S(1)}, bf16[64,3328]{1,0:T(8,128)(2,1)S(1)}, u32[]{:S(2)}, u32[]{:S(2)}) %collective-permute-start.4) | collective-permute-done | bytes 426016 | tf_op jit(solution)/shard_map/ppermute | solution.py:156
  72.0 1.9 %collective-permute-start.2 = (bf16[64,3328]{1,0:T(8,128)(2,1)S(1)}, bf16[64,3328]{1,0:T(8,128)(2,1)S(1)}, u32[]{:S(2)}, u32[]{:S(2)}) collective-permute-start(bf16[64,3328]{1,0:T(8,128)(2,1)S(1)} %collective-permute-done.1.refs_0_.refs_2_), channel_id=1, source_target_pairs={{0,3},{1,14},{2,1},{3,4},{4,7},{5,2},{6,5},{7,8},{8,11},{9,6},{10,... | collective-permute-start | bytes 1277960 | tf_op jit(solution)/shard_map/ppermute | solution.py:156
  73.9 1.9 %collective-permute-start.5 = (bf16[64,3328]{1,0:T(8,128)(2,1)S(1)}, bf16[64,3328]{1,0:T(8,128)(2,1)S(1)}, u32[]{:S(2)}, u32[]{:S(2)}) collective-permute-start(bf16[64,3328]{1,0:T(8,128)(2,1)S(1)} %collective-permute-done.4.refs_1_.refs_3_), channel_id=1, source_target_pairs={{0,3},{1,14},{2,1},{3,4},{4,7},{5,2},{6,5},{7,8},{8,11},{9,6},{10,... | collective-permute-start | bytes 1277960 | tf_op jit(solution)/shard_map/ppermute | solution.py:156
  75.9 6.7 %collective-permute-done.2.refs_0_.refs_4_ = bf16[64,3328]{1,0:T(8,128)(2,1)S(1)} collective-permute-done((bf16[64,3328]{1,0:T(8,128)(2,1)S(1)}, bf16[64,3328]{1,0:T(8,128)(2,1)S(1)}, u32[]{:S(2)}, u32[]{:S(2)}) %collective-permute-start.2) | collective-permute-done | bytes 426016 | tf_op jit(solution)/shard_map/ppermute | solution.py:156
  82.6 4.6 %collective-permute-done.5.refs_1_.refs_5_ = bf16[64,3328]{1,0:T(8,128)(2,1)S(1)} collective-permute-done((bf16[64,3328]{1,0:T(8,128)(2,1)S(1)}, bf16[64,3328]{1,0:T(8,128)(2,1)S(1)}, u32[]{:S(2)}, u32[]{:S(2)}) %collective-permute-start.5) | collective-permute-done | bytes 426016 | tf_op jit(solution)/shard_map/ppermute | solution.py:156
  87.2 1.9 %shard_map.93 = (bf16[128,512]{1,0:T(8,128)(2,1)S(1)}, bf16[128,512]{1,0:T(8,128)(2,1)S(1)}, bf16[64,1792]{1,0:T(8,128)(2,1)S(1)}, bf16[64,1792]{1,0:T(8,128)(2,1)S(1)}) custom-call(bf16[64,3328]{1,0:T(8,128)(2,1)S(1)} %collective-permute-done.2.refs_0_.refs_4_, bf16[64,3328]{1,0:T(8,128)(2,1)S(1)} %collective-permute-done.5.refs_1_.refs_5_, ...), custom_call_target="tpu_custom_call" | custom-call | flops 654311424 | bytes 4259840 | tf_op jit(solution)/shard_map/pallas_call | solution.py:23
  89.1 2.1 %collective-permute-start.8 = (bf16[64,1792]{1,0:T(8,128)(2,1)S(1)}, bf16[64,1792]{1,0:T(8,128)(2,1)S(1)}, u32[]{:S(2)}, u32[]{:S(2)}) collective-permute-start(bf16[64,1792]{1,0:T(8,128)(2,1)S(1)} %get-tuple-element.24), channel_id=1, source_target_pairs={{0,15},{1,2},{2,5},{3,0},{4,3},{5,6},{6,9},{7,4},{8,7},{9,10},{10,... | collective-permute-start | bytes 688136 | tf_op jit(solution)/shard_map/ppermute | solution.py:156
  91.2 2.1 %collective-permute-start.13 = (bf16[64,1792]{1,0:T(8,128)(2,1)S(1)}, bf16[64,1792]{1,0:T(8,128)(2,1)S(1)}, u32[]{:S(2)}, u32[]{:S(2)}) collective-permute-start(bf16[64,1792]{1,0:T(8,128)(2,1)S(1)} %get-tuple-element.28), channel_id=1, source_target_pairs={{0,15},{1,2},{2,5},{3,0},{4,3},{5,6},{6,9},{7,4},{8,7},{9,10},{10,... | collective-permute-start | bytes 688136 | tf_op jit(solution)/shard_map/ppermute | solution.py:156
  93.3 3.4 %collective-permute-start.10 = (bf16[64,3328]{1,0:T(8,128)(2,1)S(1)}, bf16[64,3328]{1,0:T(8,128)(2,1)S(1)}, u32[]{:S(2)}, u32[]{:S(2)}) collective-permute-start(bf16[64,3328]{1,0:T(8,128)(2,1)S(1)} %collective-permute-done.2.refs_0_.refs_4_), channel_id=1, source_target_pairs={{0,3},{1,14},{2,1},{3,4},{4,7},{5,2},{6,5},{7,8},{8,11},{9,6},{10,... | collective-permute-start | bytes 1277960 | tf_op jit(solution)/shard_map/ppermute | solution.py:156
  98.4 3.3 %collective-permute-start.9 = (bf16[64,1792]{1,0:T(8,128)(2,1)S(1)}, bf16[64,1792]{1,0:T(8,128)(2,1)S(1)}, u32[]{:S(2)}, u32[]{:S(2)}) collective-permute-start(bf16[64,1792]{1,0:T(8,128)(2,1)S(1)} %shard_map.95), channel_id=1, source_target_pairs={{0,15},{1,2},{2,5},{3,0},{4,3},{5,6},{6,9},{7,4},{8,7},{9,10},{10,... | collective-permute-start | bytes 688136 | tf_op jit(solution)/shard_map/ppermute | solution.py:156
  102.0 3.4 %collective-permute-start.14 = (bf16[64,1792]{1,0:T(8,128)(2,1)S(1)}, bf16[64,1792]{1,0:T(8,128)(2,1)S(1)}, u32[]{:S(2)}, u32[]{:S(2)}) collective-permute-start(bf16[64,1792]{1,0:T(8,128)(2,1)S(1)} %shard_map.99), channel_id=1, source_target_pairs={{0,15},{1,2},{2,5},{3,0},{4,3},{5,6},{6,9},{7,4},{8,7},{9,10},{10,... | collective-permute-start | bytes 688136 | tf_op jit(solution)/shard_map/ppermute | solution.py:156
  105.8 1.9 %shard_map.97 = (bf16[128,512]{1,0:T(8,128)(2,1)S(1)}, bf16[128,512]{1,0:T(8,128)(2,1)S(1)}, bf16[64,1792]{1,0:T(8,128)(2,1)S(1)}, bf16[64,1792]{1,0:T(8,128)(2,1)S(1)}) custom-call(bf16[64,3328]{1,0:T(8,128)(2,1)S(1)} %collective-permute-done.10.refs_0_.refs_6_, bf16[64,3328]{1,0:T(8,128)(2,1)S(1)} %copy-done.2, bf16[1664,256]{1,0:T(8,128)(2,1)S(1)} %bitcast.15, ...), custom_call_target="tpu_custom_call" | custom-call | flops 654311424 | bytes 4259840 | tf_op jit(solution)/shard_map/pallas_call | solution.py:23
  107.7 3.6 %collective-permute-start.11 = (bf16[64,1792]{1,0:T(8,128)(2,1)S(1)}, bf16[64,1792]{1,0:T(8,128)(2,1)S(1)}, u32[]{:S(2)}, u32[]{:S(2)}) collective-permute-start(bf16[64,1792]{1,0:T(8,128)(2,1)S(1)} %get-tuple-element.27), channel_id=1, source_target_pairs={{0,11},{1,6},{2,9},{3,12},{4,15},{5,10},{6,13},{7,0},{8,3},{9,14},... | collective-permute-start | bytes 688136 | tf_op jit(solution)/shard_map/ppermute | solution.py:156
  112.5 3.2 %collective-permute-start.16 = (bf16[1664,256]{1,0:T(8,128)(2,1)S(1)}, bf16[1664,256]{1,0:T(8,128)(2,1)S(1)}, u32[]{:S(2)}, u32[]{:S(2)}) collective-permute-start(bf16[1664,256]{1,0:T(8,128)(2,1)S(1)} %get-tuple-element.42), channel_id=1, source_target_pairs={{0,1},{1,0},{2,3},{3,2},{4,5},{5,4},{6,7},{7,6},{8,9},{9,8},{10,11... | collective-permute-start | bytes 2555912 | tf_op jit(solution)/shard_map/ppermute | solution.py:156
  115.7 1.9 %collective-permute-start.17 = (bf16[256,1664]{1,0:T(8,128)(2,1)S(1)}, bf16[256,1664]{1,0:T(8,128)(2,1)}, u32[]{:S(2)}, u32[]{:S(2)}) collective-permute-start(bf16[256,1664]{1,0:T(8,128)(2,1)S(1)} %get-tuple-element.43), channel_id=1, source_target_pairs={{0,1},{1,0},{2,3},{3,2},{4,5},{5,4},{6,7},{7,6},{8,9},{9,8},{10,11... | collective-permute-start | bytes 2555912 | tf_op jit(solution)/shard_map/ppermute | solution.py:156
  117.9 2.3 %collective-permute-start.15 = (bf16[64,1792]{1,0:T(8,128)(2,1)S(1)}, bf16[64,1792]{1,0:T(8,128)(2,1)S(1)}, u32[]{:S(2)}, u32[]{:S(2)}) collective-permute-start(bf16[64,1792]{1,0:T(8,128)(2,1)S(1)} %shard_map.100), channel_id=1, source_target_pairs={{0,14},{1,3},{2,4},{3,1},{4,2},{5,7},{6,8},{7,5},{8,6},{9,11},{10,... | collective-permute-start | bytes 688136 | tf_op jit(solution)/shard_map/ppermute | solution.py:156
  121.8 4.4 %collective-permute-start.12 = (bf16[64,1792]{1,0:T(8,128)(2,1)S(1)}, bf16[64,1792]{1,0:T(8,128)(2,1)S(1)}, u32[]{:S(2)}, u32[]{:S(2)}) collective-permute-start(bf16[64,1792]{1,0:T(8,128)(2,1)S(1)} %shard_map.98), channel_id=1, source_target_pairs={{0,15},{1,2},{2,5},{3,0},{4,3},{5,6},{6,9},{7,4},{8,7},{9,10},{10,... | collective-permute-start | bytes 688136 | tf_op jit(solution)/shard_map/ppermute | solution.py:156
  127.0 2.7 %collective-permute-done.12.refs_0_ = bf16[64,1792]{1,0:T(8,128)(2,1)S(1)} collective-permute-done((bf16[64,1792]{1,0:T(8,128)(2,1)S(1)}, bf16[64,1792]{1,0:T(8,128)(2,1)S(1)}, u32[]{:S(2)}, u32[]{:S(2)}) %collective-permute-start.12) | collective-permute-done | bytes 229408 | tf_op jit(solution)/shard_map/ppermute | solution.py:156
  130.8 4.7 %all-to-all-start.1 = ((bf16[32,2,1792]{2,1,0:T(2,128)(2,1)}), bf16[32,2,1792]{2,1,0:T(2,128)(2,1)S(1)}, u32[]{:S(2)}, u32[]{:S(2)}) async-start(bf16[32,2,1792]{2,1,0:T(2,128)(2,1)} %reshape.22), calls=%async_computation.1 | async-start | bytes 458752 | tf_op jit(solution)/shard_map/all_to_all | solution.py:217
  135.6 3.4 %fusion.2 = bf16[1,256,1664]{2,1,0:T(8,128)(2,1)} fusion(bf16[512,1664]{1,0:T(8,128)(2,1)} %copy-done.9, bf16[256,1664]{1,0:T(8,128)(2,1)} %collective-permute-done.17, bf16[128,256]{1,0:T(8,128)(2,1)S(1)} %slice.87, bf16[128,256]{1,0:T(8,128)(2,1)S(1)} %copy-done.8, bf16[128,256]{1,0:T(8,128)(2,1)S(1)} %copy-done.6, bf16[128,256]{1,0:T(8,128)(2,1)S(1)} %slice.84), kind=kOutput, calls=%fused_computation.4 | convolution fusion | flops 438534144 | bytes 3670016 | tf_op jit(solution)/shard_map/dot_general | solution.py:16
  140.6 7.7 %all-to-all-done.1 = bf16[32,2,1792]{2,1,0:T(2,128)(2,1)S(1)} async-done(((bf16[32,2,1792]{2,1,0:T(2,128)(2,1)}), bf16[32,2,1792]{2,1,0:T(2,128)(2,1)S(1)}, u32[]{:S(2)}, u32[]{:S(2)}) %all-to-all-start.1) | async-done | bytes 229408 | tf_op jit(solution)/shard_map/all_to_all | solution.py:217
  (66 shorter events, 18.7 us)
Async XLA Ops:
  0.6 12.6 %copy-start = (bf16[1,1664,256]{2,1,0:T(8,128)(2,1)S(1)}, bf16[1,1664,256]{2,1,0:T(8,128)(2,1)}, u32[]{:S(2)}) copy-start(bf16[1,1664,256]{2,1,0:T(8,128)(2,1)} %param.10) | copy-start | bytes 2555908
  0.6 14.5 %copy-start.1 = (bf16[1,256,1664]{2,1,0:T(8,128)(2,1)S(1)}, bf16[1,256,1664]{2,1,0:T(8,128)(2,1)}, u32[]{:S(2)}) copy-start(bf16[1,256,1664]{2,1,0:T(8,128)(2,1)} %param.11) | copy-start | bytes 2555908
  3.0 25.9 %all-to-all-start = ((bf16[32,2,3328]{2,1,0:T(2,128)(2,1)}), bf16[32,2,3328]{2,1,0:T(2,128)(2,1)}, u32[]{:S(2)}, u32[]{:S(2)}) async-start(bf16[32,2,3328]{2,1,0:T(2,128)(2,1)} %reshape.20), calls=%async_computation | async-start | bytes 851968 | tf_op jit(solution)/shard_map/all_to_all | solution.py:175
  13.2 30.5 %collective-permute-start.6 = (bf16[1664,256]{1,0:T(8,128)(2,1)S(1)}, bf16[1664,256]{1,0:T(8,128)(2,1)S(1)}, u32[]{:S(2)}, u32[]{:S(2)}) collective-permute-start(bf16[1664,256]{1,0:T(8,128)(2,1)S(1)} %bitcast.11), channel_id=1, source_target_pairs={{0,1},{1,0},{2,3},{3,2},{4,5},{5,4},{6,7},{7,6},{8,9},{9,8},{10,11... | collective-permute-start | bytes 2555912 | tf_op jit(solution)/shard_map/ppermute | solution.py:156
  15.1 28.6 %collective-permute-start.7 = (bf16[256,1664]{1,0:T(8,128)(2,1)S(1)}, bf16[256,1664]{1,0:T(8,128)(2,1)S(1)}, u32[]{:S(2)}, u32[]{:S(2)}) collective-permute-start(bf16[256,1664]{1,0:T(8,128)(2,1)S(1)} %bitcast.16), channel_id=1, source_target_pairs={{0,1},{1,0},{2,3},{3,2},{4,5},{5,4},{6,7},{7,6},{8,9},{9,8},{10,11... | collective-permute-start | bytes 2555912 | tf_op jit(solution)/shard_map/ppermute | solution.py:156
  30.8 14.4 %collective-permute-start = (bf16[64,3328]{1,0:T(8,128)(2,1)}, bf16[64,3328]{1,0:T(8,128)(2,1)S(1)}, u32[]{:S(2)}, u32[]{:S(2)}) collective-permute-start(bf16[64,3328]{1,0:T(8,128)(2,1)} %reshape.21.refs_1_.refs_7_), channel_id=1, source_target_pairs={{0,3},{1,14},{2,1},{3,4},{4,7},{5,2},{6,5},{7,8},{8,11},{9,6},{10,... | collective-permute-start | bytes 1277960 | tf_op jit(solution)/shard_map/ppermute | solution.py:156
  32.7 19.0 %collective-permute-start.3 = (bf16[64,3328]{1,0:T(8,128)(2,1)}, bf16[64,3328]{1,0:T(8,128)(2,1)S(1)}, u32[]{:S(2)}, u32[]{:S(2)}) collective-permute-start(bf16[64,3328]{1,0:T(8,128)(2,1)} %reshape.21.refs_1_.refs_7_), channel_id=1, source_target_pairs={{0,14},{1,3},{2,4},{3,1},{4,2},{5,7},{6,8},{7,5},{8,6},{9,11},{10,... | collective-permute-start | bytes 1277960 | tf_op jit(solution)/shard_map/ppermute | solution.py:156
  53.6 10.7 %collective-permute-start.1 = (bf16[64,3328]{1,0:T(8,128)(2,1)S(1)}, bf16[64,3328]{1,0:T(8,128)(2,1)S(1)}, u32[]{:S(2)}, u32[]{:S(2)}) collective-permute-start(bf16[64,3328]{1,0:T(8,128)(2,1)S(1)} %collective-permute-done.refs_0_), channel_id=1, source_target_pairs={{0,3},{1,14},{2,1},{3,4},{4,7},{5,2},{6,5},{7,8},{8,11},{9,6},{10,... | collective-permute-start | bytes 1277960 | tf_op jit(solution)/shard_map/ppermute | solution.py:156
  55.5 13.3 %collective-permute-start.4 = (bf16[64,3328]{1,0:T(8,128)(2,1)S(1)}, bf16[64,3328]{1,0:T(8,128)(2,1)S(1)}, u32[]{:S(2)}, u32[]{:S(2)}) collective-permute-start(bf16[64,3328]{1,0:T(8,128)(2,1)S(1)} %collective-permute-done.3.refs_1_), channel_id=1, source_target_pairs={{0,3},{1,14},{2,1},{3,4},{4,7},{5,2},{6,5},{7,8},{8,11},{9,6},{10,... | collective-permute-start | bytes 1277960 | tf_op jit(solution)/shard_map/ppermute | solution.py:156
  72.0 10.6 %collective-permute-start.2 = (bf16[64,3328]{1,0:T(8,128)(2,1)S(1)}, bf16[64,3328]{1,0:T(8,128)(2,1)S(1)}, u32[]{:S(2)}, u32[]{:S(2)}) collective-permute-start(bf16[64,3328]{1,0:T(8,128)(2,1)S(1)} %collective-permute-done.1.refs_0_.refs_2_), channel_id=1, source_target_pairs={{0,3},{1,14},{2,1},{3,4},{4,7},{5,2},{6,5},{7,8},{8,11},{9,6},{10,... | collective-permute-start | bytes 1277960 | tf_op jit(solution)/shard_map/ppermute | solution.py:156
  73.9 13.3 %collective-permute-start.5 = (bf16[64,3328]{1,0:T(8,128)(2,1)S(1)}, bf16[64,3328]{1,0:T(8,128)(2,1)S(1)}, u32[]{:S(2)}, u32[]{:S(2)}) collective-permute-start(bf16[64,3328]{1,0:T(8,128)(2,1)S(1)} %collective-permute-done.4.refs_1_.refs_3_), channel_id=1, source_target_pairs={{0,3},{1,14},{2,1},{3,4},{4,7},{5,2},{6,5},{7,8},{8,11},{9,6},{10,... | collective-permute-start | bytes 1277960 | tf_op jit(solution)/shard_map/ppermute | solution.py:156
  89.1 16.7 %copy-start.2 = (bf16[64,3328]{1,0:T(8,128)(2,1)S(1)}, bf16[64,3328]{1,0:T(8,128)(2,1)}, u32[]{:S(2)}) copy-start(bf16[64,3328]{1,0:T(8,128)(2,1)} %reshape.21.refs_1_.refs_7_) | copy-start | bytes 1277956
  89.1 9.0 %collective-permute-start.8 = (bf16[64,1792]{1,0:T(8,128)(2,1)S(1)}, bf16[64,1792]{1,0:T(8,128)(2,1)S(1)}, u32[]{:S(2)}, u32[]{:S(2)}) collective-permute-start(bf16[64,1792]{1,0:T(8,128)(2,1)S(1)} %get-tuple-element.24), channel_id=1, source_target_pairs={{0,15},{1,2},{2,5},{3,0},{4,3},{5,6},{6,9},{7,4},{8,7},{9,10},{10,... | collective-permute-start | bytes 688136 | tf_op jit(solution)/shard_map/ppermute | solution.py:156
  91.2 10.5 %collective-permute-start.13 = (bf16[64,1792]{1,0:T(8,128)(2,1)S(1)}, bf16[64,1792]{1,0:T(8,128)(2,1)S(1)}, u32[]{:S(2)}, u32[]{:S(2)}) collective-permute-start(bf16[64,1792]{1,0:T(8,128)(2,1)S(1)} %get-tuple-element.28), channel_id=1, source_target_pairs={{0,15},{1,2},{2,5},{3,0},{4,3},{5,6},{6,9},{7,4},{8,7},{9,10},{10,... | collective-permute-start | bytes 688136 | tf_op jit(solution)/shard_map/ppermute | solution.py:156
  93.3 12.4 %collective-permute-start.10 = (bf16[64,3328]{1,0:T(8,128)(2,1)S(1)}, bf16[64,3328]{1,0:T(8,128)(2,1)S(1)}, u32[]{:S(2)}, u32[]{:S(2)}) collective-permute-start(bf16[64,3328]{1,0:T(8,128)(2,1)S(1)} %collective-permute-done.2.refs_0_.refs_4_), channel_id=1, source_target_pairs={{0,3},{1,14},{2,1},{3,4},{4,7},{5,2},{6,5},{7,8},{8,11},{9,6},{10,... | collective-permute-start | bytes 1277960 | tf_op jit(solution)/shard_map/ppermute | solution.py:156
  98.4 21.9 %collective-permute-start.9 = (bf16[64,1792]{1,0:T(8,128)(2,1)S(1)}, bf16[64,1792]{1,0:T(8,128)(2,1)S(1)}, u32[]{:S(2)}, u32[]{:S(2)}) collective-permute-start(bf16[64,1792]{1,0:T(8,128)(2,1)S(1)} %shard_map.95), channel_id=1, source_target_pairs={{0,15},{1,2},{2,5},{3,0},{4,3},{5,6},{6,9},{7,4},{8,7},{9,10},{10,... | collective-permute-start | bytes 688136 | tf_op jit(solution)/shard_map/ppermute | solution.py:156
  102.0 15.7 %collective-permute-start.14 = (bf16[64,1792]{1,0:T(8,128)(2,1)S(1)}, bf16[64,1792]{1,0:T(8,128)(2,1)S(1)}, u32[]{:S(2)}, u32[]{:S(2)}) collective-permute-start(bf16[64,1792]{1,0:T(8,128)(2,1)S(1)} %shard_map.99), channel_id=1, source_target_pairs={{0,15},{1,2},{2,5},{3,0},{4,3},{5,6},{6,9},{7,4},{8,7},{9,10},{10,... | collective-permute-start | bytes 688136 | tf_op jit(solution)/shard_map/ppermute | solution.py:156
  107.7 13.8 %collective-permute-start.11 = (bf16[64,1792]{1,0:T(8,128)(2,1)S(1)}, bf16[64,1792]{1,0:T(8,128)(2,1)S(1)}, u32[]{:S(2)}, u32[]{:S(2)}) collective-permute-start(bf16[64,1792]{1,0:T(8,128)(2,1)S(1)} %get-tuple-element.27), channel_id=1, source_target_pairs={{0,11},{1,6},{2,9},{3,12},{4,15},{5,10},{6,13},{7,0},{8,3},{9,14},... | collective-permute-start | bytes 688136 | tf_op jit(solution)/shard_map/ppermute | solution.py:156
  112.5 26.5 %collective-permute-start.16 = (bf16[1664,256]{1,0:T(8,128)(2,1)S(1)}, bf16[1664,256]{1,0:T(8,128)(2,1)S(1)}, u32[]{:S(2)}, u32[]{:S(2)}) collective-permute-start(bf16[1664,256]{1,0:T(8,128)(2,1)S(1)} %get-tuple-element.42), channel_id=1, source_target_pairs={{0,1},{1,0},{2,3},{3,2},{4,5},{5,4},{6,7},{7,6},{8,9},{9,8},{10,11... | collective-permute-start | bytes 2555912 | tf_op jit(solution)/shard_map/ppermute | solution.py:156
  115.7 19.8 %collective-permute-start.17 = (bf16[256,1664]{1,0:T(8,128)(2,1)S(1)}, bf16[256,1664]{1,0:T(8,128)(2,1)}, u32[]{:S(2)}, u32[]{:S(2)}) collective-permute-start(bf16[256,1664]{1,0:T(8,128)(2,1)S(1)} %get-tuple-element.43), channel_id=1, source_target_pairs={{0,1},{1,0},{2,3},{3,2},{4,5},{5,4},{6,7},{7,6},{8,9},{9,8},{10,11... | collective-permute-start | bytes 2555912 | tf_op jit(solution)/shard_map/ppermute | solution.py:156
  117.9 9.1 %collective-permute-start.15 = (bf16[64,1792]{1,0:T(8,128)(2,1)S(1)}, bf16[64,1792]{1,0:T(8,128)(2,1)S(1)}, u32[]{:S(2)}, u32[]{:S(2)}) collective-permute-start(bf16[64,1792]{1,0:T(8,128)(2,1)S(1)} %shard_map.100), channel_id=1, source_target_pairs={{0,14},{1,3},{2,4},{3,1},{4,2},{5,7},{6,8},{7,5},{8,6},{9,11},{10,... | collective-permute-start | bytes 688136 | tf_op jit(solution)/shard_map/ppermute | solution.py:156
  121.8 13.7 %copy-start.6 = (bf16[128,256]{1,0:T(8,128)(2,1)S(1)}, bf16[128,256]{1,0:T(8,128)(2,1)}, u32[]{:S(2)}) copy-start(bf16[128,256]{1,0:T(8,128)(2,1)} %slice.85) | copy-start | bytes 196612
  121.8 13.7 %copy-start.8 = (bf16[128,256]{1,0:T(8,128)(2,1)S(1)}, bf16[128,256]{1,0:T(8,128)(2,1)}, u32[]{:S(2)}) copy-start(bf16[128,256]{1,0:T(8,128)(2,1)} %slice.86) | copy-start | bytes 196612
  121.8 7.9 %collective-permute-start.12 = (bf16[64,1792]{1,0:T(8,128)(2,1)S(1)}, bf16[64,1792]{1,0:T(8,128)(2,1)S(1)}, u32[]{:S(2)}, u32[]{:S(2)}) collective-permute-start(bf16[64,1792]{1,0:T(8,128)(2,1)S(1)} %shard_map.98), channel_id=1, source_target_pairs={{0,15},{1,2},{2,5},{3,0},{4,3},{5,6},{6,9},{7,4},{8,7},{9,10},{10,... | collective-permute-start | bytes 688136 | tf_op jit(solution)/shard_map/ppermute | solution.py:156
  126.2 3.5 %copy-start.9 = (bf16[512,1664]{1,0:T(8,128)(2,1)}, bf16[512,1664]{1,0:T(8,128)(2,1)S(1)}, u32[]{:S(2)}) copy-start(bf16[512,1664]{1,0:T(8,128)(2,1)S(1)} %get-tuple-element.44) | copy-start | bytes 5111812
  126.3 3.5 %copy-start.10 = (bf16[512,1664]{1,0:T(8,128)(2,1)}, bf16[512,1664]{1,0:T(8,128)(2,1)S(1)}, u32[]{:S(2)}) copy-start(bf16[512,1664]{1,0:T(8,128)(2,1)S(1)} %get-tuple-element.45) | copy-start | bytes 5111812
  130.8 17.4 %all-to-all-start.1 = ((bf16[32,2,1792]{2,1,0:T(2,128)(2,1)}), bf16[32,2,1792]{2,1,0:T(2,128)(2,1)S(1)}, u32[]{:S(2)}, u32[]{:S(2)}) async-start(bf16[32,2,1792]{2,1,0:T(2,128)(2,1)} %reshape.22), calls=%async_computation.1 | async-start | bytes 458752 | tf_op jit(solution)/shard_map/all_to_all | solution.py:217
  135.5 3.4 %copy-start.5 = (bf16[128,256]{1,0:T(8,128)(2,1)S(1)}, bf16[128,256]{1,0:T(8,128)(2,1)}, u32[]{:S(2)}) copy-start(bf16[128,256]{1,0:T(8,128)(2,1)} %slice.81) | copy-start | bytes 196612
  135.5 3.4 %copy-start.7 = (bf16[128,256]{1,0:T(8,128)(2,1)S(1)}, bf16[128,256]{1,0:T(8,128)(2,1)}, u32[]{:S(2)}) copy-start(bf16[128,256]{1,0:T(8,128)(2,1)} %slice.82) | copy-start | bytes 196612
  135.6 3.4 %copy-start.11 = (bf16[512,1664]{1,0:T(8,128)(2,1)S(1)}, bf16[512,1664]{1,0:T(8,128)(2,1)}, u32[]{:S(2)}) copy-start(bf16[512,1664]{1,0:T(8,128)(2,1)} %copy-done.10) | copy-start | bytes 5111812
  139.0 9.3 %copy-start.3 = (s32[16,2]{0,1:T(2,128)S(1)}, s32[16,2]{0,1:T(2,128)}, u32[]{:S(2)}) copy-start(s32[16,2]{0,1:T(2,128)} %param.8) | copy-start | bytes 388
  139.0 9.3 %copy-start.4 = (bf16[16,2]{0,1:T(2,128)(2,1)S(1)}, bf16[16,2]{0,1:T(2,128)(2,1)}, u32[]{:S(2)}) copy-start(bf16[16,2]{0,1:T(2,128)(2,1)} %param.9) | copy-start | bytes 196

commit v5 on v4

--- a/solution.py
+++ b/solution.py
@@ -116,6 +116,15 @@
     first_ref[...] = first.astype(first_ref.dtype)
 
 
+def total_body(feat, *refs):
+    *ins, out_ref = refs
+    shape = out_ref.shape[:2]
+    out_ref[:, :, :feat] = sum(r[:, :feat].astype(F32) for r in ins).reshape(*shape, feat).astype(BF16)
+    g = sum(r[:, feat:].astype(F32) for r in ins)
+    lanes = tail(g[:, 0:1] + g[:, 1:2]).astype(F32)
+    out_ref[:, :, feat:] = lanes.reshape(*shape, LANES).astype(BF16)
+
+
 def combine_body(cap, rows, back_ref, ids_ref, gates_ref, tg_ref, gg_ref):
     feat = tg_ref.shape[1]
     held, hit0, hit1 = matches(ids_ref[...], cap, rows)
@@ -204,8 +213,8 @@
     def plus(*args):
         return kernel_call(functools.partial(plus_body, feat), [((rows, slim), BF16)], *args)[0]
 
-    sa = move(part_a[hops - 2], home)
-    sb = move(part_b[hops - 2], home)
+    s = move(jnp.concatenate([part_a[hops - 2], part_b[hops - 2]], axis=0), home)
+    sa, sb = s[:rows], s[rows:]
     join = 0
     jump = hops - 1 - join
     far = move(part_a[hops - 1], shifted(-jump, jump % 2))
@@ -213,10 +222,11 @@
         sb = move(plus(sb, part_b[k]), over if k == 0 else home)
         extra = (far,) if k == join else ()
         sa = move(plus(sa, part_a[k], *extra), home)
-    total = plus(sa, sb, part_b[hops - 1])
-    back_rows = lax.all_to_all(
-        total.reshape(experts, cap, slim), "expert", split_axis=0, concat_axis=0, tiled=True
-    ).reshape(rows, slim)
+    (total,) = kernel_call(
+        functools.partial(total_body, feat), [((experts, cap, slim), BF16)],
+        sa, sb, part_b[hops - 1],
+    )
+    back_rows = lax.all_to_all(total, "expert", split_axis=0, concat_axis=0, tiled=True).reshape(rows, slim)
 
     blocks = [c for group in groups for c in group]
     held = blocks + hid + pg

time: 150 us -> 156 us (1.040)
  waiting for transfers between devices: 54.6 us -> 66.6 us
  starting transfers between devices: 69.6 us -> 63.9 us
    ppermute x18 -> x17, waiting for transfers between devices: 35.6 us -> 49.5 us  [move(): return lax.ppermute(a, 'dp', pairs)]
    ppermute x18 -> x17, starting transfers between devices: 54.7 us -> 49 us  [move(): return lax.ppermute(a, 'dp', pairs)]
    all_to_all x1, waiting for transfers between devices: 7.65 us -> 5.68 us  [per_device(): lax.all_to_all(total, 'expert', split_axis=0, concat_axis=0, tiled=True)]
  transfers between devices with their start and end apart: 20 -> 19, of which waited for: 12 -> 12; matrix products, arithmetic and copies ran while one was open for 6% -> 5% of each run, Pallas kernels for 3% -> 3%
where the time goes in v5:
time: 156 us
  waiting for transfers between devices  66.6 us (43%)
  starting transfers between devices  63.9 us (41%)
  Pallas kernels  13.1 us (8%)
  local copies, waits for them, and re-layouts  5.87 us (4%)
  matrix products  4.94 us (3%)
    ppermute x17, waiting for transfers between devices, move(): return lax.ppermute(a, 'dp', pairs)  49.5 us
    ppermute x17, starting transfers between devices, move(): return lax.ppermute(a, 'dp', pairs)  49 us
    pallas_call x11, Pallas kernels, kernel_call(): pl.pallas_call(body, out_shape=outs, in_specs=[spec] * len(args), out_spe...  11.8 us
    all_to_all x1, waiting for transfers between devices, per_device(): lax.all_to_all(send.reshape(experts, cap, wide), 'expert', split_axis=0,...  11.3 us
    all_to_all x1, starting transfers between devices, per_device(): lax.all_to_all(send.reshape(experts, cap, wide), 'expert', split_axis=0,...  10.2 us
    all_to_all x1, waiting for transfers between devices, per_device(): lax.all_to_all(total, 'expert', split_axis=0, concat_axis=0, tiled=True)  5.68 us
    dot_general x2, matrix products, mm(): return lax.dot_general(a, b, (dims, ((), ())), preferred_element_type=F32)  4.94 us
    all_to_all x1, starting transfers between devices, per_device(): lax.all_to_all(total, 'expert', split_axis=0, concat_axis=0, tiled=True)  4.67 us
  transfers between devices with their start and end apart: 19, of which 12 were waited for; matrix products, arithmetic and copies ran while one was open for 5% of the time, Pallas kernels for 3%

profile of v5, /device:TPU:8, one launch (start us, length us, event | category | flops | bytes accessed | tf_op | source)
XLA Modules:
  0.0 155.6 jit_solution(12453289817841488152)
XLA Ops:
  3.0 10.2 %all-to-all-start = ((bf16[32,2,3328]{2,1,0:T(2,128)(2,1)}), bf16[32,2,3328]{2,1,0:T(2,128)(2,1)}, u32[]{:S(2)}, u32[]{:S(2)}) async-start(bf16[32,2,3328]{2,1,0:T(2,128)(2,1)} %reshape.17), calls=%async_computation | async-start | bytes 851968 | tf_op jit(solution)/shard_map/all_to_all | solution.py:184
  13.2 1.9 %collective-permute-start.6 = (bf16[1664,256]{1,0:T(8,128)(2,1)S(1)}, bf16[1664,256]{1,0:T(8,128)(2,1)S(1)}, u32[]{:S(2)}, u32[]{:S(2)}) collective-permute-start(bf16[1664,256]{1,0:T(8,128)(2,1)S(1)} %bitcast.11), channel_id=1, source_target_pairs={{0,1},{1,0},{2,3},{3,2},{4,5},{5,4},{6,7},{7,6},{8,9},{9,8},{10,11... | collective-permute-start | bytes 2555912 | tf_op jit(solution)/shard_map/ppermute | solution.py:165
  15.1 2.4 %collective-permute-start.7 = (bf16[256,1664]{1,0:T(8,128)(2,1)S(1)}, bf16[256,1664]{1,0:T(8,128)(2,1)S(1)}, u32[]{:S(2)}, u32[]{:S(2)}) collective-permute-start(bf16[256,1664]{1,0:T(8,128)(2,1)S(1)} %bitcast.16), channel_id=1, source_target_pairs={{0,1},{1,0},{2,3},{3,2},{4,5},{5,4},{6,7},{7,6},{8,9},{9,8},{10,11... | collective-permute-start | bytes 2555912 | tf_op jit(solution)/shard_map/ppermute | solution.py:165
  17.5 11.3 %all-to-all-done = bf16[32,2,3328]{2,1,0:T(2,128)(2,1)} async-done(((bf16[32,2,3328]{2,1,0:T(2,128)(2,1)}), bf16[32,2,3328]{2,1,0:T(2,128)(2,1)}, u32[]{:S(2)}, u32[]{:S(2)}) %all-to-all-start) | async-done | bytes 426016 | tf_op jit(solution)/shard_map/all_to_all | solution.py:184
  28.9 1.9 %reshape.18.refs_1_.refs_7_ = bf16[64,3328]{1,0:T(8,128)(2,1)} reshape(bf16[32,2,3328]{2,1,0:T(2,128)(2,1)} %all-to-all-done) | data formatting | bytes 851968 | tf_op jit(solution)/shard_map/reshape | solution.py:186
  30.8 1.9 %collective-permute-start = (bf16[64,3328]{1,0:T(8,128)(2,1)}, bf16[64,3328]{1,0:T(8,128)(2,1)S(1)}, u32[]{:S(2)}, u32[]{:S(2)}) collective-permute-start(bf16[64,3328]{1,0:T(8,128)(2,1)} %reshape.18.refs_1_.refs_7_), channel_id=1, source_target_pairs={{0,3},{1,14},{2,1},{3,4},{4,7},{5,2},{6,5},{7,8},{8,11},{9,6},{10,... | collective-permute-start | bytes 1277960 | tf_op jit(solution)/shard_map/ppermute | solution.py:165
  32.7 10.9 %collective-permute-start.3 = (bf16[64,3328]{1,0:T(8,128)(2,1)}, bf16[64,3328]{1,0:T(8,128)(2,1)S(1)}, u32[]{:S(2)}, u32[]{:S(2)}) collective-permute-start(bf16[64,3328]{1,0:T(8,128)(2,1)} %reshape.18.refs_1_.refs_7_), channel_id=1, source_target_pairs={{0,14},{1,3},{2,4},{3,1},{4,2},{5,7},{6,8},{7,5},{8,6},{9,11},{10,... | collective-permute-start | bytes 1277960 | tf_op jit(solution)/shard_map/ppermute | solution.py:165
  45.2 6.5 %collective-permute-done.3.refs_1_ = bf16[64,3328]{1,0:T(8,128)(2,1)S(1)} collective-permute-done((bf16[64,3328]{1,0:T(8,128)(2,1)}, bf16[64,3328]{1,0:T(8,128)(2,1)S(1)}, u32[]{:S(2)}, u32[]{:S(2)}) %collective-permute-start.3) | collective-permute-done | bytes 426016 | tf_op jit(solution)/shard_map/ppermute | solution.py:165
  53.6 1.9 %collective-permute-start.1 = (bf16[64,3328]{1,0:T(8,128)(2,1)S(1)}, bf16[64,3328]{1,0:T(8,128)(2,1)S(1)}, u32[]{:S(2)}, u32[]{:S(2)}) collective-permute-start(bf16[64,3328]{1,0:T(8,128)(2,1)S(1)} %collective-permute-done.refs_0_), channel_id=1, source_target_pairs={{0,3},{1,14},{2,1},{3,4},{4,7},{5,2},{6,5},{7,8},{8,11},{9,6},{10,... | collective-permute-start | bytes 1277960 | tf_op jit(solution)/shard_map/ppermute | solution.py:165
  55.5 1.9 %collective-permute-start.4 = (bf16[64,3328]{1,0:T(8,128)(2,1)S(1)}, bf16[64,3328]{1,0:T(8,128)(2,1)S(1)}, u32[]{:S(2)}, u32[]{:S(2)}) collective-permute-start(bf16[64,3328]{1,0:T(8,128)(2,1)S(1)} %collective-permute-done.3.refs_1_), channel_id=1, source_target_pairs={{0,3},{1,14},{2,1},{3,4},{4,7},{5,2},{6,5},{7,8},{8,11},{9,6},{10,... | collective-permute-start | bytes 1277960 | tf_op jit(solution)/shard_map/ppermute | solution.py:165
  57.6 6.7 %collective-permute-done.1.refs_0_.refs_2_ = bf16[64,3328]{1,0:T(8,128)(2,1)S(1)} collective-permute-done((bf16[64,3328]{1,0:T(8,128)(2,1)S(1)}, bf16[64,3328]{1,0:T(8,128)(2,1)S(1)}, u32[]{:S(2)}, u32[]{:S(2)}) %collective-permute-start.1) | collective-permute-done | bytes 426016 | tf_op jit(solution)/shard_map/ppermute | solution.py:165
  64.3 4.6 %collective-permute-done.4.refs_1_.refs_3_ = bf16[64,3328]{1,0:T(8,128)(2,1)S(1)} collective-permute-done((bf16[64,3328]{1,0:T(8,128)(2,1)S(1)}, bf16[64,3328]{1,0:T(8,128)(2,1)S(1)}, u32[]{:S(2)}, u32[]{:S(2)}) %collective-permute-start.4) | collective-permute-done | bytes 426016 | tf_op jit(solution)/shard_map/ppermute | solution.py:165
  72.0 1.9 %collective-permute-start.2 = (bf16[64,3328]{1,0:T(8,128)(2,1)S(1)}, bf16[64,3328]{1,0:T(8,128)(2,1)S(1)}, u32[]{:S(2)}, u32[]{:S(2)}) collective-permute-start(bf16[64,3328]{1,0:T(8,128)(2,1)S(1)} %collective-permute-done.1.refs_0_.refs_2_), channel_id=1, source_target_pairs={{0,3},{1,14},{2,1},{3,4},{4,7},{5,2},{6,5},{7,8},{8,11},{9,6},{10,... | collective-permute-start | bytes 1277960 | tf_op jit(solution)/shard_map/ppermute | solution.py:165
  73.9 1.9 %collective-permute-start.5 = (bf16[64,3328]{1,0:T(8,128)(2,1)S(1)}, bf16[64,3328]{1,0:T(8,128)(2,1)S(1)}, u32[]{:S(2)}, u32[]{:S(2)}) collective-permute-start(bf16[64,3328]{1,0:T(8,128)(2,1)S(1)} %collective-permute-done.4.refs_1_.refs_3_), channel_id=1, source_target_pairs={{0,3},{1,14},{2,1},{3,4},{4,7},{5,2},{6,5},{7,8},{8,11},{9,6},{10,... | collective-permute-start | bytes 1277960 | tf_op jit(solution)/shard_map/ppermute | solution.py:165
  75.9 6.7 %collective-permute-done.2.refs_0_.refs_4_ = bf16[64,3328]{1,0:T(8,128)(2,1)S(1)} collective-permute-done((bf16[64,3328]{1,0:T(8,128)(2,1)S(1)}, bf16[64,3328]{1,0:T(8,128)(2,1)S(1)}, u32[]{:S(2)}, u32[]{:S(2)}) %collective-permute-start.2) | collective-permute-done | bytes 426016 | tf_op jit(solution)/shard_map/ppermute | solution.py:165
  82.6 4.6 %collective-permute-done.5.refs_1_.refs_5_ = bf16[64,3328]{1,0:T(8,128)(2,1)S(1)} collective-permute-done((bf16[64,3328]{1,0:T(8,128)(2,1)S(1)}, bf16[64,3328]{1,0:T(8,128)(2,1)S(1)}, u32[]{:S(2)}, u32[]{:S(2)}) %collective-permute-start.5) | collective-permute-done | bytes 426016 | tf_op jit(solution)/shard_map/ppermute | solution.py:165
  87.2 1.9 %shard_map.93 = (bf16[128,512]{1,0:T(8,128)(2,1)S(1)}, bf16[128,512]{1,0:T(8,128)(2,1)S(1)}, bf16[64,1792]{1,0:T(8,128)(2,1)S(1)}, bf16[64,1792]{1,0:T(8,128)(2,1)S(1)}) custom-call(bf16[64,3328]{1,0:T(8,128)(2,1)S(1)} %collective-permute-done.2.refs_0_.refs_4_, bf16[64,3328]{1,0:T(8,128)(2,1)S(1)} %collective-permute-done.5.refs_1_.refs_5_, ...), custom_call_target="tpu_custom_call" | custom-call | flops 654311424 | bytes 4259840 | tf_op jit(solution)/shard_map/pallas_call | solution.py:23
  89.2 2.1 %collective-permute-start.8 = (bf16[128,1792]{1,0:T(8,128)(2,1)S(1)}, bf16[128,1792]{1,0:T(8,128)(2,1)S(1)}, u32[]{:S(2)}, u32[]{:S(2)}) collective-permute-start(bf16[128,1792]{1,0:T(8,128)(2,1)S(1)} %pad_maximum_fusion), channel_id=1, source_target_pairs={{0,15},{1,2},{2,5},{3,0},{4,3},{5,6},{6,9},{7,4},{8,7},{9,10},{10,... | collective-permute-start | bytes 1376264 | tf_op jit(solution)/shard_map/ppermute | solution.py:165
  92.5 3.6 %collective-permute-start.10 = (bf16[64,3328]{1,0:T(8,128)(2,1)S(1)}, bf16[64,3328]{1,0:T(8,128)(2,1)S(1)}, u32[]{:S(2)}, u32[]{:S(2)}) collective-permute-start(bf16[64,3328]{1,0:T(8,128)(2,1)S(1)} %collective-permute-done.2.refs_0_.refs_4_), channel_id=1, source_target_pairs={{0,3},{1,14},{2,1},{3,4},{4,7},{5,2},{6,5},{7,8},{8,11},{9,6},{10,... | collective-permute-start | bytes 1277960 | tf_op jit(solution)/shard_map/ppermute | solution.py:165
  96.2 9.6 %collective-permute-done.10.refs_0_.refs_6_ = bf16[64,3328]{1,0:T(8,128)(2,1)S(1)} collective-permute-done((bf16[64,3328]{1,0:T(8,128)(2,1)S(1)}, bf16[64,3328]{1,0:T(8,128)(2,1)S(1)}, u32[]{:S(2)}, u32[]{:S(2)}) %collective-permute-start.10) | collective-permute-done | bytes 426016 | tf_op jit(solution)/shard_map/ppermute | solution.py:165
  107.7 2.1 %collective-permute-start.11 = (bf16[64,1792]{1,0:T(8,128)(2,1)S(1)}, bf16[64,1792]{1,0:T(8,128)(2,1)S(1)}, u32[]{:S(2)}, u32[]{:S(2)}) collective-permute-start(bf16[64,1792]{1,0:T(8,128)(2,1)S(1)} %get-tuple-element.28), channel_id=1, source_target_pairs={{0,11},{1,6},{2,9},{3,12},{4,15},{5,10},{6,13},{7,0},{8,3},{9,14},... | collective-permute-start | bytes 688136 | tf_op jit(solution)/shard_map/ppermute | solution.py:165
  111.0 2.3 %collective-permute-start.15 = (bf16[1664,256]{1,0:T(8,128)(2,1)S(1)}, bf16[1664,256]{1,0:T(8,128)(2,1)S(1)}, u32[]{:S(2)}, u32[]{:S(2)}) collective-permute-start(bf16[1664,256]{1,0:T(8,128)(2,1)S(1)} %get-tuple-element.42), channel_id=1, source_target_pairs={{0,1},{1,0},{2,3},{3,2},{4,5},{5,4},{6,7},{7,6},{8,9},{9,8},{10,11... | collective-permute-start | bytes 2555912 | tf_op jit(solution)/shard_map/ppermute | solution.py:165
  113.3 2.0 %collective-permute-start.16 = (bf16[256,1664]{1,0:T(8,128)(2,1)S(1)}, bf16[256,1664]{1,0:T(8,128)(2,1)}, u32[]{:S(2)}, u32[]{:S(2)}) collective-permute-start(bf16[256,1664]{1,0:T(8,128)(2,1)S(1)} %get-tuple-element.43), channel_id=1, source_target_pairs={{0,1},{1,0},{2,3},{3,2},{4,5},{5,4},{6,7},{7,6},{8,9},{9,8},{10,11... | collective-permute-start | bytes 2555912 | tf_op jit(solution)/shard_map/ppermute | solution.py:165
  115.6 2.8 %collective-permute-start.9 = (bf16[64,1792]{1,0:T(8,128)(2,1)S(1)}, bf16[64,1792]{1,0:T(8,128)(2,1)S(1)}, u32[]{:S(2)}, u32[]{:S(2)}) collective-permute-start(bf16[64,1792]{1,0:T(8,128)(2,1)S(1)} %shard_map.95), channel_id=1, source_target_pairs={{0,15},{1,2},{2,5},{3,0},{4,3},{5,6},{6,9},{7,4},{8,7},{9,10},{10,... | collective-permute-start | bytes 688136 | tf_op jit(solution)/shard_map/ppermute | solution.py:165
  118.7 1.9 %collective-permute-start.13 = (bf16[64,1792]{1,0:T(8,128)(2,1)S(1)}, bf16[64,1792]{1,0:T(8,128)(2,1)S(1)}, u32[]{:S(2)}, u32[]{:S(2)}) collective-permute-start(bf16[64,1792]{1,0:T(8,128)(2,1)S(1)} %shard_map.99), channel_id=1, source_target_pairs={{0,15},{1,2},{2,5},{3,0},{4,3},{5,6},{6,9},{7,4},{8,7},{9,10},{10,... | collective-permute-start | bytes 688136 | tf_op jit(solution)/shard_map/ppermute | solution.py:165
  120.7 3.5 %collective-permute-done.9.refs_0_ = bf16[64,1792]{1,0:T(8,128)(2,1)S(1)} collective-permute-done((bf16[64,1792]{1,0:T(8,128)(2,1)S(1)}, bf16[64,1792]{1,0:T(8,128)(2,1)S(1)}, u32[]{:S(2)}, u32[]{:S(2)}) %collective-permute-start.9) | collective-permute-done | bytes 229408 | tf_op jit(solution)/shard_map/ppermute | solution.py:165
  124.5 4.1 %collective-permute-start.12 = (bf16[64,1792]{1,0:T(8,128)(2,1)S(1)}, bf16[64,1792]{1,0:T(8,128)(2,1)S(1)}, u32[]{:S(2)}, u32[]{:S(2)}) collective-permute-start(bf16[64,1792]{1,0:T(8,128)(2,1)S(1)} %shard_map.98), channel_id=1, source_target_pairs={{0,15},{1,2},{2,5},{3,0},{4,3},{5,6},{6,9},{7,4},{8,7},{9,10},{10,... | collective-permute-start | bytes 688136 | tf_op jit(solution)/shard_map/ppermute | solution.py:165
  128.8 3.1 %collective-permute-start.14 = (bf16[64,1792]{1,0:T(8,128)(2,1)S(1)}, bf16[64,1792]{1,0:T(8,128)(2,1)S(1)}, u32[]{:S(2)}, u32[]{:S(2)}) collective-permute-start(bf16[64,1792]{1,0:T(8,128)(2,1)S(1)} %shard_map.100), channel_id=1, source_target_pairs={{0,14},{1,3},{2,4},{3,1},{4,2},{5,7},{6,8},{7,5},{8,6},{9,11},{10,... | collective-permute-start | bytes 688136 | tf_op jit(solution)/shard_map/ppermute | solution.py:165
  132.1 5.9 %collective-permute-done.14.refs_1_ = bf16[64,1792]{1,0:T(8,128)(2,1)S(1)} collective-permute-done((bf16[64,1792]{1,0:T(8,128)(2,1)S(1)}, bf16[64,1792]{1,0:T(8,128)(2,1)S(1)}, u32[]{:S(2)}, u32[]{:S(2)}) %collective-permute-start.14) | collective-permute-done | bytes 229408 | tf_op jit(solution)/shard_map/ppermute | solution.py:165
  139.1 4.7 %all-to-all-start.1 = ((bf16[32,2,1792]{2,1,0:T(2,128)(2,1)}), bf16[32,2,1792]{2,1,0:T(2,128)(2,1)S(1)}, u32[]{:S(2)}, u32[]{:S(2)}) async-start(bf16[32,2,1792]{2,1,0:T(2,128)(2,1)} %shard_map.101), calls=%async_computation.1 | async-start | bytes 458752 | tf_op jit(solution)/shard_map/all_to_all | solution.py:229
  143.8 3.4 %fusion.2 = bf16[1,256,1664]{2,1,0:T(8,128)(2,1)} fusion(bf16[512,1664]{1,0:T(8,128)(2,1)} %copy-done.9, bf16[256,1664]{1,0:T(8,128)(2,1)} %collective-permute-done.16, bf16[128,256]{1,0:T(8,128)(2,1)S(1)} %slice.95, bf16[128,256]{1,0:T(8,128)(2,1)S(1)} %copy-done.8, bf16[128,256]{1,0:T(8,128)(2,1)S(1)} %copy-done.6, bf16[128,256]{1,0:T(8,128)(2,1)S(1)} %slice.92), kind=kOutput, calls=%fused_computation.4 | convolution fusion | flops 438534144 | bytes 3670016 | tf_op jit(solution)/shard_map/dot_general | solution.py:16
  148.8 5.7 %all-to-all-done.1 = bf16[32,2,1792]{2,1,0:T(2,128)(2,1)S(1)} async-done(((bf16[32,2,1792]{2,1,0:T(2,128)(2,1)}), bf16[32,2,1792]{2,1,0:T(2,128)(2,1)S(1)}, u32[]{:S(2)}, u32[]{:S(2)}) %all-to-all-start.1) | async-done | bytes 229408 | tf_op jit(solution)/shard_map/all_to_all | solution.py:229
  (65 shorter events, 18.4 us)
Async XLA Ops:
  0.6 12.6 %copy-start = (bf16[1,1664,256]{2,1,0:T(8,128)(2,1)S(1)}, bf16[1,1664,256]{2,1,0:T(8,128)(2,1)}, u32[]{:S(2)}) copy-start(bf16[1,1664,256]{2,1,0:T(8,128)(2,1)} %param.10) | copy-start | bytes 2555908
  0.6 14.5 %copy-start.1 = (bf16[1,256,1664]{2,1,0:T(8,128)(2,1)S(1)}, bf16[1,256,1664]{2,1,0:T(8,128)(2,1)}, u32[]{:S(2)}) copy-start(bf16[1,256,1664]{2,1,0:T(8,128)(2,1)} %param.11) | copy-start | bytes 2555908
  3.0 25.9 %all-to-all-start = ((bf16[32,2,3328]{2,1,0:T(2,128)(2,1)}), bf16[32,2,3328]{2,1,0:T(2,128)(2,1)}, u32[]{:S(2)}, u32[]{:S(2)}) async-start(bf16[32,2,3328]{2,1,0:T(2,128)(2,1)} %reshape.17), calls=%async_computation | async-start | bytes 851968 | tf_op jit(solution)/shard_map/all_to_all | solution.py:184
  13.2 30.5 %collective-permute-start.6 = (bf16[1664,256]{1,0:T(8,128)(2,1)S(1)}, bf16[1664,256]{1,0:T(8,128)(2,1)S(1)}, u32[]{:S(2)}, u32[]{:S(2)}) collective-permute-start(bf16[1664,256]{1,0:T(8,128)(2,1)S(1)} %bitcast.11), channel_id=1, source_target_pairs={{0,1},{1,0},{2,3},{3,2},{4,5},{5,4},{6,7},{7,6},{8,9},{9,8},{10,11... | collective-permute-start | bytes 2555912 | tf_op jit(solution)/shard_map/ppermute | solution.py:165
  15.1 28.6 %collective-permute-start.7 = (bf16[256,1664]{1,0:T(8,128)(2,1)S(1)}, bf16[256,1664]{1,0:T(8,128)(2,1)S(1)}, u32[]{:S(2)}, u32[]{:S(2)}) collective-permute-start(bf16[256,1664]{1,0:T(8,128)(2,1)S(1)} %bitcast.16), channel_id=1, source_target_pairs={{0,1},{1,0},{2,3},{3,2},{4,5},{5,4},{6,7},{7,6},{8,9},{9,8},{10,11... | collective-permute-start | bytes 2555912 | tf_op jit(solution)/shard_map/ppermute | solution.py:165
  30.8 14.4 %collective-permute-start = (bf16[64,3328]{1,0:T(8,128)(2,1)}, bf16[64,3328]{1,0:T(8,128)(2,1)S(1)}, u32[]{:S(2)}, u32[]{:S(2)}) collective-permute-start(bf16[64,3328]{1,0:T(8,128)(2,1)} %reshape.18.refs_1_.refs_7_), channel_id=1, source_target_pairs={{0,3},{1,14},{2,1},{3,4},{4,7},{5,2},{6,5},{7,8},{8,11},{9,6},{10,... | collective-permute-start | bytes 1277960 | tf_op jit(solution)/shard_map/ppermute | solution.py:165
  32.7 19.0 %collective-permute-start.3 = (bf16[64,3328]{1,0:T(8,128)(2,1)}, bf16[64,3328]{1,0:T(8,128)(2,1)S(1)}, u32[]{:S(2)}, u32[]{:S(2)}) collective-permute-start(bf16[64,3328]{1,0:T(8,128)(2,1)} %reshape.18.refs_1_.refs_7_), channel_id=1, source_target_pairs={{0,14},{1,3},{2,4},{3,1},{4,2},{5,7},{6,8},{7,5},{8,6},{9,11},{10,... | collective-permute-start | bytes 1277960 | tf_op jit(solution)/shard_map/ppermute | solution.py:165
  53.6 10.7 %collective-permute-start.1 = (bf16[64,3328]{1,0:T(8,128)(2,1)S(1)}, bf16[64,3328]{1,0:T(8,128)(2,1)S(1)}, u32[]{:S(2)}, u32[]{:S(2)}) collective-permute-start(bf16[64,3328]{1,0:T(8,128)(2,1)S(1)} %collective-permute-done.refs_0_), channel_id=1, source_target_pairs={{0,3},{1,14},{2,1},{3,4},{4,7},{5,2},{6,5},{7,8},{8,11},{9,6},{10,... | collective-permute-start | bytes 1277960 | tf_op jit(solution)/shard_map/ppermute | solution.py:165
  55.5 13.3 %collective-permute-start.4 = (bf16[64,3328]{1,0:T(8,128)(2,1)S(1)}, bf16[64,3328]{1,0:T(8,128)(2,1)S(1)}, u32[]{:S(2)}, u32[]{:S(2)}) collective-permute-start(bf16[64,3328]{1,0:T(8,128)(2,1)S(1)} %collective-permute-done.3.refs_1_), channel_id=1, source_target_pairs={{0,3},{1,14},{2,1},{3,4},{4,7},{5,2},{6,5},{7,8},{8,11},{9,6},{10,... | collective-permute-start | bytes 1277960 | tf_op jit(solution)/shard_map/ppermute | solution.py:165
  72.0 10.6 %collective-permute-start.2 = (bf16[64,3328]{1,0:T(8,128)(2,1)S(1)}, bf16[64,3328]{1,0:T(8,128)(2,1)S(1)}, u32[]{:S(2)}, u32[]{:S(2)}) collective-permute-start(bf16[64,3328]{1,0:T(8,128)(2,1)S(1)} %collective-permute-done.1.refs_0_.refs_2_), channel_id=1, source_target_pairs={{0,3},{1,14},{2,1},{3,4},{4,7},{5,2},{6,5},{7,8},{8,11},{9,6},{10,... | collective-permute-start | bytes 1277960 | tf_op jit(solution)/shard_map/ppermute | solution.py:165
  73.9 13.3 %collective-permute-start.5 = (bf16[64,3328]{1,0:T(8,128)(2,1)S(1)}, bf16[64,3328]{1,0:T(8,128)(2,1)S(1)}, u32[]{:S(2)}, u32[]{:S(2)}) collective-permute-start(bf16[64,3328]{1,0:T(8,128)(2,1)S(1)} %collective-permute-done.4.refs_1_.refs_3_), channel_id=1, source_target_pairs={{0,3},{1,14},{2,1},{3,4},{4,7},{5,2},{6,5},{7,8},{8,11},{9,6},{10,... | collective-permute-start | bytes 1277960 | tf_op jit(solution)/shard_map/ppermute | solution.py:165
  89.1 16.7 %copy-start.2 = (bf16[64,3328]{1,0:T(8,128)(2,1)S(1)}, bf16[64,3328]{1,0:T(8,128)(2,1)}, u32[]{:S(2)}) copy-start(bf16[64,3328]{1,0:T(8,128)(2,1)} %reshape.18.refs_1_.refs_7_) | copy-start | bytes 1277956
  89.2 26.2 %collective-permute-start.8 = (bf16[128,1792]{1,0:T(8,128)(2,1)S(1)}, bf16[128,1792]{1,0:T(8,128)(2,1)S(1)}, u32[]{:S(2)}, u32[]{:S(2)}) collective-permute-start(bf16[128,1792]{1,0:T(8,128)(2,1)S(1)} %pad_maximum_fusion), channel_id=1, source_target_pairs={{0,15},{1,2},{2,5},{3,0},{4,3},{5,6},{6,9},{7,4},{8,7},{9,10},{10,... | collective-permute-start | bytes 1376264 | tf_op jit(solution)/shard_map/ppermute | solution.py:165
  92.5 13.3 %collective-permute-start.10 = (bf16[64,3328]{1,0:T(8,128)(2,1)S(1)}, bf16[64,3328]{1,0:T(8,128)(2,1)S(1)}, u32[]{:S(2)}, u32[]{:S(2)}) collective-permute-start(bf16[64,3328]{1,0:T(8,128)(2,1)S(1)} %collective-permute-done.2.refs_0_.refs_4_), channel_id=1, source_target_pairs={{0,3},{1,14},{2,1},{3,4},{4,7},{5,2},{6,5},{7,8},{8,11},{9,6},{10,... | collective-permute-start | bytes 1277960 | tf_op jit(solution)/shard_map/ppermute | solution.py:165
  107.7 12.9 %collective-permute-start.11 = (bf16[64,1792]{1,0:T(8,128)(2,1)S(1)}, bf16[64,1792]{1,0:T(8,128)(2,1)S(1)}, u32[]{:S(2)}, u32[]{:S(2)}) collective-permute-start(bf16[64,1792]{1,0:T(8,128)(2,1)S(1)} %get-tuple-element.28), channel_id=1, source_target_pairs={{0,11},{1,6},{2,9},{3,12},{4,15},{5,10},{6,13},{7,0},{8,3},{9,14},... | collective-permute-start | bytes 688136 | tf_op jit(solution)/shard_map/ppermute | solution.py:165
  111.0 36.2 %collective-permute-start.15 = (bf16[1664,256]{1,0:T(8,128)(2,1)S(1)}, bf16[1664,256]{1,0:T(8,128)(2,1)S(1)}, u32[]{:S(2)}, u32[]{:S(2)}) collective-permute-start(bf16[1664,256]{1,0:T(8,128)(2,1)S(1)} %get-tuple-element.42), channel_id=1, source_target_pairs={{0,1},{1,0},{2,3},{3,2},{4,5},{5,4},{6,7},{7,6},{8,9},{9,8},{10,11... | collective-permute-start | bytes 2555912 | tf_op jit(solution)/shard_map/ppermute | solution.py:165
  113.3 30.5 %collective-permute-start.16 = (bf16[256,1664]{1,0:T(8,128)(2,1)S(1)}, bf16[256,1664]{1,0:T(8,128)(2,1)}, u32[]{:S(2)}, u32[]{:S(2)}) collective-permute-start(bf16[256,1664]{1,0:T(8,128)(2,1)S(1)} %get-tuple-element.43), channel_id=1, source_target_pairs={{0,1},{1,0},{2,3},{3,2},{4,5},{5,4},{6,7},{7,6},{8,9},{9,8},{10,11... | collective-permute-start | bytes 2555912 | tf_op jit(solution)/shard_map/ppermute | solution.py:165
  115.6 8.5 %collective-permute-start.9 = (bf16[64,1792]{1,0:T(8,128)(2,1)S(1)}, bf16[64,1792]{1,0:T(8,128)(2,1)S(1)}, u32[]{:S(2)}, u32[]{:S(2)}) collective-permute-start(bf16[64,1792]{1,0:T(8,128)(2,1)S(1)} %shard_map.95), channel_id=1, source_target_pairs={{0,15},{1,2},{2,5},{3,0},{4,3},{5,6},{6,9},{7,4},{8,7},{9,10},{10,... | collective-permute-start | bytes 688136 | tf_op jit(solution)/shard_map/ppermute | solution.py:165
  118.7 9.9 %collective-permute-start.13 = (bf16[64,1792]{1,0:T(8,128)(2,1)S(1)}, bf16[64,1792]{1,0:T(8,128)(2,1)S(1)}, u32[]{:S(2)}, u32[]{:S(2)}) collective-permute-start(bf16[64,1792]{1,0:T(8,128)(2,1)S(1)} %shard_map.99), channel_id=1, source_target_pairs={{0,15},{1,2},{2,5},{3,0},{4,3},{5,6},{6,9},{7,4},{8,7},{9,10},{10,... | collective-permute-start | bytes 688136 | tf_op jit(solution)/shard_map/ppermute | solution.py:165
  124.4 19.4 %copy-start.6 = (bf16[128,256]{1,0:T(8,128)(2,1)S(1)}, bf16[128,256]{1,0:T(8,128)(2,1)}, u32[]{:S(2)}) copy-start(bf16[128,256]{1,0:T(8,128)(2,1)} %slice.93) | copy-start | bytes 196612
  124.4 19.4 %copy-start.8 = (bf16[128,256]{1,0:T(8,128)(2,1)S(1)}, bf16[128,256]{1,0:T(8,128)(2,1)}, u32[]{:S(2)}) copy-start(bf16[128,256]{1,0:T(8,128)(2,1)} %slice.94) | copy-start | bytes 196612
  124.5 7.7 %collective-permute-start.12 = (bf16[64,1792]{1,0:T(8,128)(2,1)S(1)}, bf16[64,1792]{1,0:T(8,128)(2,1)S(1)}, u32[]{:S(2)}, u32[]{:S(2)}) collective-permute-start(bf16[64,1792]{1,0:T(8,128)(2,1)S(1)} %shard_map.98), channel_id=1, source_target_pairs={{0,15},{1,2},{2,5},{3,0},{4,3},{5,6},{6,9},{7,4},{8,7},{9,10},{10,... | collective-permute-start | bytes 688136 | tf_op jit(solution)/shard_map/ppermute | solution.py:165
  128.8 9.1 %collective-permute-start.14 = (bf16[64,1792]{1,0:T(8,128)(2,1)S(1)}, bf16[64,1792]{1,0:T(8,128)(2,1)S(1)}, u32[]{:S(2)}, u32[]{:S(2)}) collective-permute-start(bf16[64,1792]{1,0:T(8,128)(2,1)S(1)} %shard_map.100), channel_id=1, source_target_pairs={{0,14},{1,3},{2,4},{3,1},{4,2},{5,7},{6,8},{7,5},{8,6},{9,11},{10,... | collective-permute-start | bytes 688136 | tf_op jit(solution)/shard_map/ppermute | solution.py:165
  132.0 6.0 %copy-start.9 = (bf16[512,1664]{1,0:T(8,128)(2,1)}, bf16[512,1664]{1,0:T(8,128)(2,1)S(1)}, u32[]{:S(2)}) copy-start(bf16[512,1664]{1,0:T(8,128)(2,1)S(1)} %get-tuple-element.46) | copy-start | bytes 5111812
  132.0 6.0 %copy-start.10 = (bf16[512,1664]{1,0:T(8,128)(2,1)}, bf16[512,1664]{1,0:T(8,128)(2,1)S(1)}, u32[]{:S(2)}) copy-start(bf16[512,1664]{1,0:T(8,128)(2,1)S(1)} %get-tuple-element.47) | copy-start | bytes 5111812
  139.1 15.4 %all-to-all-start.1 = ((bf16[32,2,1792]{2,1,0:T(2,128)(2,1)}), bf16[32,2,1792]{2,1,0:T(2,128)(2,1)S(1)}, u32[]{:S(2)}, u32[]{:S(2)}) async-start(bf16[32,2,1792]{2,1,0:T(2,128)(2,1)} %shard_map.101), calls=%async_computation.1 | async-start | bytes 458752 | tf_op jit(solution)/shard_map/all_to_all | solution.py:229
  143.8 3.4 %copy-start.5 = (bf16[128,256]{1,0:T(8,128)(2,1)S(1)}, bf16[128,256]{1,0:T(8,128)(2,1)}, u32[]{:S(2)}) copy-start(bf16[128,256]{1,0:T(8,128)(2,1)} %slice.89) | copy-start | bytes 196612
  143.8 3.4 %copy-start.7 = (bf16[128,256]{1,0:T(8,128)(2,1)S(1)}, bf16[128,256]{1,0:T(8,128)(2,1)}, u32[]{:S(2)}) copy-start(bf16[128,256]{1,0:T(8,128)(2,1)} %slice.90) | copy-start | bytes 196612
  143.8 3.4 %copy-start.11 = (bf16[512,1664]{1,0:T(8,128)(2,1)S(1)}, bf16[512,1664]{1,0:T(8,128)(2,1)}, u32[]{:S(2)}) copy-start(bf16[512,1664]{1,0:T(8,128)(2,1)} %copy-done.10) | copy-start | bytes 5111812
  147.2 7.4 %copy-start.3 = (s32[16,2]{0,1:T(2,128)S(1)}, s32[16,2]{0,1:T(2,128)}, u32[]{:S(2)}) copy-start(s32[16,2]{0,1:T(2,128)} %param.8) | copy-start | bytes 388
  147.2 7.4 %copy-start.4 = (bf16[16,2]{0,1:T(2,128)(2,1)S(1)}, bf16[16,2]{0,1:T(2,128)(2,1)}, u32[]{:S(2)}) copy-start(bf16[16,2]{0,1:T(2,128)(2,1)} %param.9) | copy-start | bytes 196

commit v6 on v5

--- a/solution.py
+++ b/solution.py
@@ -128,8 +128,9 @@
 def combine_body(cap, rows, back_ref, ids_ref, gates_ref, tg_ref, gg_ref):
     feat = tg_ref.shape[1]
     held, hit0, hit1 = matches(ids_ref[...], cap, rows)
-    tg_ref[...] = mm(held.astype(BF16), back_ref[:, :feat], ((0,), (0,))).astype(BF16)
-    g = back_ref[:, feat:].astype(F32)
+    back = back_ref[...].astype(F32).reshape(rows, back_ref.shape[2])
+    tg_ref[...] = mm(held.astype(BF16), back[:, :feat].astype(BF16), ((0,), (0,))).astype(BF16)
+    g = back[:, feat:]
     g = g[:, 0:1] + g[:, 1:2]
     g0 = jnp.sum(held * hit0 * g, axis=0, keepdims=True)
     g1 = jnp.sum(held * hit1 * g, axis=0, keepdims=True)
@@ -226,7 +227,7 @@
         functools.partial(total_body, feat), [((experts, cap, slim), BF16)],
         sa, sb, part_b[hops - 1],
     )
-    back_rows = lax.all_to_all(total, "expert", split_axis=0, concat_axis=0, tiled=True).reshape(rows, slim)
+    back_rows = lax.all_to_all(total, "expert", split_axis=0, concat_axis=0, tiled=True)
 
     blocks = [c for group in groups for c in group]
     held = blocks + hid + pg

time: 156 us -> 156 us (level)
  no operation moved by 1% of the time
where the time goes in v6:
time: 156 us; the launch traced here: 155 us
  waiting for transfers between devices  66.6 us (43%)
  starting transfers between devices  63.9 us (41%)
  Pallas kernels  13.1 us (8%)
  local copies, waits for them, and re-layouts  5.78 us (4%)
  matrix products  4.94 us (3%)
    ppermute x17, waiting for transfers between devices, move(): return lax.ppermute(a, 'dp', pairs)  49.5 us
    ppermute x17, starting transfers between devices, move(): return lax.ppermute(a, 'dp', pairs)  49 us
    pallas_call x11, Pallas kernels, kernel_call(): pl.pallas_call(body, out_shape=outs, in_specs=[spec] * len(args), out_spe...  11.8 us
    all_to_all x1, waiting for transfers between devices, per_device(): lax.all_to_all(send.reshape(experts, cap, wide), 'expert', split_axis=0,...  11.3 us
    all_to_all x1, starting transfers between devices, per_device(): lax.all_to_all(send.reshape(experts, cap, wide), 'expert', split_axis=0,...  10.2 us
    all_to_all x1, waiting for transfers between devices, per_device(): lax.all_to_all(total, 'expert', split_axis=0, concat_axis=0, tiled=True)  5.68 us
    dot_general x2, matrix products, mm(): return lax.dot_general(a, b, (dims, ((), ())), preferred_element_type=F32)  4.94 us
    all_to_all x1, starting transfers between devices, per_device(): lax.all_to_all(total, 'expert', split_axis=0, concat_axis=0, tiled=True)  4.67 us
  transfers between devices with their start and end apart: 19, of which 12 were waited for; matrix products, arithmetic and copies ran while one was open for 5% of the time, Pallas kernels for 3%

profile of v6, /device:TPU:8, one launch (start us, length us, event | category | flops | bytes accessed | tf_op | source)
XLA Modules:
  0.0 155.5 jit_solution(13066908471307496017)
XLA Ops:
  3.0 10.2 %all-to-all-start = ((bf16[32,2,3328]{2,1,0:T(2,128)(2,1)}), bf16[32,2,3328]{2,1,0:T(2,128)(2,1)}, u32[]{:S(2)}, u32[]{:S(2)}) async-start(bf16[32,2,3328]{2,1,0:T(2,128)(2,1)} %reshape.14), calls=%async_computation | async-start | bytes 851968 | tf_op jit(solution)/shard_map/all_to_all | solution.py:185
  13.2 1.9 %collective-permute-start.6 = (bf16[1664,256]{1,0:T(8,128)(2,1)S(1)}, bf16[1664,256]{1,0:T(8,128)(2,1)S(1)}, u32[]{:S(2)}, u32[]{:S(2)}) collective-permute-start(bf16[1664,256]{1,0:T(8,128)(2,1)S(1)} %bitcast.11), channel_id=1, source_target_pairs={{0,1},{1,0},{2,3},{3,2},{4,5},{5,4},{6,7},{7,6},{8,9},{9,8},{10,11... | collective-permute-start | bytes 2555912 | tf_op jit(solution)/shard_map/ppermute | solution.py:166
  15.1 2.4 %collective-permute-start.7 = (bf16[256,1664]{1,0:T(8,128)(2,1)S(1)}, bf16[256,1664]{1,0:T(8,128)(2,1)S(1)}, u32[]{:S(2)}, u32[]{:S(2)}) collective-permute-start(bf16[256,1664]{1,0:T(8,128)(2,1)S(1)} %bitcast.16), channel_id=1, source_target_pairs={{0,1},{1,0},{2,3},{3,2},{4,5},{5,4},{6,7},{7,6},{8,9},{9,8},{10,11... | collective-permute-start | bytes 2555912 | tf_op jit(solution)/shard_map/ppermute | solution.py:166
  17.5 11.3 %all-to-all-done = bf16[32,2,3328]{2,1,0:T(2,128)(2,1)} async-done(((bf16[32,2,3328]{2,1,0:T(2,128)(2,1)}), bf16[32,2,3328]{2,1,0:T(2,128)(2,1)}, u32[]{:S(2)}, u32[]{:S(2)}) %all-to-all-start) | async-done | bytes 426016 | tf_op jit(solution)/shard_map/all_to_all | solution.py:185
  28.9 1.9 %reshape.15.refs_1_.refs_7_ = bf16[64,3328]{1,0:T(8,128)(2,1)} reshape(bf16[32,2,3328]{2,1,0:T(2,128)(2,1)} %all-to-all-done) | data formatting | bytes 851968 | tf_op jit(solution)/shard_map/reshape | solution.py:187
  30.8 1.9 %collective-permute-start = (bf16[64,3328]{1,0:T(8,128)(2,1)}, bf16[64,3328]{1,0:T(8,128)(2,1)S(1)}, u32[]{:S(2)}, u32[]{:S(2)}) collective-permute-start(bf16[64,3328]{1,0:T(8,128)(2,1)} %reshape.15.refs_1_.refs_7_), channel_id=1, source_target_pairs={{0,3},{1,14},{2,1},{3,4},{4,7},{5,2},{6,5},{7,8},{8,11},{9,6},{10,... | collective-permute-start | bytes 1277960 | tf_op jit(solution)/shard_map/ppermute | solution.py:166
  32.7 10.9 %collective-permute-start.3 = (bf16[64,3328]{1,0:T(8,128)(2,1)}, bf16[64,3328]{1,0:T(8,128)(2,1)S(1)}, u32[]{:S(2)}, u32[]{:S(2)}) collective-permute-start(bf16[64,3328]{1,0:T(8,128)(2,1)} %reshape.15.refs_1_.refs_7_), channel_id=1, source_target_pairs={{0,14},{1,3},{2,4},{3,1},{4,2},{5,7},{6,8},{7,5},{8,6},{9,11},{10,... | collective-permute-start | bytes 1277960 | tf_op jit(solution)/shard_map/ppermute | solution.py:166
  45.2 6.5 %collective-permute-done.3.refs_1_ = bf16[64,3328]{1,0:T(8,128)(2,1)S(1)} collective-permute-done((bf16[64,3328]{1,0:T(8,128)(2,1)}, bf16[64,3328]{1,0:T(8,128)(2,1)S(1)}, u32[]{:S(2)}, u32[]{:S(2)}) %collective-permute-start.3) | collective-permute-done | bytes 426016 | tf_op jit(solution)/shard_map/ppermute | solution.py:166
  53.6 1.9 %collective-permute-start.1 = (bf16[64,3328]{1,0:T(8,128)(2,1)S(1)}, bf16[64,3328]{1,0:T(8,128)(2,1)S(1)}, u32[]{:S(2)}, u32[]{:S(2)}) collective-permute-start(bf16[64,3328]{1,0:T(8,128)(2,1)S(1)} %collective-permute-done.refs_0_), channel_id=1, source_target_pairs={{0,3},{1,14},{2,1},{3,4},{4,7},{5,2},{6,5},{7,8},{8,11},{9,6},{10,... | collective-permute-start | bytes 1277960 | tf_op jit(solution)/shard_map/ppermute | solution.py:166
  55.5 1.9 %collective-permute-start.4 = (bf16[64,3328]{1,0:T(8,128)(2,1)S(1)}, bf16[64,3328]{1,0:T(8,128)(2,1)S(1)}, u32[]{:S(2)}, u32[]{:S(2)}) collective-permute-start(bf16[64,3328]{1,0:T(8,128)(2,1)S(1)} %collective-permute-done.3.refs_1_), channel_id=1, source_target_pairs={{0,3},{1,14},{2,1},{3,4},{4,7},{5,2},{6,5},{7,8},{8,11},{9,6},{10,... | collective-permute-start | bytes 1277960 | tf_op jit(solution)/shard_map/ppermute | solution.py:166
  57.6 6.7 %collective-permute-done.1.refs_0_.refs_2_ = bf16[64,3328]{1,0:T(8,128)(2,1)S(1)} collective-permute-done((bf16[64,3328]{1,0:T(8,128)(2,1)S(1)}, bf16[64,3328]{1,0:T(8,128)(2,1)S(1)}, u32[]{:S(2)}, u32[]{:S(2)}) %collective-permute-start.1) | collective-permute-done | bytes 426016 | tf_op jit(solution)/shard_map/ppermute | solution.py:166
  64.3 4.6 %collective-permute-done.4.refs_1_.refs_3_ = bf16[64,3328]{1,0:T(8,128)(2,1)S(1)} collective-permute-done((bf16[64,3328]{1,0:T(8,128)(2,1)S(1)}, bf16[64,3328]{1,0:T(8,128)(2,1)S(1)}, u32[]{:S(2)}, u32[]{:S(2)}) %collective-permute-start.4) | collective-permute-done | bytes 426016 | tf_op jit(solution)/shard_map/ppermute | solution.py:166
  72.0 1.9 %collective-permute-start.2 = (bf16[64,3328]{1,0:T(8,128)(2,1)S(1)}, bf16[64,3328]{1,0:T(8,128)(2,1)S(1)}, u32[]{:S(2)}, u32[]{:S(2)}) collective-permute-start(bf16[64,3328]{1,0:T(8,128)(2,1)S(1)} %collective-permute-done.1.refs_0_.refs_2_), channel_id=1, source_target_pairs={{0,3},{1,14},{2,1},{3,4},{4,7},{5,2},{6,5},{7,8},{8,11},{9,6},{10,... | collective-permute-start | bytes 1277960 | tf_op jit(solution)/shard_map/ppermute | solution.py:166
  73.9 1.9 %collective-permute-start.5 = (bf16[64,3328]{1,0:T(8,128)(2,1)S(1)}, bf16[64,3328]{1,0:T(8,128)(2,1)S(1)}, u32[]{:S(2)}, u32[]{:S(2)}) collective-permute-start(bf16[64,3328]{1,0:T(8,128)(2,1)S(1)} %collective-permute-done.4.refs_1_.refs_3_), channel_id=1, source_target_pairs={{0,3},{1,14},{2,1},{3,4},{4,7},{5,2},{6,5},{7,8},{8,11},{9,6},{10,... | collective-permute-start | bytes 1277960 | tf_op jit(solution)/shard_map/ppermute | solution.py:166
  75.9 6.7 %collective-permute-done.2.refs_0_.refs_4_ = bf16[64,3328]{1,0:T(8,128)(2,1)S(1)} collective-permute-done((bf16[64,3328]{1,0:T(8,128)(2,1)S(1)}, bf16[64,3328]{1,0:T(8,128)(2,1)S(1)}, u32[]{:S(2)}, u32[]{:S(2)}) %collective-permute-start.2) | collective-permute-done | bytes 426016 | tf_op jit(solution)/shard_map/ppermute | solution.py:166
  82.6 4.6 %collective-permute-done.5.refs_1_.refs_5_ = bf16[64,3328]{1,0:T(8,128)(2,1)S(1)} collective-permute-done((bf16[64,3328]{1,0:T(8,128)(2,1)S(1)}, bf16[64,3328]{1,0:T(8,128)(2,1)S(1)}, u32[]{:S(2)}, u32[]{:S(2)}) %collective-permute-start.5) | collective-permute-done | bytes 426016 | tf_op jit(solution)/shard_map/ppermute | solution.py:166
  87.2 1.9 %shard_map.93 = (bf16[128,512]{1,0:T(8,128)(2,1)S(1)}, bf16[128,512]{1,0:T(8,128)(2,1)S(1)}, bf16[64,1792]{1,0:T(8,128)(2,1)S(1)}, bf16[64,1792]{1,0:T(8,128)(2,1)S(1)}) custom-call(bf16[64,3328]{1,0:T(8,128)(2,1)S(1)} %collective-permute-done.2.refs_0_.refs_4_, bf16[64,3328]{1,0:T(8,128)(2,1)S(1)} %collective-permute-done.5.refs_1_.refs_5_, ...), custom_call_target="tpu_custom_call" | custom-call | flops 654311424 | bytes 4259840 | tf_op jit(solution)/shard_map/pallas_call | solution.py:23
  89.2 2.1 %collective-permute-start.8 = (bf16[128,1792]{1,0:T(8,128)(2,1)S(1)}, bf16[128,1792]{1,0:T(8,128)(2,1)S(1)}, u32[]{:S(2)}, u32[]{:S(2)}) collective-permute-start(bf16[128,1792]{1,0:T(8,128)(2,1)S(1)} %pad_maximum_fusion), channel_id=1, source_target_pairs={{0,15},{1,2},{2,5},{3,0},{4,3},{5,6},{6,9},{7,4},{8,7},{9,10},{10,... | collective-permute-start | bytes 1376264 | tf_op jit(solution)/shard_map/ppermute | solution.py:166
  92.5 3.6 %collective-permute-start.10 = (bf16[64,3328]{1,0:T(8,128)(2,1)S(1)}, bf16[64,3328]{1,0:T(8,128)(2,1)S(1)}, u32[]{:S(2)}, u32[]{:S(2)}) collective-permute-start(bf16[64,3328]{1,0:T(8,128)(2,1)S(1)} %collective-permute-done.2.refs_0_.refs_4_), channel_id=1, source_target_pairs={{0,3},{1,14},{2,1},{3,4},{4,7},{5,2},{6,5},{7,8},{8,11},{9,6},{10,... | collective-permute-start | bytes 1277960 | tf_op jit(solution)/shard_map/ppermute | solution.py:166
  96.2 9.6 %collective-permute-done.10.refs_0_.refs_6_ = bf16[64,3328]{1,0:T(8,128)(2,1)S(1)} collective-permute-done((bf16[64,3328]{1,0:T(8,128)(2,1)S(1)}, bf16[64,3328]{1,0:T(8,128)(2,1)S(1)}, u32[]{:S(2)}, u32[]{:S(2)}) %collective-permute-start.10) | collective-permute-done | bytes 426016 | tf_op jit(solution)/shard_map/ppermute | solution.py:166
  107.7 2.1 %collective-permute-start.11 = (bf16[64,1792]{1,0:T(8,128)(2,1)S(1)}, bf16[64,1792]{1,0:T(8,128)(2,1)S(1)}, u32[]{:S(2)}, u32[]{:S(2)}) collective-permute-start(bf16[64,1792]{1,0:T(8,128)(2,1)S(1)} %get-tuple-element.28), channel_id=1, source_target_pairs={{0,11},{1,6},{2,9},{3,12},{4,15},{5,10},{6,13},{7,0},{8,3},{9,14},... | collective-permute-start | bytes 688136 | tf_op jit(solution)/shard_map/ppermute | solution.py:166
  111.0 2.3 %collective-permute-start.15 = (bf16[1664,256]{1,0:T(8,128)(2,1)S(1)}, bf16[1664,256]{1,0:T(8,128)(2,1)S(1)}, u32[]{:S(2)}, u32[]{:S(2)}) collective-permute-start(bf16[1664,256]{1,0:T(8,128)(2,1)S(1)} %get-tuple-element.42), channel_id=1, source_target_pairs={{0,1},{1,0},{2,3},{3,2},{4,5},{5,4},{6,7},{7,6},{8,9},{9,8},{10,11... | collective-permute-start | bytes 2555912 | tf_op jit(solution)/shard_map/ppermute | solution.py:166
  113.3 2.0 %collective-permute-start.16 = (bf16[256,1664]{1,0:T(8,128)(2,1)S(1)}, bf16[256,1664]{1,0:T(8,128)(2,1)}, u32[]{:S(2)}, u32[]{:S(2)}) collective-permute-start(bf16[256,1664]{1,0:T(8,128)(2,1)S(1)} %get-tuple-element.43), channel_id=1, source_target_pairs={{0,1},{1,0},{2,3},{3,2},{4,5},{5,4},{6,7},{7,6},{8,9},{9,8},{10,11... | collective-permute-start | bytes 2555912 | tf_op jit(solution)/shard_map/ppermute | solution.py:166
  115.6 2.8 %collective-permute-start.9 = (bf16[64,1792]{1,0:T(8,128)(2,1)S(1)}, bf16[64,1792]{1,0:T(8,128)(2,1)S(1)}, u32[]{:S(2)}, u32[]{:S(2)}) collective-permute-start(bf16[64,1792]{1,0:T(8,128)(2,1)S(1)} %shard_map.95), channel_id=1, source_target_pairs={{0,15},{1,2},{2,5},{3,0},{4,3},{5,6},{6,9},{7,4},{8,7},{9,10},{10,... | collective-permute-start | bytes 688136 | tf_op jit(solution)/shard_map/ppermute | solution.py:166
  118.7 1.9 %collective-permute-start.13 = (bf16[64,1792]{1,0:T(8,128)(2,1)S(1)}, bf16[64,1792]{1,0:T(8,128)(2,1)S(1)}, u32[]{:S(2)}, u32[]{:S(2)}) collective-permute-start(bf16[64,1792]{1,0:T(8,128)(2,1)S(1)} %shard_map.99), channel_id=1, source_target_pairs={{0,15},{1,2},{2,5},{3,0},{4,3},{5,6},{6,9},{7,4},{8,7},{9,10},{10,... | collective-permute-start | bytes 688136 | tf_op jit(solution)/shard_map/ppermute | solution.py:166
  120.7 3.5 %collective-permute-done.9.refs_0_ = bf16[64,1792]{1,0:T(8,128)(2,1)S(1)} collective-permute-done((bf16[64,1792]{1,0:T(8,128)(2,1)S(1)}, bf16[64,1792]{1,0:T(8,128)(2,1)S(1)}, u32[]{:S(2)}, u32[]{:S(2)}) %collective-permute-start.9) | collective-permute-done | bytes 229408 | tf_op jit(solution)/shard_map/ppermute | solution.py:166
  124.5 4.1 %collective-permute-start.12 = (bf16[64,1792]{1,0:T(8,128)(2,1)S(1)}, bf16[64,1792]{1,0:T(8,128)(2,1)S(1)}, u32[]{:S(2)}, u32[]{:S(2)}) collective-permute-start(bf16[64,1792]{1,0:T(8,128)(2,1)S(1)} %shard_map.98), channel_id=1, source_target_pairs={{0,15},{1,2},{2,5},{3,0},{4,3},{5,6},{6,9},{7,4},{8,7},{9,10},{10,... | collective-permute-start | bytes 688136 | tf_op jit(solution)/shard_map/ppermute | solution.py:166
  128.8 3.1 %collective-permute-start.14 = (bf16[64,1792]{1,0:T(8,128)(2,1)S(1)}, bf16[64,1792]{1,0:T(8,128)(2,1)S(1)}, u32[]{:S(2)}, u32[]{:S(2)}) collective-permute-start(bf16[64,1792]{1,0:T(8,128)(2,1)S(1)} %shard_map.100), channel_id=1, source_target_pairs={{0,14},{1,3},{2,4},{3,1},{4,2},{5,7},{6,8},{7,5},{8,6},{9,11},{10,... | collective-permute-start | bytes 688136 | tf_op jit(solution)/shard_map/ppermute | solution.py:166
  132.1 5.9 %collective-permute-done.14.refs_1_ = bf16[64,1792]{1,0:T(8,128)(2,1)S(1)} collective-permute-done((bf16[64,1792]{1,0:T(8,128)(2,1)S(1)}, bf16[64,1792]{1,0:T(8,128)(2,1)S(1)}, u32[]{:S(2)}, u32[]{:S(2)}) %collective-permute-start.14) | collective-permute-done | bytes 229408 | tf_op jit(solution)/shard_map/ppermute | solution.py:166
  139.1 4.7 %all-to-all-start.1 = ((bf16[32,2,1792]{2,1,0:T(2,128)(2,1)}), bf16[32,2,1792]{2,1,0:T(2,128)(2,1)S(1)}, u32[]{:S(2)}, u32[]{:S(2)}) async-start(bf16[32,2,1792]{2,1,0:T(2,128)(2,1)} %shard_map.101), calls=%async_computation.1 | async-start | bytes 458752 | tf_op jit(solution)/shard_map/all_to_all | solution.py:230
  143.8 3.4 %fusion.2 = bf16[1,256,1664]{2,1,0:T(8,128)(2,1)} fusion(bf16[512,1664]{1,0:T(8,128)(2,1)} %copy-done.9, bf16[256,1664]{1,0:T(8,128)(2,1)} %collective-permute-done.16, bf16[128,256]{1,0:T(8,128)(2,1)S(1)} %slice.95, bf16[128,256]{1,0:T(8,128)(2,1)S(1)} %copy-done.8, bf16[128,256]{1,0:T(8,128)(2,1)S(1)} %copy-done.6, bf16[128,256]{1,0:T(8,128)(2,1)S(1)} %slice.92), kind=kOutput, calls=%fused_computation.4 | convolution fusion | flops 438534144 | bytes 3670016 | tf_op jit(solution)/shard_map/dot_general | solution.py:16
  148.8 5.7 %all-to-all-done.1.back_ref = bf16[32,2,1792]{2,1,0:T(2,128)(2,1)S(1)} async-done(((bf16[32,2,1792]{2,1,0:T(2,128)(2,1)}), bf16[32,2,1792]{2,1,0:T(2,128)(2,1)S(1)}, u32[]{:S(2)}, u32[]{:S(2)}) %all-to-all-start.1) | async-done | bytes 229408 | tf_op jit(solution)/shard_map/all_to_all | solution.py:230
  (64 shorter events, 18.3 us)
Async XLA Ops:
  0.6 12.6 %copy-start = (bf16[1,1664,256]{2,1,0:T(8,128)(2,1)S(1)}, bf16[1,1664,256]{2,1,0:T(8,128)(2,1)}, u32[]{:S(2)}) copy-start(bf16[1,1664,256]{2,1,0:T(8,128)(2,1)} %param.10) | copy-start | bytes 2555908
  0.6 14.5 %copy-start.1 = (bf16[1,256,1664]{2,1,0:T(8,128)(2,1)S(1)}, bf16[1,256,1664]{2,1,0:T(8,128)(2,1)}, u32[]{:S(2)}) copy-start(bf16[1,256,1664]{2,1,0:T(8,128)(2,1)} %param.11) | copy-start | bytes 2555908
  3.0 25.9 %all-to-all-start = ((bf16[32,2,3328]{2,1,0:T(2,128)(2,1)}), bf16[32,2,3328]{2,1,0:T(2,128)(2,1)}, u32[]{:S(2)}, u32[]{:S(2)}) async-start(bf16[32,2,3328]{2,1,0:T(2,128)(2,1)} %reshape.14), calls=%async_computation | async-start | bytes 851968 | tf_op jit(solution)/shard_map/all_to_all | solution.py:185
  13.2 30.5 %collective-permute-start.6 = (bf16[1664,256]{1,0:T(8,128)(2,1)S(1)}, bf16[1664,256]{1,0:T(8,128)(2,1)S(1)}, u32[]{:S(2)}, u32[]{:S(2)}) collective-permute-start(bf16[1664,256]{1,0:T(8,128)(2,1)S(1)} %bitcast.11), channel_id=1, source_target_pairs={{0,1},{1,0},{2,3},{3,2},{4,5},{5,4},{6,7},{7,6},{8,9},{9,8},{10,11... | collective-permute-start | bytes 2555912 | tf_op jit(solution)/shard_map/ppermute | solution.py:166
  15.1 28.6 %collective-permute-start.7 = (bf16[256,1664]{1,0:T(8,128)(2,1)S(1)}, bf16[256,1664]{1,0:T(8,128)(2,1)S(1)}, u32[]{:S(2)}, u32[]{:S(2)}) collective-permute-start(bf16[256,1664]{1,0:T(8,128)(2,1)S(1)} %bitcast.16), channel_id=1, source_target_pairs={{0,1},{1,0},{2,3},{3,2},{4,5},{5,4},{6,7},{7,6},{8,9},{9,8},{10,11... | collective-permute-start | bytes 2555912 | tf_op jit(solution)/shard_map/ppermute | solution.py:166
  30.8 14.4 %collective-permute-start = (bf16[64,3328]{1,0:T(8,128)(2,1)}, bf16[64,3328]{1,0:T(8,128)(2,1)S(1)}, u32[]{:S(2)}, u32[]{:S(2)}) collective-permute-start(bf16[64,3328]{1,0:T(8,128)(2,1)} %reshape.15.refs_1_.refs_7_), channel_id=1, source_target_pairs={{0,3},{1,14},{2,1},{3,4},{4,7},{5,2},{6,5},{7,8},{8,11},{9,6},{10,... | collective-permute-start | bytes 1277960 | tf_op jit(solution)/shard_map/ppermute | solution.py:166
  32.7 19.0 %collective-permute-start.3 = (bf16[64,3328]{1,0:T(8,128)(2,1)}, bf16[64,3328]{1,0:T(8,128)(2,1)S(1)}, u32[]{:S(2)}, u32[]{:S(2)}) collective-permute-start(bf16[64,3328]{1,0:T(8,128)(2,1)} %reshape.15.refs_1_.refs_7_), channel_id=1, source_target_pairs={{0,14},{1,3},{2,4},{3,1},{4,2},{5,7},{6,8},{7,5},{8,6},{9,11},{10,... | collective-permute-start | bytes 1277960 | tf_op jit(solution)/shard_map/ppermute | solution.py:166
  53.6 10.7 %collective-permute-start.1 = (bf16[64,3328]{1,0:T(8,128)(2,1)S(1)}, bf16[64,3328]{1,0:T(8,128)(2,1)S(1)}, u32[]{:S(2)}, u32[]{:S(2)}) collective-permute-start(bf16[64,3328]{1,0:T(8,128)(2,1)S(1)} %collective-permute-done.refs_0_), channel_id=1, source_target_pairs={{0,3},{1,14},{2,1},{3,4},{4,7},{5,2},{6,5},{7,8},{8,11},{9,6},{10,... | collective-permute-start | bytes 1277960 | tf_op jit(solution)/shard_map/ppermute | solution.py:166
  55.5 13.3 %collective-permute-start.4 = (bf16[64,3328]{1,0:T(8,128)(2,1)S(1)}, bf16[64,3328]{1,0:T(8,128)(2,1)S(1)}, u32[]{:S(2)}, u32[]{:S(2)}) collective-permute-start(bf16[64,3328]{1,0:T(8,128)(2,1)S(1)} %collective-permute-done.3.refs_1_), channel_id=1, source_target_pairs={{0,3},{1,14},{2,1},{3,4},{4,7},{5,2},{6,5},{7,8},{8,11},{9,6},{10,... | collective-permute-start | bytes 1277960 | tf_op jit(solution)/shard_map/ppermute | solution.py:166
  72.0 10.6 %collective-permute-start.2 = (bf16[64,3328]{1,0:T(8,128)(2,1)S(1)}, bf16[64,3328]{1,0:T(8,128)(2,1)S(1)}, u32[]{:S(2)}, u32[]{:S(2)}) collective-permute-start(bf16[64,3328]{1,0:T(8,128)(2,1)S(1)} %collective-permute-done.1.refs_0_.refs_2_), channel_id=1, source_target_pairs={{0,3},{1,14},{2,1},{3,4},{4,7},{5,2},{6,5},{7,8},{8,11},{9,6},{10,... | collective-permute-start | bytes 1277960 | tf_op jit(solution)/shard_map/ppermute | solution.py:166
  73.9 13.3 %collective-permute-start.5 = (bf16[64,3328]{1,0:T(8,128)(2,1)S(1)}, bf16[64,3328]{1,0:T(8,128)(2,1)S(1)}, u32[]{:S(2)}, u32[]{:S(2)}) collective-permute-start(bf16[64,3328]{1,0:T(8,128)(2,1)S(1)} %collective-permute-done.4.refs_1_.refs_3_), channel_id=1, source_target_pairs={{0,3},{1,14},{2,1},{3,4},{4,7},{5,2},{6,5},{7,8},{8,11},{9,6},{10,... | collective-permute-start | bytes 1277960 | tf_op jit(solution)/shard_map/ppermute | solution.py:166
  89.1 16.7 %copy-start.2 = (bf16[64,3328]{1,0:T(8,128)(2,1)S(1)}, bf16[64,3328]{1,0:T(8,128)(2,1)}, u32[]{:S(2)}) copy-start(bf16[64,3328]{1,0:T(8,128)(2,1)} %reshape.15.refs_1_.refs_7_) | copy-start | bytes 1277956
  89.2 26.2 %collective-permute-start.8 = (bf16[128,1792]{1,0:T(8,128)(2,1)S(1)}, bf16[128,1792]{1,0:T(8,128)(2,1)S(1)}, u32[]{:S(2)}, u32[]{:S(2)}) collective-permute-start(bf16[128,1792]{1,0:T(8,128)(2,1)S(1)} %pad_maximum_fusion), channel_id=1, source_target_pairs={{0,15},{1,2},{2,5},{3,0},{4,3},{5,6},{6,9},{7,4},{8,7},{9,10},{10,... | collective-permute-start | bytes 1376264 | tf_op jit(solution)/shard_map/ppermute | solution.py:166
  92.5 13.3 %collective-permute-start.10 = (bf16[64,3328]{1,0:T(8,128)(2,1)S(1)}, bf16[64,3328]{1,0:T(8,128)(2,1)S(1)}, u32[]{:S(2)}, u32[]{:S(2)}) collective-permute-start(bf16[64,3328]{1,0:T(8,128)(2,1)S(1)} %collective-permute-done.2.refs_0_.refs_4_), channel_id=1, source_target_pairs={{0,3},{1,14},{2,1},{3,4},{4,7},{5,2},{6,5},{7,8},{8,11},{9,6},{10,... | collective-permute-start | bytes 1277960 | tf_op jit(solution)/shard_map/ppermute | solution.py:166
  107.7 12.9 %collective-permute-start.11 = (bf16[64,1792]{1,0:T(8,128)(2,1)S(1)}, bf16[64,1792]{1,0:T(8,128)(2,1)S(1)}, u32[]{:S(2)}, u32[]{:S(2)}) collective-permute-start(bf16[64,1792]{1,0:T(8,128)(2,1)S(1)} %get-tuple-element.28), channel_id=1, source_target_pairs={{0,11},{1,6},{2,9},{3,12},{4,15},{5,10},{6,13},{7,0},{8,3},{9,14},... | collective-permute-start | bytes 688136 | tf_op jit(solution)/shard_map/ppermute | solution.py:166
  111.0 36.2 %collective-permute-start.15 = (bf16[1664,256]{1,0:T(8,128)(2,1)S(1)}, bf16[1664,256]{1,0:T(8,128)(2,1)S(1)}, u32[]{:S(2)}, u32[]{:S(2)}) collective-permute-start(bf16[1664,256]{1,0:T(8,128)(2,1)S(1)} %get-tuple-element.42), channel_id=1, source_target_pairs={{0,1},{1,0},{2,3},{3,2},{4,5},{5,4},{6,7},{7,6},{8,9},{9,8},{10,11... | collective-permute-start | bytes 2555912 | tf_op jit(solution)/shard_map/ppermute | solution.py:166
  113.3 30.5 %collective-permute-start.16 = (bf16[256,1664]{1,0:T(8,128)(2,1)S(1)}, bf16[256,1664]{1,0:T(8,128)(2,1)}, u32[]{:S(2)}, u32[]{:S(2)}) collective-permute-start(bf16[256,1664]{1,0:T(8,128)(2,1)S(1)} %get-tuple-element.43), channel_id=1, source_target_pairs={{0,1},{1,0},{2,3},{3,2},{4,5},{5,4},{6,7},{7,6},{8,9},{9,8},{10,11... | collective-permute-start | bytes 2555912 | tf_op jit(solution)/shard_map/ppermute | solution.py:166
  115.6 8.5 %collective-permute-start.9 = (bf16[64,1792]{1,0:T(8,128)(2,1)S(1)}, bf16[64,1792]{1,0:T(8,128)(2,1)S(1)}, u32[]{:S(2)}, u32[]{:S(2)}) collective-permute-start(bf16[64,1792]{1,0:T(8,128)(2,1)S(1)} %shard_map.95), channel_id=1, source_target_pairs={{0,15},{1,2},{2,5},{3,0},{4,3},{5,6},{6,9},{7,4},{8,7},{9,10},{10,... | collective-permute-start | bytes 688136 | tf_op jit(solution)/shard_map/ppermute | solution.py:166
  118.7 9.9 %collective-permute-start.13 = (bf16[64,1792]{1,0:T(8,128)(2,1)S(1)}, bf16[64,1792]{1,0:T(8,128)(2,1)S(1)}, u32[]{:S(2)}, u32[]{:S(2)}) collective-permute-start(bf16[64,1792]{1,0:T(8,128)(2,1)S(1)} %shard_map.99), channel_id=1, source_target_pairs={{0,15},{1,2},{2,5},{3,0},{4,3},{5,6},{6,9},{7,4},{8,7},{9,10},{10,... | collective-permute-start | bytes 688136 | tf_op jit(solution)/shard_map/ppermute | solution.py:166
  124.4 19.4 %copy-start.6 = (bf16[128,256]{1,0:T(8,128)(2,1)S(1)}, bf16[128,256]{1,0:T(8,128)(2,1)}, u32[]{:S(2)}) copy-start(bf16[128,256]{1,0:T(8,128)(2,1)} %slice.93) | copy-start | bytes 196612
  124.4 19.4 %copy-start.8 = (bf16[128,256]{1,0:T(8,128)(2,1)S(1)}, bf16[128,256]{1,0:T(8,128)(2,1)}, u32[]{:S(2)}) copy-start(bf16[128,256]{1,0:T(8,128)(2,1)} %slice.94) | copy-start | bytes 196612
  124.5 7.7 %collective-permute-start.12 = (bf16[64,1792]{1,0:T(8,128)(2,1)S(1)}, bf16[64,1792]{1,0:T(8,128)(2,1)S(1)}, u32[]{:S(2)}, u32[]{:S(2)}) collective-permute-start(bf16[64,1792]{1,0:T(8,128)(2,1)S(1)} %shard_map.98), channel_id=1, source_target_pairs={{0,15},{1,2},{2,5},{3,0},{4,3},{5,6},{6,9},{7,4},{8,7},{9,10},{10,... | collective-permute-start | bytes 688136 | tf_op jit(solution)/shard_map/ppermute | solution.py:166
  128.8 9.1 %collective-permute-start.14 = (bf16[64,1792]{1,0:T(8,128)(2,1)S(1)}, bf16[64,1792]{1,0:T(8,128)(2,1)S(1)}, u32[]{:S(2)}, u32[]{:S(2)}) collective-permute-start(bf16[64,1792]{1,0:T(8,128)(2,1)S(1)} %shard_map.100), channel_id=1, source_target_pairs={{0,14},{1,3},{2,4},{3,1},{4,2},{5,7},{6,8},{7,5},{8,6},{9,11},{10,... | collective-permute-start | bytes 688136 | tf_op jit(solution)/shard_map/ppermute | solution.py:166
  132.0 6.0 %copy-start.9 = (bf16[512,1664]{1,0:T(8,128)(2,1)}, bf16[512,1664]{1,0:T(8,128)(2,1)S(1)}, u32[]{:S(2)}) copy-start(bf16[512,1664]{1,0:T(8,128)(2,1)S(1)} %get-tuple-element.46) | copy-start | bytes 5111812
  132.0 6.0 %copy-start.10 = (bf16[512,1664]{1,0:T(8,128)(2,1)}, bf16[512,1664]{1,0:T(8,128)(2,1)S(1)}, u32[]{:S(2)}) copy-start(bf16[512,1664]{1,0:T(8,128)(2,1)S(1)} %get-tuple-element.47) | copy-start | bytes 5111812
  139.1 15.4 %all-to-all-start.1 = ((bf16[32,2,1792]{2,1,0:T(2,128)(2,1)}), bf16[32,2,1792]{2,1,0:T(2,128)(2,1)S(1)}, u32[]{:S(2)}, u32[]{:S(2)}) async-start(bf16[32,2,1792]{2,1,0:T(2,128)(2,1)} %shard_map.101), calls=%async_computation.1 | async-start | bytes 458752 | tf_op jit(solution)/shard_map/all_to_all | solution.py:230
  143.8 3.4 %copy-start.5 = (bf16[128,256]{1,0:T(8,128)(2,1)S(1)}, bf16[128,256]{1,0:T(8,128)(2,1)}, u32[]{:S(2)}) copy-start(bf16[128,256]{1,0:T(8,128)(2,1)} %slice.89) | copy-start | bytes 196612
  143.8 3.4 %copy-start.7 = (bf16[128,256]{1,0:T(8,128)(2,1)S(1)}, bf16[128,256]{1,0:T(8,128)(2,1)}, u32[]{:S(2)}) copy-start(bf16[128,256]{1,0:T(8,128)(2,1)} %slice.90) | copy-start | bytes 196612
  143.8 3.4 %copy-start.11 = (bf16[512,1664]{1,0:T(8,128)(2,1)S(1)}, bf16[512,1664]{1,0:T(8,128)(2,1)}, u32[]{:S(2)}) copy-start(bf16[512,1664]{1,0:T(8,128)(2,1)} %copy-done.10) | copy-start | bytes 5111812
  147.2 7.3 %copy-start.3 = (s32[16,2]{0,1:T(2,128)S(1)}, s32[16,2]{0,1:T(2,128)}, u32[]{:S(2)}) copy-start(s32[16,2]{0,1:T(2,128)} %param.8) | copy-start | bytes 388
  147.2 7.3 %copy-start.4 = (bf16[16,2]{0,1:T(2,128)(2,1)S(1)}, bf16[16,2]{0,1:T(2,128)(2,1)}, u32[]{:S(2)}) copy-start(bf16[16,2]{0,1:T(2,128)(2,1)} %param.9) | copy-start | bytes 196
